TPU v7x, 32 devices: a whole 2x2x4 slice. The times are simulated.
32 devices in a mesh: slab: 8 (over z, core), grp: 4 (over y, x).
Axes of the slice: x: 2, y: 2, z: 4, core: 2. Of those that a mesh axis runs over, the one named last changes fastest.
Arguments:
- stress: bfloat16 [6, 262144], P(None, ('slab', 'grp')), may hold values from -6 to 6
- interp_weight: bfloat16 [2048, 64, 128], P(('slab', 'grp')), may hold values from -0.5 to 0.5
- block_owner: int32 [2048, 1], P(('slab', 'grp')), may hold values from 0 to 3; in each aligned block of 64 rows (0 to 63, 64 to 127, ...) at most 48 rows name the same one
- block_local: int32 [2048], P(('slab', 'grp')), may hold values from 0 to 63
- slip_system: int32 [131072], P(('slab', 'grp')), may hold values from 0 to 11
- mobility: float32 [131072], P(('slab', 'grp')), may hold values from 0.3 to 3
- position: float32 [3, 131072], P(None, ('slab', 'grp')), may hold values from -6 to 6
- target_slab: int32 [131072, 1], P(('slab', 'grp')), may hold values from 0 to 7; in each aligned block of 4096 rows (0 to 4095, 4096 to 8191, ...) at most 1024 rows name the same one
Outputs:
- distortion: float32 [6, 262144], P(None, ('slab', 'grp'))
- arrived: float32 [4, 262144], P(None, ('slab', 'grp'))
Inputs may be any that keep to these rules, and one draw needn't show every extreme that they name: Among the 64 segment blocks of one device at most 48 have the same block_owner; on some device exactly 48 do. Among the 4096 segments of one device at most 1024 have the same target_slab; on some device exactly 1024 do.
All inputs are finite; a program needn't handle non-finite values.
Results may differ from a plain program's by a relative error of at most 0.01.
Values may be sent and summed in bfloat16 or wider, within the bound.
No kernel may reach another device: no remote copies, remote signals or barrier semaphores. Data moves between devices by JAX's collectives and lax.ppermute only.
A program may use at most 64 MiB of HBM per device.

v0:
```python
import jax
import jax.numpy as jnp
import numpy as np
from jax import lax
from jax.sharding import PartitionSpec as P

NC = 6
NSYS = 12
BLK = 128
SEGB = 64


glide_time = 0.5


def slip_tables():
    normal_list = [(1.0, 1.0, 1.0), (-1.0, 1.0, 1.0), (1.0, -1.0, 1.0), (1.0, 1.0, -1.0)]
    schmid_rows = []
    glide_rows = []
    for along_x, along_y, along_z in normal_list:
        normal_vec = np.array([along_x, along_y, along_z]) / np.sqrt(3.0)
        for burgers in (
            (along_y, -along_x, 0.0),
            (along_z, 0.0, -along_x),
            (0.0, along_z, -along_y),
        ):
            burgers_vec = np.array(burgers) / np.sqrt(2.0)
            tensor = 0.5 * (np.outer(normal_vec, burgers_vec) + np.outer(burgers_vec, normal_vec))
            schmid_rows.append(
                [
                    tensor[0, 0],
                    tensor[1, 1],
                    tensor[2, 2],
                    2.0 * tensor[1, 2],
                    2.0 * tensor[0, 2],
                    2.0 * tensor[0, 1],
                ]
            )
            glide_rows.append(burgers_vec)
    return (np.array(schmid_rows, np.float32).T, np.array(glide_rows, np.float32).T)


def slot_ranks(labels, count):
    onehot = (labels[:, None] == jnp.arange(count, dtype=jnp.int32)[None, :]).astype(jnp.int32)
    return jnp.sum((jnp.cumsum(onehot, axis=0) - onehot) * onehot, axis=1)


def body(
    stress, interp_weight, block_owner, block_local, slip_system, mobility, position, target_slab
):
    schmid_np, glide_np = slip_tables()
    schmid = jnp.asarray(schmid_np, jnp.float32)
    glide_table = jnp.asarray(glide_np, jnp.float32)
    group_size = lax.axis_size("grp")
    slab_count = lax.axis_size("slab")
    block_count = interp_weight.shape[0]
    local_blocks = stress.shape[1] // BLK
    owner_index = block_owner[:, 0]
    slab_stress = lax.all_gather(stress, "grp", axis=1, tiled=True)
    stress_tiles = slab_stress.reshape(NC, group_size * local_blocks, BLK)[
        :, owner_index * local_blocks + block_local, :
    ]
    sampled = jnp.einsum(
        "cbv,bsv->cbs", stress_tiles, interp_weight, preferred_element_type=jnp.float32
    ).reshape(NC, -1)
    systems_hot = (jnp.arange(NSYS, dtype=jnp.int32)[:, None] == slip_system[None, :]).astype(
        jnp.float32
    )
    factors = jnp.dot(schmid, systems_hot, precision=lax.Precision.HIGHEST)
    resolved = jnp.sum(factors * sampled, axis=0)
    glide_step = glide_time * mobility * resolved
    weight_term = (
        (glide_step[None, :] * factors).astype(jnp.bfloat16).reshape(NC, block_count, SEGB)
    )
    spread = jnp.einsum(
        "cbs,bsv->cbv", weight_term, interp_weight, preferred_element_type=jnp.float32
    )
    dense_term = (
        jnp.zeros((NC, group_size * local_blocks, BLK), jnp.float32)
        .at[:, owner_index * local_blocks + block_local, :]
        .add(spread)
    )
    distortion = lax.psum_scatter(
        dense_term.reshape(NC, -1).astype(jnp.bfloat16), "grp", scatter_dimension=1, tiled=True
    ).astype(jnp.float32)
    glide_dirs = jnp.dot(glide_table, systems_hot, precision=lax.Precision.HIGHEST)
    moved_position = position + glide_dirs * glide_step[None, :]
    payload = jnp.concatenate([moved_position, glide_step[None, :]], axis=0)
    target = target_slab[:, 0]
    target_rank = slot_ranks(target, slab_count)
    per_peer = 2 * payload.shape[1] // slab_count
    outgoing_moves = (
        jnp.zeros((4, slab_count, per_peer), jnp.float32).at[:, target, target_rank].set(payload)
    )
    arrived = (
        lax.all_to_all(
            outgoing_moves.astype(jnp.bfloat16), "slab", split_axis=1, concat_axis=1, tiled=True
        )
        .astype(outgoing_moves.dtype)
        .reshape(4, -1)
    )
    return (distortion, arrived)


def solution(mesh):
    placed = (
        P(None, ("slab", "grp")),
        P(("slab", "grp"), None, None),
        P(("slab", "grp"), None),
        P(("slab", "grp")),
        P(("slab", "grp")),
        P(("slab", "grp")),
        P(None, ("slab", "grp")),
        P(("slab", "grp"), None),
    )
    return jax.shard_map(
        body,
        mesh=mesh,
        in_specs=placed,
        out_specs=(P(None, ("slab", "grp")), P(None, ("slab", "grp"))),
        check_vma=False,
    )
```

profile of v0, /device:TPU:0, one launch (start us, length us, event | category | flops | bytes accessed | tf_op | source)
XLA Modules:
  0.0 67.4 jit_solution(1898360276803271494)
XLA Ops:
  7.2 0.0 copy-start
  7.2 0.0 reduce-scatter.2.cloned.1.call-start
  7.2 0.8 %compare_select_fusion.2 = s32[64]{0:T(128)S(1)} fusion(s32[64]{0:T(128)} %param.13, s32[64,1]{0,1:T(1,128)} %param.12), kind=kLoop, calls=%fused_computation.37 | loop fusion | flops 320 | bytes 768 | tf_op jit(solution)/shard_map/select_n | solution.py:81
  8.0 11.8 %all_gather.3 = bf16[6,32768]{1,0:T(8,128)(2,1)S(1)} all-gather(bf16[6,8192]{1,0:T(8,128)(2,1)} %param.10), channel_id=1, replica_groups=mesh['slab'=8,'grp'=4] {'grp'}, dimensions={1}, use_global_device_ids=true | all-gather | bytes 491520 | tf_op jit(solution)/shard_map/all_gather | solution.py:59
  19.8 0.6 gather_fusion
  20.5 0.6 convolution_bitcast_fusion
  21.1 0.1 copy.20
  21.2 0.1 reshape.55
  21.3 1.0 %multiply_reduce_fusion = (f32[4096]{0:T(1024)S(1)}, f32[6,4096]{1,0:T(8,128)S(1)}) fusion(f32[6,4096]{1,0:T(8,128)S(1)} %reshape.55, f32[6,12]{1,0:T(8,128)} %constant.7.clone, s32[4096]{0:T(1024)} %param.14), kind=kOutput, calls=%fused_computation.24 | convolution fusion | flops 3633152 | bytes 229664 | tf_op jit(solution)/shard_map/dot_general | solution.py:69
  22.3 0.7 %multiply_multiply_fusion = f32[4096]{0:T(1024)S(1)} fusion(f32[4096]{0:T(1024)S(1)} %get-tuple-element.2, f32[4096]{0:T(1024)} %param.15), kind=kLoop, calls=%fused_computation.34 | loop fusion | flops 8192 | bytes 49152 | tf_op jit(solution)/shard_map/mul | solution.py:71
  23.0 0.1 reshape.56
  23.1 0.0 copy-start.6
  23.2 0.4 fusion.9
  23.5 0.1 broadcast_in_dim.8
  23.6 2.7 %scatter_fusion = f32[6,256,128]{2,0,1:T(8,128)S(1)} fusion(f32[6,256,128]{2,0,1:T(8,128)S(1)} %broadcast_in_dim.8, s32[64]{0:T(128)S(1)} %compare_select_fusion.2, f32[64,6,128]{2,1,0:T(8,128)S(1)} %fusion.9), kind=kCustom, calls=%fused_computation.1 | custom fusion | flops 49152 | bytes 590080 | tf_op jit(solution)/shard_map/scatter-add | solution.py:81
  26.4 0.9 %convert_bitcast_fusion = bf16[6,32768]{1,0:T(8,128)(2,1)} fusion(f32[6,256,128]{2,0,1:T(8,128)S(1)} %scatter_fusion), kind=kLoop, calls=%fused_computation.9 | loop fusion | flops 196608 | bytes 1179648 | tf_op jit(solution)/shard_map/convert_element_type | solution.py:84
  27.2 0.0 reduce-scatter.2.cloned.1.call-update
  27.3 2.3 %reduce-window.6 = s32[8,32,128]{2,1,0:T(8,128)S(1)} reduce-window(s32[8,32,128]{2,1,0:T(8,128)S(1)} %fusion.13, s32[]{:T(128)} %constant.11.clone.1), window={size=1x1x128 pad=0_0x0_0x127_0}, to_apply=%region_3.0 | reduce-window | flops 4161536 | bytes 262148 | tf_op jit(solution)/shard_map/reduce-window
  29.6 0.3 slice_reduce_fusion
  29.9 0.2 reduce-window.9
  30.1 0.1 add_bitcast_fusion
  30.2 0.1 fusion.7
  30.4 0.2 fusion.1
  30.7 0.6 copy.22
  31.3 0.1 multiply_reduce_fusion.1
  31.4 0.1 and_reduce_fusion
  31.6 12.8 %scatter_custom_fusion.1 = f32[4,8192]{0,1:T(8,128)} fusion(s32[4096]{0:T(1024)S(1)} %broadcast_select_fusion, f32[4096,4]{1,0:T(8,128)S(1)} %copy.22, f32[]{:T(128)} %constant.9.clone.1), kind=kCustom, calls=%fused_computation.6 | custom fusion | bytes 131076
  44.3 2.4 %convert_element_type.31 = bf16[4,8192]{0,1:T(8,128)(2,1)S(1)} convert(f32[4,8192]{0,1:T(8,128)} %scatter_custom_fusion.1) | non-fusion elementwise | flops 32768 | bytes 196608 | tf_op jit(solution)/shard_map/convert_element_type | solution.py:97
  46.7 0.9 %copy.23 = bf16[4,8,1024]{2,0,1:T(4,128)(2,1)S(1)} copy(bf16[4,8,1024]{0,2,1:T(8,128)(2,1)S(1)} %bitcast.48) | data formatting | bytes 131072 | tf_op jit(solution)/shard_map/convert_element_type | solution.py:97
  47.6 10.6 %all_to_all.5 = bf16[4,8,1024]{2,0,1:T(4,128)(2,1)S(1)} all-to-all(bf16[4,8,1024]{2,0,1:T(4,128)(2,1)S(1)} %copy.23), channel_id=1, replica_groups=mesh['slab'=8,'grp'=4] {'slab'}, dimensions={1} | all-to-all | bytes 131072 | tf_op jit(solution)/shard_map/all_to_all | solution.py:96
  58.2 0.7 convert.1
  58.9 1.6 %convert_element_type.27 = f32[6,8192]{1,0:T(8,128)} convert(bf16[6,8192]{1,0:T(8,128)(2,1)} %reduce-scatter.2.cloned.1.call-done) | non-fusion elementwise | flops 49152 | bytes 294912 | tf_op jit(solution)/shard_map/convert_element_type | solution.py:85
  (19 shorter events, 0.1 us)
Async XLA Ops:
  7.2 13.3 %copy-start = (bf16[64,64,128]{2,1,0:T(8,128)(2,1)S(1)}, bf16[64,64,128]{2,1,0:T(8,128)(2,1)}, u32[]{:S(2)}) copy-start(bf16[64,64,128]{2,1,0:T(8,128)(2,1)} %param.11) | copy-start | bytes 3145732
  7.2 51.7 %reduce-scatter.2.cloned.1.call-start = ((), (), s32[]{:S(2)}) async-start(), calls=%async_computation.2 | async-start | bytes 655360 | tf_op jit(solution)/shard_map/reduce_scatter | solution.py:83
  20.5 6.8 %copy-start.1 = (s32[4096,1]{0,1:T(1,128)S(1)}, s32[4096,1]{0,1:T(1,128)}, u32[]{:S(2)}) copy-start(s32[4096,1]{0,1:T(1,128)} %param.17) | copy-start | bytes 49156
  21.1 9.2 %copy-start.2 = (f32[3,4096]{1,0:T(4,128)S(1)}, f32[3,4096]{1,0:T(4,128)}, u32[]{:S(2)}) copy-start(f32[3,4096]{1,0:T(4,128)} %param.16) | copy-start | bytes 147460
  21.1 9.2 %copy-start.3 = (s32[4096]{0:T(1024)S(1)}, s32[4096]{0:T(1024)}, u32[]{:S(2)}) copy-start(s32[4096]{0:T(1024)} %param.14) | copy-start | bytes 49156
  21.1 9.2 %copy-start.4 = (f32[3,12]{1,0:T(4,128)S(1)}, f32[3,12]{1,0:T(4,128)}, u32[]{:S(2)}) copy-start(f32[3,12]{1,0:T(4,128)} %constant.8.clone) | copy-start | bytes 436
  23.1 8.2 %copy-start.6 = (s32[2]{0:T(128)S(1)}, s32[2]{0:T(128)}, u32[]{:S(2)}) copy-start(s32[2]{0:T(128)} %constant.28) | copy-start | bytes 28
  23.1 8.3 %copy-start.5 = (s32[2]{0:T(128)S(1)}, s32[2]{0:T(128)}, u32[]{:S(2)}) copy-start(s32[2]{0:T(128)} %constant.31) | copy-start | bytes 28
Sparse Core Ops, SparseCore 0:
  27.4 25.0 reduce-scatter.1
where the time goes:
time: 67.8 us; the launch traced here: 67.4 us
  blocking collectives  22.4 us (33%)
  local copies, waits for them, and re-layouts  15.6 us (23%)
  between operations  14.2 us (21%)
  other arithmetic  12.8 us (19%)
  matrix products  2.21 us (3%)
    unnamed x15, local copies, waits for them, and re-layouts  12.8 us
    all_gather x1, blocking collectives, body(): slab_stress = lax.all_gather(stress, 'grp', axis=1, tiled=True)  11.8 us
    all_to_all x1, blocking collectives, body(): lax.all_to_all(outgoing_moves.astype(jnp.bfloat16), 'slab', split_axis=1,...  10.6 us
    scatter-add x1, other arithmetic, body(): dense_term = jnp.zeros((NC, group_size * local_blocks, BLK), jnp.float32)...  2.74 us
    another operation x2, other arithmetic  2.5 us
    convert_element_type x1, other arithmetic, body(): outgoing_moves.astype(jnp.bfloat16)  2.39 us
    convert_element_type x1, other arithmetic, body(): distortion = lax.psum_scatter(dense_term.reshape(NC, -1).astype(jnp.bfloa...  1.62 us
  transfers between devices with their start and end apart: 1, of which 0 were waited for; matrix products, arithmetic and copies ran while one was open for 31% of the time, Pallas kernels for 0%

commit v1 on v0

v1 whole, which is shorter than its diff:
```python
import functools

import jax
import jax.numpy as jnp
import numpy as np
from jax import lax
from jax.experimental import pallas as pl
from jax.experimental.pallas import tpu as pltpu
from jax.sharding import PartitionSpec as P

NC = 6
NSYS = 12
BLK = 128
SEGB = 64
LANES = 128
SUB = 8
PACK = 4

glide_time = 0.5

VMEM = pl.BlockSpec(memory_space=pltpu.VMEM)
SMEM = pl.BlockSpec(memory_space=pltpu.SMEM)
CONTRACT_LANES = (((1,), (1,)), ((), ()))


def slip_signs():
    normal_list = [(1, 1, 1), (-1, 1, 1), (1, -1, 1), (1, 1, -1)]
    table = np.zeros((16, 16), np.float32)
    system = 0
    for x, y, z in normal_list:
        for burgers in ((y, -x, 0), (z, 0, -x), (0, z, -y)):
            outer = np.outer((x, y, z), burgers)
            tensor = outer + outer.T
            table[:NC, system] = (
                tensor[0, 0] / 2,
                tensor[1, 1] / 2,
                tensor[2, 2] / 2,
                tensor[1, 2],
                tensor[0, 2],
                tensor[0, 1],
            )
            table[8:11, system] = burgers
            system += 1
    return table


def iota(shape, dim):
    return lax.broadcasted_iota(jnp.int32, shape, dim)


def mask(condition):
    return jnp.where(condition, 1.0, 0.0).astype(jnp.bfloat16)


def prepare_kernel(slabs, cap, table_ref, slip_ref, target_ref, factor_ref, high_ref, low_ref):
    segments = slip_ref.shape[1]
    chunks = segments // LANES
    hot = mask(iota((16, segments), 0) == slip_ref[...])
    signs = jnp.dot(table_ref[...], hot, preferred_element_type=jnp.float32)
    scale = jnp.where(iota((16, 1), 0) < 8, np.float32(1 / np.sqrt(6.0)), np.float32(1 / np.sqrt(2.0)))
    factor_ref[...] = signs * scale

    target = target_ref[...]
    upto = mask(iota((LANES, LANES), 0) <= iota((LANES, LANES), 1))
    ones = jnp.ones((LANES, LANES), jnp.bfloat16)
    before = mask(iota((chunks, chunks), 1) < iota((chunks, chunks), 0))
    slot = target * cap
    for t in range(slabs):
        here = mask(target == t)
        inside = jnp.dot(here, upto, preferred_element_type=jnp.float32)
        total = jnp.dot(here, ones, preferred_element_type=jnp.float32)
        ahead = jnp.dot(before, total.astype(jnp.bfloat16), preferred_element_type=jnp.float32)
        rank = (inside + ahead).astype(jnp.int32) - 1
        slot = slot + jnp.where(target == t, rank, 0)
    high = slot // LANES
    low = slot % LANES
    rows = slabs * cap // LANES
    for r in range(chunks):
        at = pl.ds(r * LANES, LANES)
        high_ref[:, at] = mask(iota((rows, LANES), 0) == high[r : r + 1, :])
        low_ref[:, at] = mask(iota((LANES, LANES), 0) == low[r : r + 1, :])


def glide_kernel(group, *refs):
    owner_ref, local_ref, own_ref, mobility_ref, factor_ref, weight_ref = refs[:6]
    stress_refs = refs[6 : 6 + group]
    step_ref, kept_ref = refs[6 + group : 8 + group]
    sent_refs = refs[8 + group : 7 + 2 * group]
    tiles_ref, dense_ref = refs[7 + 2 * group :]
    blocks = local_ref.shape[0]
    rows, width = stress_refs[0].shape
    per_row = width // LANES
    me = own_ref[0]
    for k in range(group):
        for t in range(per_row):
            tiles_ref[k, t, :rows, :] = stress_refs[k][:, t * LANES : (t + 1) * LANES].astype(jnp.float32)
            tiles_ref[k, t, rows:, :] = jnp.zeros((tiles_ref.shape[2] - rows, LANES), jnp.float32)
    dense_ref[...] = jnp.zeros_like(dense_ref)

    span = PACK * SEGB
    part = iota((SUB, span), 1) // SEGB
    for g in range(blocks // PACK):
        places = []
        for j in range(PACK):
            local = local_ref[g * PACK + j]
            places.append((owner_ref[g * PACK + j] ^ me, local % per_row, pl.ds(local // per_row, SUB, stride=SUB)))
        stress = jnp.concatenate([tiles_ref[a, b, c, :] for a, b, c in places], axis=0).astype(jnp.bfloat16)
        at = pl.ds(g * span, span)
        weight = weight_ref[at, :]
        crossed = lax.dot_general(stress, weight, CONTRACT_LANES, preferred_element_type=jnp.float32)
        sampled = jnp.where(part == 0, crossed[:SUB], 0.0)
        for j in range(1, PACK):
            sampled = jnp.where(part == j, crossed[j * SUB : (j + 1) * SUB], sampled)
        factors = factor_ref[:SUB, at]
        resolved = jnp.sum(factors * sampled, axis=0, keepdims=True)
        step = glide_time * mobility_ref[:, at] * resolved
        step_ref[:, at] = step
        term = step * factors
        term = jnp.concatenate([jnp.where(part == j, term, 0.0) for j in range(PACK)], axis=0).astype(jnp.bfloat16)
        spread = jnp.dot(term, weight, preferred_element_type=jnp.float32)
        for j, (a, b, c) in enumerate(places):
            dense_ref[a, b, c, :] = dense_ref[a, b, c, :] + spread[j * SUB : (j + 1) * SUB]

    for t in range(per_row):
        kept_ref[:, t * LANES : (t + 1) * LANES] = dense_ref[0, t, :rows, :]
        for k in range(1, group):
            sent_refs[k - 1][:, t * LANES : (t + 1) * LANES] = dense_ref[k, t, :rows, :].astype(jnp.bfloat16)


def route_kernel(slabs, step_ref, position_ref, factor_ref, high_ref, low_ref, out_ref, code_ref, slot_ref, move_ref):
    step = step_ref[...]
    high = high_ref[...]
    rows = high.shape[0]
    deep = rows // slabs
    for c in range(4):
        value = step if c == 3 else position_ref[c : c + 1, :] + factor_ref[8 + c : 9 + c, :] * step
        code_ref[c * rows : (c + 1) * rows, :] = high * value.astype(jnp.bfloat16)
    slot_ref[...] = lax.dot_general(code_ref[...], low_ref[...], CONTRACT_LANES, preferred_element_type=jnp.float32)
    for t in range(slabs):
        for c in range(4):
            move_ref[(t * 4 + c) * deep : (t * 4 + c + 1) * deep, :] = slot_ref[c * rows + t * deep : c * rows + (t + 1) * deep, :]
    out_ref[...] = move_ref[...].astype(jnp.bfloat16)


def finish_kernel(group, slabs, *refs):
    kept_ref = refs[0]
    got_refs = refs[1:group]
    moved_ref = refs[group]
    distortion_ref, arrived_ref = refs[group + 1 : group + 3]
    sum_ref, slot_ref = refs[group + 3 :]
    per_row = kept_ref.shape[1] // LANES
    for t in range(per_row):
        at = slice(t * LANES, (t + 1) * LANES)
        total = kept_ref[:, at]
        for ref in got_refs:
            total = total + ref[:, at].astype(jnp.float32)
        sum_ref[t] = total
    deep_rows = kept_ref.shape[0] // NC
    for b in range(deep_rows):
        for t in range(per_row):
            lane = (b * per_row + t) * LANES
            distortion_ref[:, lane : lane + LANES] = sum_ref[t, pl.ds(b, NC, stride=deep_rows), :]
    slot_ref[...] = moved_ref[...].astype(jnp.float32)
    rows = moved_ref.shape[0] // slabs
    deep = rows // 4
    for s in range(slabs):
        for b in range(deep):
            lane = (s * deep + b) * LANES
            arrived_ref[:, lane : lane + LANES] = slot_ref[pl.ds(s * rows + b, 4, stride=deep), :]


def body(
    stress, interp_weight, block_owner, block_local, slip_system, mobility, position, target_slab
):
    group = lax.axis_size("grp")
    slabs = lax.axis_size("slab")
    segments = slip_system.shape[0]
    voxels = stress.shape[1]
    cap = 2 * segments // slabs
    slot_rows = slabs * cap // LANES
    f32, bf16 = jnp.float32, jnp.bfloat16
    shape = jax.ShapeDtypeStruct
    params = pltpu.CompilerParams(vmem_limit_bytes=48 * 1024 * 1024)

    def swap(x, k):
        return lax.ppermute(x, "grp", [(i, i ^ k) for i in range(group)])

    peers = sorted(range(1, group), key=lambda k: -bin(k).count("1"))
    packed = stress.reshape(NC * SUB, voxels // SUB)
    parts = {k: swap(packed, k) for k in peers}
    parts[0] = packed

    factor, high, low = pl.pallas_call(
        functools.partial(prepare_kernel, slabs, cap),
        out_shape=(
            shape((16, segments), f32),
            shape((slot_rows, segments), bf16),
            shape((LANES, segments), bf16),
        ),
        in_specs=[VMEM] * 3,
        out_specs=[VMEM] * 3,
        compiler_params=params,
        name="prepare",
    )(
        jnp.asarray(slip_signs(), bf16),
        slip_system.reshape(1, segments),
        target_slab.reshape(segments // LANES, LANES),
    )

    me = lax.axis_index("grp").astype(jnp.int32).reshape(1)
    tile_shape = (group, voxels // SUB // LANES, SUB * SUB, LANES)
    step, kept, *sent = pl.pallas_call(
        functools.partial(glide_kernel, group),
        out_shape=(shape((1, segments), f32), shape(packed.shape, f32))
        + (shape(packed.shape, bf16),) * (group - 1),
        in_specs=[SMEM] * 3 + [VMEM] * (3 + group),
        out_specs=[VMEM] * (group + 1),
        scratch_shapes=[pltpu.VMEM(tile_shape, f32), pltpu.VMEM(tile_shape, f32)],
        compiler_params=params,
        name="glide",
    )(
        block_owner.reshape(-1),
        block_local,
        me,
        mobility.reshape(1, segments),
        factor,
        interp_weight.reshape(segments, BLK),
        *[parts[k] for k in range(group)],
    )
    got = [swap(sent[k - 1], k) for k in peers]

    moves = pl.pallas_call(
        functools.partial(route_kernel, slabs),
        out_shape=shape((4 * slot_rows, LANES), bf16),
        in_specs=[VMEM] * 5,
        out_specs=VMEM,
        scratch_shapes=[
            pltpu.VMEM((4 * slot_rows, segments), bf16),
            pltpu.VMEM((4 * slot_rows, LANES), f32),
            pltpu.VMEM((4 * slot_rows, LANES), f32),
        ],
        compiler_params=params,
        name="route",
    )(step, position, factor, high, low)
    moved = lax.all_to_all(moves, "slab", split_axis=0, concat_axis=0, tiled=True)

    return pl.pallas_call(
        functools.partial(finish_kernel, group, slabs),
        out_shape=(shape((NC, voxels), f32), shape((4, slabs * cap), f32)),
        in_specs=[VMEM] * (group + 1),
        out_specs=[VMEM] * 2,
        scratch_shapes=[
            pltpu.VMEM((voxels // SUB // LANES, NC * SUB, LANES), f32),
            pltpu.VMEM((4 * slot_rows, LANES), f32),
        ],
        compiler_params=params,
        name="finish",
    )(kept, *got, moved)


def solution(mesh):
    placed = (
        P(None, ("slab", "grp")),
        P(("slab", "grp"), None, None),
        P(("slab", "grp"), None),
        P(("slab", "grp")),
        P(("slab", "grp")),
        P(("slab", "grp")),
        P(None, ("slab", "grp")),
        P(("slab", "grp"), None),
    )
    return jax.shard_map(
        body,
        mesh=mesh,
        in_specs=placed,
        out_specs=(P(None, ("slab", "grp")), P(None, ("slab", "grp"))),
        check_vma=False,
    )
```

time: 67.8 us -> 31.9 us (0.47)
  blocking collectives: 22.4 us -> 0 us
  between operations: 14.2 us -> 0.69 us
  starting transfers between devices: 0.04 us -> 13 us
  other arithmetic: 12.8 us -> 0 us
  local copies, waits for them, and re-layouts: 15.6 us -> 3.67 us
  waiting for transfers between devices: 0.02 us -> 7.47 us
  Pallas kernels: 0 us -> 6.87 us
  matrix products: 2.21 us -> 0 us
    all_gather x1 -> x0, blocking collectives: 11.8 us -> none  [body(): slab_stress = lax.all_gather(stress, 'grp', axis=1, tiled=True)]
    all_to_all x1 -> x0, blocking collectives: 10.6 us -> none  [body(): lax.all_to_all(outgoing_moves.astype(jnp.bfloat16), 'slab', split_axis=1,...]
    unnamed x15 -> x16, local copies, waits for them, and re-layouts: 12.8 us -> 2.59 us
    ppermute x0 -> x6, starting transfers between devices: none -> 8.09 us  [swap(): return lax.ppermute(x, 'grp', [(i, i ^ k) for i in range(group)])]
    ppermute x0 -> x6, waiting for transfers between devices: none -> 7.46 us  [swap(): return lax.ppermute(x, 'grp', [(i, i ^ k) for i in range(group)])]
    pallas_call x0 -> x4, Pallas kernels: none -> 6.87 us  [the longest x1 3.54 us: body(): pl.pallas_call(functools.partial(glide_kernel, group), out_shape=(shape((...]
    convert_element_type x5 -> x0, other arithmetic: 4.9 us -> none  [the longest x1 2.39 us: body(): outgoing_moves.astype(jnp.bfloat16)]
    all_to_all x0 -> x1, starting transfers between devices: none -> 4.87 us  [body(): lax.all_to_all(moves, 'slab', split_axis=0, concat_axis=0, tiled=True)]
  transfers between devices with their start and end apart: 1 -> 7, of which waited for: 0 -> 6; matrix products, arithmetic and copies ran while one was open for 31% -> 0% of each run, Pallas kernels for 0% -> 4%
where the time goes in v1:
time: 31.9 us; the launch traced here: 31.7 us
  starting transfers between devices  13 us (41%)
  waiting for transfers between devices  7.47 us (23%)
  Pallas kernels  6.87 us (22%)
  local copies, waits for them, and re-layouts  3.67 us (12%)
  between operations  0.69 us (2%)
    ppermute x6, starting transfers between devices, swap(): return lax.ppermute(x, 'grp', [(i, i ^ k) for i in range(group)])  8.09 us
    ppermute x6, waiting for transfers between devices, swap(): return lax.ppermute(x, 'grp', [(i, i ^ k) for i in range(group)])  7.46 us
    all_to_all x1, starting transfers between devices, body(): lax.all_to_all(moves, 'slab', split_axis=0, concat_axis=0, tiled=True)  4.87 us
    pallas_call x1, Pallas kernels, body(): pl.pallas_call(functools.partial(glide_kernel, group), out_shape=(shape((...  3.54 us
    unnamed x16, local copies, waits for them, and re-layouts  2.59 us
    pallas_call x1, Pallas kernels, body(): pl.pallas_call(functools.partial(route_kernel, slabs), out_shape=shape((4...  1.35 us
    pallas_call x1, Pallas kernels, body(): pl.pallas_call(functools.partial(prepare_kernel, slabs, cap), out_shape=(...  1.15 us
    reshape x1, local copies, waits for them, and re-layouts, body(): packed = stress.reshape(NC * SUB, voxels // SUB)  1.08 us
  transfers between devices with their start and end apart: 7, of which 6 were waited for; matrix products, arithmetic and copies ran while one was open for 0% of the time, Pallas kernels for 4%

profile of v1, /device:TPU:0, one launch (start us, length us, event | category | flops | bytes accessed | tf_op | source)
XLA Modules:
  0.0 31.7 jit_solution(14672599961158083075)
XLA Ops:
  0.6 0.0 copy-start.3
  0.6 0.0 copy-start.4
  0.6 1.1 %reshape.33.refs_6_ = bf16[48,1024]{1,0:T(8,128)(2,1)S(1)} reshape(bf16[6,8192]{1,0:T(8,128)(2,1)} %param.9) | data formatting | bytes 196608 | tf_op jit(solution)/shard_map/reshape | solution.py:189
  1.7 4.0 %collective-permute-start.2 = (bf16[48,1024]{1,0:T(8,128)(2,1)S(1)}, bf16[48,1024]{1,0:T(8,128)(2,1)S(1)}, u32[]{:S(2)}, u32[]{:S(2)}) collective-permute-start(bf16[48,1024]{1,0:T(8,128)(2,1)S(1)} %reshape.33.refs_6_), channel_id=1, source_target_pairs={{0,3},{1,2},{2,1},{3,0},{4,7},{5,6},{6,5},{7,4},{8,11},{9,10},{10,... | collective-permute-start | bytes 294920 | tf_op jit(solution)/shard_map/ppermute | solution.py:186
  5.7 0.5 %collective-permute-start.1 = (bf16[48,1024]{1,0:T(8,128)(2,1)S(1)}, bf16[48,1024]{1,0:T(8,128)(2,1)S(1)}, u32[]{:S(2)}, u32[]{:S(2)}) collective-permute-start(bf16[48,1024]{1,0:T(8,128)(2,1)S(1)} %reshape.33.refs_6_), channel_id=1, source_target_pairs={{0,2},{1,3},{2,0},{3,1},{4,6},{5,7},{6,4},{7,5},{8,10},{9,11},{10,... | collective-permute-start | bytes 294920 | tf_op jit(solution)/shard_map/ppermute | solution.py:186
  6.2 0.1 collective-permute-start
  6.3 0.0 copy-start.5
  6.3 0.0 copy-done.3
  6.3 0.0 copy-done.4
  6.3 0.7 %copy-done.5 = bf16[16,16]{1,0:T(8,128)(2,1)S(1)} copy-done((bf16[16,16]{1,0:T(8,128)(2,1)S(1)}, bf16[16,16]{1,0:T(8,128)(2,1)}, u32[]{:S(2)}) %copy-start.5) | copy-done | bytes 536
  7.0 0.0 copy-start.2
  7.0 1.1 %prepare.1 = (f32[16,4096]{1,0:T(8,128)S(1)}, bf16[64,4096]{1,0:T(8,128)(2,1)S(1)}, bf16[128,4096]{1,0:T(8,128)(2,1)S(1)}) custom-call(bf16[16,16]{1,0:T(8,128)(2,1)S(1)} %copy-done.5, s32[1,4096]{1,0:T(1,128)S(1)} %bitcast.11, s32[32,128]{1,0:T(8,128)S(1)} %bitcast.12), custom_call_target="tpu_custom_call" | custom-call | tf_op jit(solution)/shard_map/prepare/pallas_call | solution.py:193
  8.2 0.7 %collective-permute-done.2.refs_9_ = bf16[48,1024]{1,0:T(8,128)(2,1)S(1)} collective-permute-done((bf16[48,1024]{1,0:T(8,128)(2,1)S(1)}, bf16[48,1024]{1,0:T(8,128)(2,1)S(1)}, u32[]{:S(2)}, u32[]{:S(2)}) %collective-permute-start.2) | collective-permute-done | bytes 98336 | tf_op jit(solution)/shard_map/ppermute | solution.py:186
  8.9 1.7 %collective-permute-done.1.refs_8_ = bf16[48,1024]{1,0:T(8,128)(2,1)S(1)} collective-permute-done((bf16[48,1024]{1,0:T(8,128)(2,1)S(1)}, bf16[48,1024]{1,0:T(8,128)(2,1)S(1)}, u32[]{:S(2)}, u32[]{:S(2)}) %collective-permute-start.1) | collective-permute-done | bytes 98336 | tf_op jit(solution)/shard_map/ppermute | solution.py:186
  10.6 0.3 %collective-permute-done.refs_7_ = bf16[48,1024]{1,0:T(8,128)(2,1)S(1)} collective-permute-done((bf16[48,1024]{1,0:T(8,128)(2,1)S(1)}, bf16[48,1024]{1,0:T(8,128)(2,1)S(1)}, u32[]{:S(2)}, u32[]{:S(2)}) %collective-permute-start) | collective-permute-done | bytes 98336 | tf_op jit(solution)/shard_map/ppermute | solution.py:186
  10.9 0.0 copy-start.6
  10.9 0.0 copy-done.2
  10.9 0.6 %copy-done.6 = s32[64,1]{0,1:T(1,128)S(1)} copy-done((s32[64,1]{0,1:T(1,128)S(1)}, s32[64,1]{0,1:T(1,128)}, u32[]{:S(2)}) %copy-start.6) | copy-done | bytes 280
  11.6 0.0 copy-done.7
  11.6 1.2 %copy-done = bf16[64,64,128]{2,1,0:T(8,128)(2,1)S(1)} copy-done((bf16[64,64,128]{2,1,0:T(8,128)(2,1)S(1)}, bf16[64,64,128]{2,1,0:T(8,128)(2,1)}, u32[]{:S(2)}) %copy-start) | copy-done | bytes 1048600
  12.8 3.5 %glide.1 = (f32[1,4096]{1,0:T(1,128)S(1)}, f32[48,1024]{1,0:T(8,128)S(1)}, bf16[48,1024]{1,0:T(8,128)(2,1)S(1)}, bf16[48,1024]{1,0:T(8,128)(2,1)S(1)}, bf16[48,1024]{1,0:T(8,128)(2,1)S(1)}) custom-call(s32[64]{0:T(128)S(1)} %bitcast.13, s32[64]{0:T(128)S(1)} %copy-done.7, s32[1]{0:T(128)} %bitcast.1.refs_2_, f32[1,4096]{1,0:T(1,128)S(1)} %bitcast.10, ...), custom_call_target="tpu_custom_call" | custom-call | tf_op jit(solution)/shard_map/glide/pallas_call | solution.py:212
  16.4 0.0 copy-done.1
  16.4 1.3 %route.1 = bf16[256,128]{1,0:T(8,128)(2,1)} custom-call(f32[1,4096]{1,0:T(1,128)S(1)} %get-tuple-element.15.step_ref, f32[3,4096]{1,0:T(4,128)S(1)} %copy-done.1, f32[16,4096]{1,0:T(8,128)S(1)} %get-tuple-element.10.refs_4_.factor_ref, bf16[64,4096]{1,0:T(8,128)(2,1)S(1)} %get-tuple-element.16.high_ref, bf16[128,4096]{1,0:T(8,128)(2,1)S(1)} %get-tuple-element.17.low_ref), custom_call_target="tpu_custom_call" | custom-call | tf_op jit(solution)/shard_map/route/pallas_call | solution.py:232
  17.7 4.9 %all-to-all-start = ((bf16[8,32,128]{2,1,0:T(8,128)(2,1)}), bf16[8,32,128]{2,1,0:T(8,128)(2,1)S(1)}, u32[]{:S(2)}, u32[]{:S(2)}) async-start(bf16[8,32,128]{2,1,0:T(8,128)(2,1)} %bitcast.6), calls=%async_computation | async-start | bytes 131072 | tf_op jit(solution)/shard_map/all_to_all | solution.py:245
  22.6 1.6 %collective-permute-start.3 = (bf16[48,1024]{1,0:T(8,128)(2,1)S(1)}, bf16[48,1024]{1,0:T(8,128)(2,1)S(1)}, u32[]{:S(2)}, u32[]{:S(2)}) collective-permute-start(bf16[48,1024]{1,0:T(8,128)(2,1)S(1)} %get-tuple-element.12), channel_id=1, source_target_pairs={{0,3},{1,2},{2,1},{3,0},{4,7},{5,6},{6,5},{7,4},{8,11},{9,10},{10,... | collective-permute-start | bytes 294920 | tf_op jit(solution)/shard_map/ppermute | solution.py:186
  24.2 1.3 %collective-permute-start.4 = (bf16[48,1024]{1,0:T(8,128)(2,1)S(1)}, bf16[48,1024]{1,0:T(8,128)(2,1)S(1)}, u32[]{:S(2)}, u32[]{:S(2)}) collective-permute-start(bf16[48,1024]{1,0:T(8,128)(2,1)S(1)} %get-tuple-element.13), channel_id=1, source_target_pairs={{0,1},{1,0},{2,3},{3,2},{4,5},{5,4},{6,7},{7,6},{8,9},{9,8},{10,11... | collective-permute-start | bytes 294920 | tf_op jit(solution)/shard_map/ppermute | solution.py:186
  25.5 0.6 %collective-permute-start.5 = (bf16[48,1024]{1,0:T(8,128)(2,1)S(1)}, bf16[48,1024]{1,0:T(8,128)(2,1)S(1)}, u32[]{:S(2)}, u32[]{:S(2)}) collective-permute-start(bf16[48,1024]{1,0:T(8,128)(2,1)S(1)} %get-tuple-element.14), channel_id=1, source_target_pairs={{0,2},{1,3},{2,0},{3,1},{4,6},{5,7},{6,4},{7,5},{8,10},{9,11},{10,... | collective-permute-start | bytes 294920 | tf_op jit(solution)/shard_map/ppermute | solution.py:186
  26.1 3.0 %collective-permute-done.3.refs_1_ = bf16[48,1024]{1,0:T(8,128)(2,1)S(1)} collective-permute-done((bf16[48,1024]{1,0:T(8,128)(2,1)S(1)}, bf16[48,1024]{1,0:T(8,128)(2,1)S(1)}, u32[]{:S(2)}, u32[]{:S(2)}) %collective-permute-start.3) | collective-permute-done | bytes 98336 | tf_op jit(solution)/shard_map/ppermute | solution.py:186
  29.1 1.7 %collective-permute-done.4.refs_2_ = bf16[48,1024]{1,0:T(8,128)(2,1)S(1)} collective-permute-done((bf16[48,1024]{1,0:T(8,128)(2,1)S(1)}, bf16[48,1024]{1,0:T(8,128)(2,1)S(1)}, u32[]{:S(2)}, u32[]{:S(2)}) %collective-permute-start.4) | collective-permute-done | bytes 98336 | tf_op jit(solution)/shard_map/ppermute | solution.py:186
  30.8 0.1 collective-permute-done.5.refs_3_
  30.8 0.0 all-to-all-done
  30.8 0.8 %finish.1 = (f32[6,8192]{1,0:T(8,128)}, f32[4,8192]{1,0:T(4,128)}) custom-call(f32[48,1024]{1,0:T(8,128)S(1)} %get-tuple-element.11.refs_0_, bf16[48,1024]{1,0:T(8,128)(2,1)S(1)} %collective-permute-done.3.refs_1_, bf16[48,1024]{1,0:T(8,128)(2,1)S(1)} %collective-permute-done.4.refs_2_, bf16[48,1024]{1,0:T(8,128)(2,1)S(1)} %collective-permute-done.5.refs_3_, ...), custom_call_target="tpu_custom_call" | custom-call | tf_op jit(solution)/shard_map/finish/pallas_call | solution.py:247
  (3 shorter events, 0.0 us)
Async XLA Ops:
  0.6 5.7 %copy-start.3 = (s32[4096]{0:T(1024)S(1)}, s32[4096]{0:T(1024)}, u32[]{:S(2)}) copy-start(s32[4096]{0:T(1024)} %param.13) | copy-start | bytes 49156
  0.6 5.7 %copy-start.4 = (s32[4096,1]{0,1:T(1,128)S(1)}, s32[4096,1]{0,1:T(1,128)}, u32[]{:S(2)}) copy-start(s32[4096,1]{0,1:T(1,128)} %param.16) | copy-start | bytes 49156
  1.7 7.1 %collective-permute-start.2 = (bf16[48,1024]{1,0:T(8,128)(2,1)S(1)}, bf16[48,1024]{1,0:T(8,128)(2,1)S(1)}, u32[]{:S(2)}, u32[]{:S(2)}) collective-permute-start(bf16[48,1024]{1,0:T(8,128)(2,1)S(1)} %reshape.33.refs_6_), channel_id=1, source_target_pairs={{0,3},{1,2},{2,1},{3,0},{4,7},{5,6},{6,5},{7,4},{8,11},{9,10},{10,... | collective-permute-start | bytes 294920 | tf_op jit(solution)/shard_map/ppermute | solution.py:186
  5.7 4.9 %collective-permute-start.1 = (bf16[48,1024]{1,0:T(8,128)(2,1)S(1)}, bf16[48,1024]{1,0:T(8,128)(2,1)S(1)}, u32[]{:S(2)}, u32[]{:S(2)}) collective-permute-start(bf16[48,1024]{1,0:T(8,128)(2,1)S(1)} %reshape.33.refs_6_), channel_id=1, source_target_pairs={{0,2},{1,3},{2,0},{3,1},{4,6},{5,7},{6,4},{7,5},{8,10},{9,11},{10,... | collective-permute-start | bytes 294920 | tf_op jit(solution)/shard_map/ppermute | solution.py:186
  6.2 4.7 %collective-permute-start = (bf16[48,1024]{1,0:T(8,128)(2,1)S(1)}, bf16[48,1024]{1,0:T(8,128)(2,1)S(1)}, u32[]{:S(2)}, u32[]{:S(2)}) collective-permute-start(bf16[48,1024]{1,0:T(8,128)(2,1)S(1)} %reshape.33.refs_6_), channel_id=1, source_target_pairs={{0,1},{1,0},{2,3},{3,2},{4,5},{5,4},{6,7},{7,6},{8,9},{9,8},{10,11... | collective-permute-start | bytes 294920 | tf_op jit(solution)/shard_map/ppermute | solution.py:186
  6.3 0.7 %copy-start.5 = (bf16[16,16]{1,0:T(8,128)(2,1)S(1)}, bf16[16,16]{1,0:T(8,128)(2,1)}, u32[]{:S(2)}) copy-start(bf16[16,16]{1,0:T(8,128)(2,1)} %constant.6.clone.table_ref) | copy-start | bytes 1540
  7.0 3.9 %copy-start.2 = (f32[4096]{0:T(1024)S(1)}, f32[4096]{0:T(1024)}, u32[]{:S(2)}) copy-start(f32[4096]{0:T(1024)} %param.14) | copy-start | bytes 49156
  10.9 0.7 %copy-start.6 = (s32[64,1]{0,1:T(1,128)S(1)}, s32[64,1]{0,1:T(1,128)}, u32[]{:S(2)}) copy-start(s32[64,1]{0,1:T(1,128)} %param.11) | copy-start | bytes 772
  10.9 0.7 %copy-start.7 = (s32[64]{0:T(128)S(1)}, s32[64]{0:T(128)}, u32[]{:S(2)}) copy-start(s32[64]{0:T(128)} %refs_1_.1) | copy-start | bytes 772
  11.6 1.2 %copy-start = (bf16[64,64,128]{2,1,0:T(8,128)(2,1)S(1)}, bf16[64,64,128]{2,1,0:T(8,128)(2,1)}, u32[]{:S(2)}) copy-start(bf16[64,64,128]{2,1,0:T(8,128)(2,1)} %param.10) | copy-start | bytes 3145732
  12.8 3.6 %copy-start.1 = (f32[3,4096]{1,0:T(4,128)S(1)}, f32[3,4096]{1,0:T(4,128)}, u32[]{:S(2)}) copy-start(f32[3,4096]{1,0:T(4,128)} %position_ref.1) | copy-start | bytes 147460
  17.7 13.1 %all-to-all-start = ((bf16[8,32,128]{2,1,0:T(8,128)(2,1)}), bf16[8,32,128]{2,1,0:T(8,128)(2,1)S(1)}, u32[]{:S(2)}, u32[]{:S(2)}) async-start(bf16[8,32,128]{2,1,0:T(8,128)(2,1)} %bitcast.6), calls=%async_computation | async-start | bytes 131072 | tf_op jit(solution)/shard_map/all_to_all | solution.py:245
  22.6 6.5 %collective-permute-start.3 = (bf16[48,1024]{1,0:T(8,128)(2,1)S(1)}, bf16[48,1024]{1,0:T(8,128)(2,1)S(1)}, u32[]{:S(2)}, u32[]{:S(2)}) collective-permute-start(bf16[48,1024]{1,0:T(8,128)(2,1)S(1)} %get-tuple-element.12), channel_id=1, source_target_pairs={{0,3},{1,2},{2,1},{3,0},{4,7},{5,6},{6,5},{7,4},{8,11},{9,10},{10,... | collective-permute-start | bytes 294920 | tf_op jit(solution)/shard_map/ppermute | solution.py:186
  24.2 6.5 %collective-permute-start.4 = (bf16[48,1024]{1,0:T(8,128)(2,1)S(1)}, bf16[48,1024]{1,0:T(8,128)(2,1)S(1)}, u32[]{:S(2)}, u32[]{:S(2)}) collective-permute-start(bf16[48,1024]{1,0:T(8,128)(2,1)S(1)} %get-tuple-element.13), channel_id=1, source_target_pairs={{0,1},{1,0},{2,3},{3,2},{4,5},{5,4},{6,7},{7,6},{8,9},{9,8},{10,11... | collective-permute-start | bytes 294920 | tf_op jit(solution)/shard_map/ppermute | solution.py:186
  25.5 5.3 %collective-permute-start.5 = (bf16[48,1024]{1,0:T(8,128)(2,1)S(1)}, bf16[48,1024]{1,0:T(8,128)(2,1)S(1)}, u32[]{:S(2)}, u32[]{:S(2)}) collective-permute-start(bf16[48,1024]{1,0:T(8,128)(2,1)S(1)} %get-tuple-element.14), channel_id=1, source_target_pairs={{0,2},{1,3},{2,0},{3,1},{4,6},{5,7},{6,4},{7,5},{8,10},{9,11},{10,... | collective-permute-start | bytes 294920 | tf_op jit(solution)/shard_map/ppermute | solution.py:186

commit v2 on v1

v2 whole, which is shorter than its diff:
```python
import functools

import jax
import jax.numpy as jnp
import numpy as np
from jax import lax
from jax.experimental import pallas as pl
from jax.experimental.pallas import tpu as pltpu
from jax.sharding import PartitionSpec as P

NC = 6
NSYS = 12
BLK = 128
SEGB = 64
LANES = 128
SUB = 8
PACK = 4

glide_time = 0.5

VMEM = pl.BlockSpec(memory_space=pltpu.VMEM)
SMEM = pl.BlockSpec(memory_space=pltpu.SMEM)
HBM = pl.BlockSpec(memory_space=pl.ANY)
CONTRACT_LANES = (((1,), (1,)), ((), ()))


def slip_signs():
    normal_list = [(1, 1, 1), (-1, 1, 1), (1, -1, 1), (1, 1, -1)]
    table = np.zeros((16, 16), np.float32)
    system = 0
    for x, y, z in normal_list:
        for burgers in ((y, -x, 0), (z, 0, -x), (0, z, -y)):
            outer = np.outer((x, y, z), burgers)
            tensor = outer + outer.T
            table[:NC, system] = (
                tensor[0, 0] / 2,
                tensor[1, 1] / 2,
                tensor[2, 2] / 2,
                tensor[1, 2],
                tensor[0, 2],
                tensor[0, 1],
            )
            table[8:11, system] = burgers
            system += 1
    return table


def iota(shape, dim):
    return lax.broadcasted_iota(jnp.int32, shape, dim)


def mask(condition):
    return jnp.where(condition, 1.0, 0.0).astype(jnp.bfloat16)


def prepare_kernel(slabs, cap, table_ref, slip_ref, target_ref, source_ref, factor_ref, high_ref, low_ref, weight_ref, sem):
    fetch = pltpu.make_async_copy(source_ref, weight_ref, sem)
    fetch.start()
    segments = slip_ref.shape[1]
    chunks = segments // LANES
    hot = mask(iota((16, segments), 0) == slip_ref[...])
    signs = jnp.dot(table_ref[...], hot, preferred_element_type=jnp.float32)
    scale = jnp.where(iota((16, 1), 0) < 8, np.float32(1 / np.sqrt(6.0)), np.float32(1 / np.sqrt(2.0)))
    factor_ref[...] = signs * scale

    target = target_ref[...] ^ lax.axis_index("slab")
    upto = mask(iota((LANES, LANES), 0) <= iota((LANES, LANES), 1))
    ones = jnp.ones((LANES, LANES), jnp.bfloat16)
    before = mask(iota((chunks, chunks), 1) < iota((chunks, chunks), 0))
    slot = target * cap
    for t in range(slabs):
        here = mask(target == t)
        inside = jnp.dot(here, upto, preferred_element_type=jnp.float32)
        total = jnp.dot(here, ones, preferred_element_type=jnp.float32)
        ahead = jnp.dot(before, total.astype(jnp.bfloat16), preferred_element_type=jnp.float32)
        rank = (inside + ahead).astype(jnp.int32) - 1
        slot = slot + jnp.where(target == t, rank, 0)
    high = slot // LANES
    low = slot % LANES
    rows = slabs * cap // LANES
    for r in range(chunks):
        at = pl.ds(r * LANES, LANES)
        high_ref[:, at] = mask(iota((rows, LANES), 0) == high[r : r + 1, :])
        low_ref[:, at] = mask(iota((LANES, LANES), 0) == low[r : r + 1, :])
    fetch.wait()


def place_of(place_ref, per_row, j):
    spot = place_ref[j]
    return spot // (SUB * per_row), spot % per_row, spot // per_row % SUB


def glide_kernel(group, slabs, *refs):
    place_ref, mobility_ref, position_ref, factor_ref, high_ref, low_ref, weight_ref = refs[:7]
    stress_refs = refs[7 : 7 + group]
    term_ref = refs[7 + group]
    move_refs = refs[8 + group : 9 + group + slabs // 2]
    tiles_ref, step_ref, code_ref, slot_ref, move_ref = refs[9 + group + slabs // 2 :]
    blocks = place_ref.shape[0]
    rows, width = stress_refs[0].shape
    per_row = width // LANES
    for k in range(group):
        for t in range(per_row):
            tiles_ref[k, t, :rows, :] = stress_refs[k][:, t * LANES : (t + 1) * LANES].astype(jnp.float32)

    span = PACK * SEGB
    part = iota((SUB, span), 1) // SEGB
    real = iota((SUB, span), 0) < NC
    for g in range(blocks // PACK):
        tiles = []
        for j in range(PACK):
            a, b, c = place_of(place_ref, per_row, g * PACK + j)
            tiles.append(tiles_ref[a, b, pl.ds(c, SUB, stride=SUB), :])
        stress = jnp.concatenate(tiles, axis=0).astype(jnp.bfloat16)
        at = pl.ds(g * span, span)
        crossed = lax.dot_general(stress, weight_ref[at, :], CONTRACT_LANES, preferred_element_type=jnp.float32)
        sampled = crossed[:SUB]
        for j in range(1, PACK):
            sampled = jnp.where(part == j, crossed[j * SUB : (j + 1) * SUB], sampled)
        factors = factor_ref[:SUB, at]
        resolved = jnp.sum(jnp.where(real, factors * sampled, 0.0), axis=0, keepdims=True)
        step = glide_time * mobility_ref[:, at] * resolved
        step_ref[:, at] = step
        term_ref[:, at] = step * factors

    step = step_ref[...]
    high = high_ref[...]
    slot_rows = high.shape[0]
    deep = slot_rows // slabs
    for c in range(4):
        value = step if c == 3 else position_ref[c : c + 1, :] + factor_ref[8 + c : 9 + c, :] * step
        code_ref[c * slot_rows : (c + 1) * slot_rows, :] = high * value.astype(jnp.bfloat16)
    slot_ref[...] = lax.dot_general(code_ref[...], low_ref[...], CONTRACT_LANES, preferred_element_type=jnp.float32)
    for t in range(slabs):
        for c in range(4):
            source = c * slot_rows + t * deep
            move_ref[(t * 4 + c) * deep : (t * 4 + c + 1) * deep, :] = slot_ref[source : source + deep, :]
    sizes = [1, 1] + [2] * (slabs // 2 - 1)
    start = 0
    for ref, size in zip(move_refs, sizes):
        stop = start + size * 4 * deep
        ref[...] = move_ref[start:stop, :].astype(ref.dtype)
        start = stop


def spread_kernel(group, *refs):
    place_ref, term_ref, weight_ref, kept_ref = refs[:4]
    sent_refs = refs[4 : 3 + group]
    dense_ref, spread_ref = refs[3 + group :]
    blocks = place_ref.shape[0]
    rows, width = kept_ref.shape
    per_row = width // LANES
    span = PACK * SEGB
    part = iota((SUB, span), 1) // SEGB
    dense_ref[...] = jnp.zeros_like(dense_ref)
    for g in range(blocks // PACK):
        at = pl.ds(g * span, span)
        term = term_ref[:, at]
        term = jnp.concatenate([jnp.where(part == j, term, 0.0) for j in range(PACK)], axis=0).astype(jnp.bfloat16)
        spread_ref[g * PACK * SUB : (g + 1) * PACK * SUB, :] = jnp.dot(term, weight_ref[at, :], preferred_element_type=jnp.float32)
    for j in range(blocks):
        a, b, c = place_of(place_ref, per_row, j)
        at = pl.ds(c, NC, stride=SUB)
        dense_ref[a, b, at, :] = dense_ref[a, b, at, :] + spread_ref[j * SUB : j * SUB + NC, :]
    for t in range(per_row):
        kept_ref[:, t * LANES : (t + 1) * LANES] = dense_ref[0, t]
        for k in range(1, group):
            sent_refs[k - 1][:, t * LANES : (t + 1) * LANES] = dense_ref[k, t].astype(jnp.bfloat16)


def finish_kernel(group, slabs, *refs):
    kept_ref = refs[0]
    got_refs = refs[1:group]
    own_ref, near_ref, across_ref = refs[group : group + 3]
    far_refs = refs[group + 3 : group + 2 + slabs // 2]
    distortion_ref, arrived_ref, sum_ref, slot_ref = refs[group + 2 + slabs // 2 :]
    per_row = kept_ref.shape[1] // LANES
    for t in range(per_row):
        at = slice(t * LANES, (t + 1) * LANES)
        total = kept_ref[:, at]
        for ref in got_refs:
            total = total + ref[:, at].astype(jnp.float32)
        sum_ref[t] = total
    deep_rows = kept_ref.shape[0] // NC
    for b in range(deep_rows):
        for t in range(per_row):
            lane = (b * per_row + t) * LANES
            distortion_ref[:, lane : lane + LANES] = sum_ref[t, pl.ds(b, NC, stride=deep_rows), :]
    rows = own_ref.shape[0]
    deep = rows // 4
    slot_ref[0] = own_ref[...].astype(jnp.float32)
    slot_ref[1] = near_ref[...].astype(jnp.float32)
    for k, ref in enumerate(far_refs):
        slot_ref[2 * k + 2] = ref[:rows, :].astype(jnp.float32)
        slot_ref[2 * k + 3] = across_ref[k * rows : (k + 1) * rows, :].astype(jnp.float32)
    me = lax.axis_index("slab")
    for s in range(slabs):
        for b in range(deep):
            lane = (s * deep + b) * LANES
            arrived_ref[:, lane : lane + LANES] = slot_ref[me ^ s, pl.ds(b, 4, stride=deep), :]


def body(
    stress, interp_weight, block_owner, block_local, slip_system, mobility, position, target_slab
):
    group = lax.axis_size("grp")
    slabs = lax.axis_size("slab")
    segments = slip_system.shape[0]
    voxels = stress.shape[1]
    cap = 2 * segments // slabs
    slot_rows = slabs * cap // LANES
    f32, bf16 = jnp.float32, jnp.bfloat16
    shape = jax.ShapeDtypeStruct
    params = pltpu.CompilerParams(vmem_limit_bytes=48 * 1024 * 1024)

    def swap(x, k):
        return lax.ppermute(x, "grp", [(i, i ^ k) for i in range(group)])

    peers = sorted(range(1, group), key=lambda k: -bin(k).count("1"))
    packed = stress.reshape(NC * SUB, voxels // SUB)
    parts = {k: swap(packed, k) for k in peers}
    parts[0] = packed

    factor, high, low, weight = pl.pallas_call(
        functools.partial(prepare_kernel, slabs, cap),
        out_shape=(
            shape((16, segments), f32),
            shape((slot_rows, segments), bf16),
            shape((LANES, segments), bf16),
            shape((segments, BLK), bf16),
        ),
        in_specs=[VMEM] * 3 + [HBM],
        out_specs=[VMEM] * 4,
        scratch_shapes=[pltpu.SemaphoreType.DMA],
        compiler_params=params,
        name="prepare",
    )(
        jnp.asarray(slip_signs(), bf16),
        slip_system.reshape(1, segments),
        target_slab.reshape(segments // LANES, LANES),
        interp_weight.reshape(segments, BLK),
    )

    me = lax.axis_index("grp").astype(jnp.int32)
    place = (block_owner.reshape(-1) ^ me) * (voxels // BLK) + block_local
    tile_shape = (group, voxels // SUB // LANES, SUB * SUB, LANES)
    chunk = 4 * slot_rows // slabs
    term, own, near, *far = pl.pallas_call(
        functools.partial(glide_kernel, group, slabs),
        out_shape=(shape((SUB, segments), f32), shape((chunk, LANES), bf16), shape((chunk, LANES), bf16))
        + (shape((2 * chunk, LANES), bf16),) * (slabs // 2 - 1),
        in_specs=[SMEM] + [VMEM] * (6 + group),
        out_specs=[VMEM] * (2 + slabs // 2),
        scratch_shapes=[
            pltpu.VMEM(tile_shape, f32),
            pltpu.VMEM((1, segments), f32),
            pltpu.VMEM((4 * slot_rows, segments), bf16),
            pltpu.VMEM((4 * slot_rows, LANES), f32),
            pltpu.VMEM((4 * slot_rows, LANES), f32),
        ],
        compiler_params=params,
        name="glide",
    )(
        place,
        mobility.reshape(1, segments),
        position,
        factor,
        high,
        low,
        weight,
        *[parts[k] for k in range(group)],
    )

    def hop(x, k):
        return lax.ppermute(x, "slab", [(i, i ^ k) for i in range(slabs)])

    far = [hop(x, 2 * k + 2) for k, x in enumerate(far)]
    near = hop(near, 1)

    kept, *sent = pl.pallas_call(
        functools.partial(spread_kernel, group),
        out_shape=(shape(packed.shape, f32),) + (shape(packed.shape, bf16),) * (group - 1),
        in_specs=[SMEM] + [VMEM] * 2,
        out_specs=[VMEM] * group,
        scratch_shapes=[
            pltpu.VMEM((group, voxels // SUB // LANES, NC * SUB, LANES), f32),
            pltpu.VMEM((segments // SEGB * SUB, LANES), f32),
        ],
        compiler_params=params,
        name="spread",
    )(place, term, weight)
    got = [swap(sent[k - 1], k) for k in peers]
    across = hop(jnp.concatenate([x[chunk:] for x in far], axis=0), 1)

    return pl.pallas_call(
        functools.partial(finish_kernel, group, slabs),
        out_shape=(shape((NC, voxels), f32), shape((4, slabs * cap), f32)),
        in_specs=[VMEM] * (group + 2 + slabs // 2),
        out_specs=[VMEM] * 2,
        scratch_shapes=[
            pltpu.VMEM((voxels // SUB // LANES, NC * SUB, LANES), f32),
            pltpu.VMEM((slabs, chunk, LANES), f32),
        ],
        compiler_params=params,
        name="finish",
    )(kept, *got, own, near, across, *far)


def solution(mesh):
    placed = (
        P(None, ("slab", "grp")),
        P(("slab", "grp"), None, None),
        P(("slab", "grp"), None),
        P(("slab", "grp")),
        P(("slab", "grp")),
        P(("slab", "grp")),
        P(None, ("slab", "grp")),
        P(("slab", "grp"), None),
    )
    return jax.shard_map(
        body,
        mesh=mesh,
        in_specs=placed,
        out_specs=(P(None, ("slab", "grp")), P(None, ("slab", "grp"))),
        check_vma=False,
    )
```

time: 31.9 us -> 27.6 us (0.87)
  waiting for transfers between devices: 7.47 us -> 2.86 us
  Pallas kernels: 6.87 us -> 5.48 us
  local copies, waits for them, and re-layouts: 3.67 us -> 4.98 us
    ppermute x6, waiting for transfers between devices: 7.46 us -> 2.02 us  [swap(): return lax.ppermute(x, 'grp', [(i, i ^ k) for i in range(group)])]
    ppermute x0 -> x5, starting transfers between devices: none -> 5.01 us  [hop(): return lax.ppermute(x, 'slab', [(i, i ^ k) for i in range(slabs)])]
    all_to_all x1 -> x0, starting transfers between devices: 4.87 us -> none  [body(): lax.all_to_all(moves, 'slab', split_axis=0, concat_axis=0, tiled=True)]
    pallas_call x2, Pallas kernels: 4.89 us -> 3.41 us  [the longest x1 1.99 us: body(): pl.pallas_call(functools.partial(glide_kernel, group, slabs), out_shape=(...]
    ppermute x0 -> x5, waiting for transfers between devices: none -> 0.84 us  [hop(): return lax.ppermute(x, 'slab', [(i, i ^ k) for i in range(slabs)])]
    slice x0 -> x5, local copies, waits for them, and re-layouts: none -> 0.71 us  [body(): across = hop(jnp.concatenate([x[chunk:] for x in far], axis=0), 1)]
    unnamed x16 -> x24, local copies, waits for them, and re-layouts: 2.59 us -> 3.19 us
  transfers between devices with their start and end apart: 7 -> 11, of which waited for: 6 -> 5; matrix products, arithmetic and copies ran while one was open for 0% -> 0% of each run, Pallas kernels for 4% -> 10%
where the time goes in v2:
time: 27.6 us; the launch traced here: 27.2 us
  starting transfers between devices  13.2 us (48%)
  Pallas kernels  5.48 us (20%)
  local copies, waits for them, and re-layouts  4.98 us (18%)
  waiting for transfers between devices  2.86 us (10%)
  between operations  0.73 us (3%)
    ppermute x6, starting transfers between devices, swap(): return lax.ppermute(x, 'grp', [(i, i ^ k) for i in range(group)])  8.16 us
    ppermute x5, starting transfers between devices, hop(): return lax.ppermute(x, 'slab', [(i, i ^ k) for i in range(slabs)])  5.01 us
    unnamed x24, local copies, waits for them, and re-layouts  3.19 us
    ppermute x6, waiting for transfers between devices, swap(): return lax.ppermute(x, 'grp', [(i, i ^ k) for i in range(group)])  2.02 us
    pallas_call x1, Pallas kernels, body(): pl.pallas_call(functools.partial(glide_kernel, group, slabs), out_shape=(...  1.99 us
    pallas_call x1, Pallas kernels, body(): pl.pallas_call(functools.partial(spread_kernel, group), out_shape=(shape(...  1.42 us
    pallas_call x1, Pallas kernels, body(): pl.pallas_call(functools.partial(prepare_kernel, slabs, cap), out_shape=(...  1.23 us
    reshape x1, local copies, waits for them, and re-layouts, body(): packed = stress.reshape(NC * SUB, voxels // SUB)  1.08 us
  transfers between devices with their start and end apart: 11, of which 5 were waited for; matrix products, arithmetic and copies ran while one was open for 0% of the time, Pallas kernels for 10%

profile of v2, /device:TPU:0, one launch (start us, length us, event | category | flops | bytes accessed | tf_op | source)
XLA Modules:
  0.0 27.2 jit_solution(12953652457006596640)
XLA Ops:
  0.7 1.1 %reshape.28.refs_7_ = bf16[48,1024]{1,0:T(8,128)(2,1)S(1)} reshape(bf16[6,8192]{1,0:T(8,128)(2,1)} %param.9) | data formatting | bytes 196608 | tf_op jit(solution)/shard_map/reshape | solution.py:220
  1.7 4.0 %collective-permute-start.2 = (bf16[48,1024]{1,0:T(8,128)(2,1)S(1)}, bf16[48,1024]{1,0:T(8,128)(2,1)S(1)}, u32[]{:S(2)}, u32[]{:S(2)}) collective-permute-start(bf16[48,1024]{1,0:T(8,128)(2,1)S(1)} %reshape.28.refs_7_), channel_id=1, source_target_pairs={{0,3},{1,2},{2,1},{3,0},{4,7},{5,6},{6,5},{7,4},{8,11},{9,10},{10,... | collective-permute-start | bytes 294920 | tf_op jit(solution)/shard_map/ppermute | solution.py:217
  5.7 0.5 %collective-permute-start.1 = (bf16[48,1024]{1,0:T(8,128)(2,1)S(1)}, bf16[48,1024]{1,0:T(8,128)(2,1)S(1)}, u32[]{:S(2)}, u32[]{:S(2)}) collective-permute-start(bf16[48,1024]{1,0:T(8,128)(2,1)S(1)} %reshape.28.refs_7_), channel_id=1, source_target_pairs={{0,2},{1,3},{2,0},{3,1},{4,6},{5,7},{6,4},{7,5},{8,10},{9,11},{10,... | collective-permute-start | bytes 294920 | tf_op jit(solution)/shard_map/ppermute | solution.py:217
  6.2 0.1 collective-permute-start
  6.3 0.7 %copy-done.10 = s32[64]{0:T(128)S(1)} copy-done((s32[64]{0:T(128)S(1)}, s32[64]{0:T(128)}, u32[]{:S(2)}) %copy-start.10) | copy-done | bytes 280
  7.0 0.0 copy-done.11
  7.0 0.7 %copy-done.9 = bf16[16,16]{1,0:T(8,128)(2,1)S(1)} copy-done((bf16[16,16]{1,0:T(8,128)(2,1)S(1)}, bf16[16,16]{1,0:T(8,128)(2,1)}, u32[]{:S(2)}) %copy-start.9) | copy-done | bytes 536
  7.7 1.2 %copy-done = bf16[64,64,128]{2,1,0:T(8,128)(2,1)S(1)} copy-done((bf16[64,64,128]{2,1,0:T(8,128)(2,1)S(1)}, bf16[64,64,128]{2,1,0:T(8,128)(2,1)}, u32[]{:S(2)}) %copy-start) | copy-done | bytes 1048600
  8.9 1.2 %prepare.1 = (f32[16,4096]{1,0:T(8,128)S(1)}, bf16[64,4096]{1,0:T(8,128)(2,1)S(1)}, bf16[128,4096]{1,0:T(8,128)(2,1)S(1)}, bf16[4096,128]{1,0:T(8,128)(2,1)S(1)}) custom-call(bf16[16,16]{1,0:T(8,128)(2,1)S(1)} %copy-done.9, s32[1,4096]{1,0:T(1,128)S(1)} %bitcast.7, s32[32,128]{1,0:T(8,128)S(1)} %bitcast.8, bf16[4096,128]{1,0:T(8,128)(2,1)S(1)} %bitcast.6), custom_call_target="tpu_custom_call" | custom-call | tf_op jit(solution)/shard_map/prepare/pallas_call | solution.py:224
  10.2 0.0 collective-permute-done.2.refs_10_
  10.2 0.4 %collective-permute-done.1.refs_9_ = bf16[48,1024]{1,0:T(8,128)(2,1)S(1)} collective-permute-done((bf16[48,1024]{1,0:T(8,128)(2,1)S(1)}, bf16[48,1024]{1,0:T(8,128)(2,1)S(1)}, u32[]{:S(2)}, u32[]{:S(2)}) %collective-permute-start.1) | collective-permute-done | bytes 98336 | tf_op jit(solution)/shard_map/ppermute | solution.py:217
  10.6 0.3 %collective-permute-done.refs_8_ = bf16[48,1024]{1,0:T(8,128)(2,1)S(1)} collective-permute-done((bf16[48,1024]{1,0:T(8,128)(2,1)S(1)}, bf16[48,1024]{1,0:T(8,128)(2,1)S(1)}, u32[]{:S(2)}, u32[]{:S(2)}) %collective-permute-start) | collective-permute-done | bytes 98336 | tf_op jit(solution)/shard_map/ppermute | solution.py:217
  10.9 2.0 %glide.1 = (f32[8,4096]{1,0:T(8,128)S(1)}, bf16[32,128]{1,0:T(8,128)(2,1)S(1)}, bf16[32,128]{1,0:T(8,128)(2,1)S(1)}, bf16[64,128]{1,0:T(8,128)(2,1)S(1)}, bf16[6...) custom-call(s32[64]{0:T(128)S(1)} %bitcast_add_fusion.refs_0_, f32[1,4096]{1,0:T(1,128)S(1)} %bitcast.9, ...), custom_call_target="tpu_custom_call" | custom-call | tf_op jit(solution)/shard_map/glide/pallas_call | solution.py:248
  12.9 1.6 %collective-permute-start.7 = (bf16[64,128]{1,0:T(8,128)(2,1)S(1)}, bf16[64,128]{1,0:T(8,128)(2,1)S(1)}, u32[]{:S(2)}, u32[]{:S(2)}) collective-permute-start(bf16[64,128]{1,0:T(8,128)(2,1)S(1)} %get-tuple-element.27), channel_id=1, source_target_pairs={{0,8},{4,12},{8,0},{12,4},{16,24},{20,28},{24,16},{28,20},{1,9},{5... | collective-permute-start | bytes 49160 | tf_op jit(solution)/shard_map/ppermute | solution.py:275
  14.6 2.6 %collective-permute-start.8 = (bf16[64,128]{1,0:T(8,128)(2,1)S(1)}, bf16[64,128]{1,0:T(8,128)(2,1)S(1)}, u32[]{:S(2)}, u32[]{:S(2)}) collective-permute-start(bf16[64,128]{1,0:T(8,128)(2,1)S(1)} %get-tuple-element.28), channel_id=1, source_target_pairs={{0,16},{4,20},{8,24},{12,28},{16,0},{20,4},{24,8},{28,12},{1,17},{... | collective-permute-start | bytes 49160 | tf_op jit(solution)/shard_map/ppermute | solution.py:275
  17.2 0.2 collective-permute-start.9
  17.4 1.4 %spread.1 = (f32[48,1024]{1,0:T(8,128)S(1)}, bf16[48,1024]{1,0:T(8,128)(2,1)S(1)}, bf16[48,1024]{1,0:T(8,128)(2,1)S(1)}, bf16[48,1024]{1,0:T(8,128)(2,1)S(1)}) custom-call(s32[64]{0:T(128)S(1)} %bitcast_add_fusion.refs_0_, f32[8,4096]{1,0:T(8,128)S(1)} %get-tuple-element.20.refs_1_, bf16[4096,128]{1,0:T(8,128)(2,1)S(1)} %get-tuple-element.19.refs_6_.refs_2_), custom_call_target="tpu_custom_call" | custom-call | tf_op jit(solution)/shard_map/spread/pallas_call | solution.py:280
  18.8 2.2 %collective-permute-start.3 = (bf16[48,1024]{1,0:T(8,128)(2,1)S(1)}, bf16[48,1024]{1,0:T(8,128)(2,1)S(1)}, u32[]{:S(2)}, u32[]{:S(2)}) collective-permute-start(bf16[48,1024]{1,0:T(8,128)(2,1)S(1)} %get-tuple-element.22), channel_id=1, source_target_pairs={{0,3},{1,2},{2,1},{3,0},{4,7},{5,6},{6,5},{7,4},{8,11},{9,10},{10,... | collective-permute-start | bytes 294920 | tf_op jit(solution)/shard_map/ppermute | solution.py:217
  21.0 0.7 %collective-permute-start.4 = (bf16[48,1024]{1,0:T(8,128)(2,1)S(1)}, bf16[48,1024]{1,0:T(8,128)(2,1)S(1)}, u32[]{:S(2)}, u32[]{:S(2)}) collective-permute-start(bf16[48,1024]{1,0:T(8,128)(2,1)S(1)} %get-tuple-element.23), channel_id=1, source_target_pairs={{0,1},{1,0},{2,3},{3,2},{4,5},{5,4},{6,7},{7,6},{8,9},{9,8},{10,11... | collective-permute-start | bytes 294920 | tf_op jit(solution)/shard_map/ppermute | solution.py:217
  21.8 0.0 collective-permute-done.7.refs_7_
  21.8 0.6 %collective-permute-start.5 = (bf16[48,1024]{1,0:T(8,128)(2,1)S(1)}, bf16[48,1024]{1,0:T(8,128)(2,1)S(1)}, u32[]{:S(2)}, u32[]{:S(2)}) collective-permute-start(bf16[48,1024]{1,0:T(8,128)(2,1)S(1)} %get-tuple-element.24), channel_id=1, source_target_pairs={{0,2},{1,3},{2,0},{3,1},{4,6},{5,7},{6,4},{7,5},{8,10},{9,11},{10,... | collective-permute-start | bytes 294920 | tf_op jit(solution)/shard_map/ppermute | solution.py:217
  22.4 0.6 %copy-done.4 = bf16[64,128]{1,0:T(8,128)(2,1)} copy-done((bf16[64,128]{1,0:T(8,128)(2,1)}, bf16[64,128]{1,0:T(8,128)(2,1)S(1)}, u32[]{:S(2)}) %copy-start.4) | copy-done | bytes 16408
  23.0 0.0 collective-permute-done.9.refs_9_
  23.0 0.7 %slice-done = bf16[32,128]{1,0:T(8,128)(2,1)S(1)} async-done(((bf16[64,128]{1,0:T(8,128)(2,1)}), bf16[32,128]{1,0:T(8,128)(2,1)S(1)}, s32[]{:S(2)}) %slice-start) | async-done | bytes 8216 | tf_op jit(solution)/shard_map/slice | solution.py:293
  23.7 0.0 slice-done.1
  23.7 0.1 collective-permute-start.10
  23.8 0.5 %collective-permute-start.6 = (bf16[32,128]{1,0:T(8,128)(2,1)S(1)}, bf16[32,128]{1,0:T(8,128)(2,1)S(1)}, u32[]{:S(2)}, u32[]{:S(2)}) collective-permute-start(bf16[32,128]{1,0:T(8,128)(2,1)S(1)} %get-tuple-element.26), channel_id=1, source_target_pairs={{0,4},{4,0},{8,12},{12,8},{16,20},{20,16},{24,28},{28,24},{1,5},{5... | collective-permute-start | bytes 24584 | tf_op jit(solution)/shard_map/ppermute | solution.py:275
  24.3 0.8 %collective-permute-done.6.refs_5_ = bf16[32,128]{1,0:T(8,128)(2,1)S(1)} collective-permute-done((bf16[32,128]{1,0:T(8,128)(2,1)S(1)}, bf16[32,128]{1,0:T(8,128)(2,1)S(1)}, u32[]{:S(2)}, u32[]{:S(2)}) %collective-permute-start.6) | collective-permute-done | bytes 8224 | tf_op jit(solution)/shard_map/ppermute | solution.py:275
  25.1 0.0 collective-permute-done.10.refs_6_
  25.1 0.5 %collective-permute-done.4.refs_2_ = bf16[48,1024]{1,0:T(8,128)(2,1)S(1)} collective-permute-done((bf16[48,1024]{1,0:T(8,128)(2,1)S(1)}, bf16[48,1024]{1,0:T(8,128)(2,1)S(1)}, u32[]{:S(2)}, u32[]{:S(2)}) %collective-permute-start.4) | collective-permute-done | bytes 98336 | tf_op jit(solution)/shard_map/ppermute | solution.py:217
  25.7 0.7 %collective-permute-done.5.refs_3_ = bf16[48,1024]{1,0:T(8,128)(2,1)S(1)} collective-permute-done((bf16[48,1024]{1,0:T(8,128)(2,1)S(1)}, bf16[48,1024]{1,0:T(8,128)(2,1)S(1)}, u32[]{:S(2)}, u32[]{:S(2)}) %collective-permute-start.5) | collective-permute-done | bytes 98336 | tf_op jit(solution)/shard_map/ppermute | solution.py:217
  26.4 0.8 %finish.1 = (f32[6,8192]{1,0:T(8,128)}, f32[4,8192]{1,0:T(4,128)}) custom-call(f32[48,1024]{1,0:T(8,128)S(1)} %get-tuple-element.21.refs_0_, bf16[48,1024]{1,0:T(8,128)(2,1)S(1)} %collective-permute-done.3.refs_1_, bf16[48,1024]{1,0:T(8,128)(2,1)S(1)} %collective-permute-done.4.refs_2_, bf16[48,1024]{1,0:T(8,128)(2,1)S(1)} %collective-permute-done.5.refs_3_, ...), custom_call_target="tpu_custom_call" | custom-call | tf_op jit(solution)/shard_map/finish/pallas_call | solution.py:295
  (26 shorter events, 0.1 us)
Async XLA Ops:
  0.6 6.4 %copy-start.6 = (s32[4096]{0:T(1024)S(1)}, s32[4096]{0:T(1024)}, u32[]{:S(2)}) copy-start(s32[4096]{0:T(1024)} %param.13) | copy-start | bytes 49156
  0.6 6.4 %copy-start.7 = (s32[4096,1]{0,1:T(1,128)S(1)}, s32[4096,1]{0,1:T(1,128)}, u32[]{:S(2)}) copy-start(s32[4096,1]{0,1:T(1,128)} %param.16) | copy-start | bytes 49156
  1.7 8.4 %collective-permute-start.2 = (bf16[48,1024]{1,0:T(8,128)(2,1)S(1)}, bf16[48,1024]{1,0:T(8,128)(2,1)S(1)}, u32[]{:S(2)}, u32[]{:S(2)}) collective-permute-start(bf16[48,1024]{1,0:T(8,128)(2,1)S(1)} %reshape.28.refs_7_), channel_id=1, source_target_pairs={{0,3},{1,2},{2,1},{3,0},{4,7},{5,6},{6,5},{7,4},{8,11},{9,10},{10,... | collective-permute-start | bytes 294920 | tf_op jit(solution)/shard_map/ppermute | solution.py:217
  5.7 4.9 %collective-permute-start.1 = (bf16[48,1024]{1,0:T(8,128)(2,1)S(1)}, bf16[48,1024]{1,0:T(8,128)(2,1)S(1)}, u32[]{:S(2)}, u32[]{:S(2)}) collective-permute-start(bf16[48,1024]{1,0:T(8,128)(2,1)S(1)} %reshape.28.refs_7_), channel_id=1, source_target_pairs={{0,2},{1,3},{2,0},{3,1},{4,6},{5,7},{6,4},{7,5},{8,10},{9,11},{10,... | collective-permute-start | bytes 294920 | tf_op jit(solution)/shard_map/ppermute | solution.py:217
  6.2 4.7 %collective-permute-start = (bf16[48,1024]{1,0:T(8,128)(2,1)S(1)}, bf16[48,1024]{1,0:T(8,128)(2,1)S(1)}, u32[]{:S(2)}, u32[]{:S(2)}) collective-permute-start(bf16[48,1024]{1,0:T(8,128)(2,1)S(1)} %reshape.28.refs_7_), channel_id=1, source_target_pairs={{0,1},{1,0},{2,3},{3,2},{4,5},{5,4},{6,7},{7,6},{8,9},{9,8},{10,11... | collective-permute-start | bytes 294920 | tf_op jit(solution)/shard_map/ppermute | solution.py:217
  6.3 0.7 %copy-start.10 = (s32[64]{0:T(128)S(1)}, s32[64]{0:T(128)}, u32[]{:S(2)}) copy-start(s32[64]{0:T(128)} %param.12) | copy-start | bytes 772
  6.3 0.7 %copy-start.11 = (s32[64,1]{0,1:T(1,128)S(1)}, s32[64,1]{0,1:T(1,128)}, u32[]{:S(2)}) copy-start(s32[64,1]{0,1:T(1,128)} %param.11) | copy-start | bytes 772
  7.0 0.7 %copy-start.9 = (bf16[16,16]{1,0:T(8,128)(2,1)S(1)}, bf16[16,16]{1,0:T(8,128)(2,1)}, u32[]{:S(2)}) copy-start(bf16[16,16]{1,0:T(8,128)(2,1)} %constant.8.clone.table_ref) | copy-start | bytes 1540
  7.7 1.2 %copy-start = (bf16[64,64,128]{2,1,0:T(8,128)(2,1)S(1)}, bf16[64,64,128]{2,1,0:T(8,128)(2,1)}, u32[]{:S(2)}) copy-start(bf16[64,64,128]{2,1,0:T(8,128)(2,1)} %param.10) | copy-start | bytes 3145732
  8.9 2.0 %copy-start.1 = (f32[3,4096]{1,0:T(4,128)S(1)}, f32[3,4096]{1,0:T(4,128)}, u32[]{:S(2)}) copy-start(f32[3,4096]{1,0:T(4,128)} %refs_2_.1) | copy-start | bytes 147460
  8.9 2.0 %copy-start.8 = (f32[4096]{0:T(1024)S(1)}, f32[4096]{0:T(1024)}, u32[]{:S(2)}) copy-start(f32[4096]{0:T(1024)} %param.14) | copy-start | bytes 49156
  12.9 8.8 %collective-permute-start.7 = (bf16[64,128]{1,0:T(8,128)(2,1)S(1)}, bf16[64,128]{1,0:T(8,128)(2,1)S(1)}, u32[]{:S(2)}, u32[]{:S(2)}) collective-permute-start(bf16[64,128]{1,0:T(8,128)(2,1)S(1)} %get-tuple-element.27), channel_id=1, source_target_pairs={{0,8},{4,12},{8,0},{12,4},{16,24},{20,28},{24,16},{28,20},{1,9},{5... | collective-permute-start | bytes 49160 | tf_op jit(solution)/shard_map/ppermute | solution.py:275
  14.6 7.8 %collective-permute-start.8 = (bf16[64,128]{1,0:T(8,128)(2,1)S(1)}, bf16[64,128]{1,0:T(8,128)(2,1)S(1)}, u32[]{:S(2)}, u32[]{:S(2)}) collective-permute-start(bf16[64,128]{1,0:T(8,128)(2,1)S(1)} %get-tuple-element.28), channel_id=1, source_target_pairs={{0,16},{4,20},{8,24},{12,28},{16,0},{20,4},{24,8},{28,12},{1,17},{... | collective-permute-start | bytes 49160 | tf_op jit(solution)/shard_map/ppermute | solution.py:275
  17.2 5.8 %collective-permute-start.9 = (bf16[64,128]{1,0:T(8,128)(2,1)S(1)}, bf16[64,128]{1,0:T(8,128)(2,1)S(1)}, u32[]{:S(2)}, u32[]{:S(2)}) collective-permute-start(bf16[64,128]{1,0:T(8,128)(2,1)S(1)} %get-tuple-element.29), channel_id=1, source_target_pairs={{0,24},{4,28},{8,16},{12,20},{16,8},{20,12},{24,0},{28,4},{1,25},{... | collective-permute-start | bytes 49160 | tf_op jit(solution)/shard_map/ppermute | solution.py:275
  18.8 6.3 %collective-permute-start.3 = (bf16[48,1024]{1,0:T(8,128)(2,1)S(1)}, bf16[48,1024]{1,0:T(8,128)(2,1)S(1)}, u32[]{:S(2)}, u32[]{:S(2)}) collective-permute-start(bf16[48,1024]{1,0:T(8,128)(2,1)S(1)} %get-tuple-element.22), channel_id=1, source_target_pairs={{0,3},{1,2},{2,1},{3,0},{4,7},{5,6},{6,5},{7,4},{8,11},{9,10},{10,... | collective-permute-start | bytes 294920 | tf_op jit(solution)/shard_map/ppermute | solution.py:217
  21.0 4.6 %collective-permute-start.4 = (bf16[48,1024]{1,0:T(8,128)(2,1)S(1)}, bf16[48,1024]{1,0:T(8,128)(2,1)S(1)}, u32[]{:S(2)}, u32[]{:S(2)}) collective-permute-start(bf16[48,1024]{1,0:T(8,128)(2,1)S(1)} %get-tuple-element.23), channel_id=1, source_target_pairs={{0,1},{1,0},{2,3},{3,2},{4,5},{5,4},{6,7},{7,6},{8,9},{9,8},{10,11... | collective-permute-start | bytes 294920 | tf_op jit(solution)/shard_map/ppermute | solution.py:217
  21.8 0.6 %copy-start.2 = (bf16[64,128]{1,0:T(8,128)(2,1)}, bf16[64,128]{1,0:T(8,128)(2,1)S(1)}, u32[]{:S(2)}) copy-start(bf16[64,128]{1,0:T(8,128)(2,1)S(1)} %collective-permute-done.7.refs_7_) | copy-start | bytes 49156
  21.8 4.6 %collective-permute-start.5 = (bf16[48,1024]{1,0:T(8,128)(2,1)S(1)}, bf16[48,1024]{1,0:T(8,128)(2,1)S(1)}, u32[]{:S(2)}, u32[]{:S(2)}) collective-permute-start(bf16[48,1024]{1,0:T(8,128)(2,1)S(1)} %get-tuple-element.24), channel_id=1, source_target_pairs={{0,2},{1,3},{2,0},{3,1},{4,6},{5,7},{6,4},{7,5},{8,10},{9,11},{10,... | collective-permute-start | bytes 294920 | tf_op jit(solution)/shard_map/ppermute | solution.py:217
  22.4 0.6 %copy-start.4 = (bf16[64,128]{1,0:T(8,128)(2,1)}, bf16[64,128]{1,0:T(8,128)(2,1)S(1)}, u32[]{:S(2)}) copy-start(bf16[64,128]{1,0:T(8,128)(2,1)S(1)} %collective-permute-done.8.refs_8_) | copy-start | bytes 49156
  23.0 0.7 %slice-start = ((bf16[64,128]{1,0:T(8,128)(2,1)}), bf16[32,128]{1,0:T(8,128)(2,1)S(1)}, s32[]{:S(2)}) async-start(bf16[64,128]{1,0:T(8,128)(2,1)} %copy-done.2), calls=%async_computation | async-start | bytes 16384 | tf_op jit(solution)/shard_map/slice | solution.py:293
  23.0 0.7 %slice-start.1 = ((bf16[64,128]{1,0:T(8,128)(2,1)}), bf16[32,128]{1,0:T(8,128)(2,1)S(1)}, s32[]{:S(2)}) async-start(bf16[64,128]{1,0:T(8,128)(2,1)} %copy-done.4), calls=%async_computation.1 | async-start | bytes 16384 | tf_op jit(solution)/shard_map/slice | solution.py:293
  23.7 2.7 %copy-start.3 = (bf16[64,128]{1,0:T(8,128)(2,1)S(1)}, bf16[64,128]{1,0:T(8,128)(2,1)}, u32[]{:S(2)}) copy-start(bf16[64,128]{1,0:T(8,128)(2,1)} %copy-done.2) | copy-start | bytes 49156
  23.7 2.7 %copy-start.5 = (bf16[64,128]{1,0:T(8,128)(2,1)S(1)}, bf16[64,128]{1,0:T(8,128)(2,1)}, u32[]{:S(2)}) copy-start(bf16[64,128]{1,0:T(8,128)(2,1)} %copy-done.4) | copy-start | bytes 49156
  23.7 1.4 %collective-permute-start.10 = (bf16[96,128]{1,0:T(8,128)(2,1)S(1)}, bf16[96,128]{1,0:T(8,128)(2,1)S(1)}, u32[]{:S(2)}, u32[]{:S(2)}) collective-permute-start(bf16[96,128]{1,0:T(8,128)(2,1)S(1)} %pad_maximum_fusion), channel_id=1, source_target_pairs={{0,4},{4,0},{8,12},{12,8},{16,20},{20,16},{24,28},{28,24},{1,5},{5... | collective-permute-start | bytes 73736 | tf_op jit(solution)/shard_map/ppermute | solution.py:275
  23.8 1.3 %collective-permute-start.6 = (bf16[32,128]{1,0:T(8,128)(2,1)S(1)}, bf16[32,128]{1,0:T(8,128)(2,1)S(1)}, u32[]{:S(2)}, u32[]{:S(2)}) collective-permute-start(bf16[32,128]{1,0:T(8,128)(2,1)S(1)} %get-tuple-element.26), channel_id=1, source_target_pairs={{0,4},{4,0},{8,12},{12,8},{16,20},{20,16},{24,28},{28,24},{1,5},{5... | collective-permute-start | bytes 24584 | tf_op jit(solution)/shard_map/ppermute | solution.py:275

commit v3 on v2

v3 whole, which is shorter than its diff:
```python
import functools

import jax
import jax.numpy as jnp
import numpy as np
from jax import lax
from jax.experimental import pallas as pl
from jax.experimental.pallas import tpu as pltpu
from jax.sharding import PartitionSpec as P

NC = 6
NR = 5
NSYS = 12
BLK = 128
SEGB = 64
LANES = 128
SUB = 8
PACK = 4
FIELD = 1 << 16

glide_time = 0.5

VMEM = pl.BlockSpec(memory_space=pltpu.VMEM)
SMEM = pl.BlockSpec(memory_space=pltpu.SMEM)
HBM = pl.BlockSpec(memory_space=pltpu.HBM)
CONTRACT_LANES = (((1,), (1,)), ((), ()))


def slip_signs():
    normal_list = [(1, 1, 1), (-1, 1, 1), (1, -1, 1), (1, 1, -1)]
    table = np.zeros((16, 16), np.int32)
    system = 0
    for x, y, z in normal_list:
        for burgers in ((y, -x, 0), (z, 0, -x), (0, z, -y)):
            outer = np.outer((x, y, z), burgers)
            tensor = outer + outer.T
            table[:NR, system] = (tensor[0, 0] // 2, tensor[1, 1] // 2, tensor[1, 2], tensor[0, 2], tensor[0, 1])
            table[8:11, system] = burgers
            system += 1
    return table


def iota(shape, dim):
    return lax.broadcasted_iota(jnp.int32, shape, dim)


def mask(condition):
    return jnp.where(condition, 1.0, 0.0).astype(jnp.bfloat16)


def pack_kernel(source_ref, owner_ref, local_ref, packed_ref, place_ref, stress_ref, rows_ref, block_ref, sems):
    copies = [
        pltpu.make_async_copy(source_ref, stress_ref, sems.at[0]),
        pltpu.make_async_copy(owner_ref, block_ref.at[0], sems.at[1]),
        pltpu.make_async_copy(local_ref, block_ref.at[1], sems.at[2]),
    ]
    for copy in copies:
        copy.start()
    for copy in copies:
        copy.wait()
    local = block_ref[1]
    place_ref[...] = (block_ref[0] ^ lax.axis_index("grp")) * FIELD + local // SUB * (NR * SUB) + local % SUB
    for block in range(stress_ref.shape[1] // LANES):
        stress = stress_ref[:, block * LANES : (block + 1) * LANES].astype(jnp.float32)
        row = block // SUB * NR * SUB + block % SUB
        rows_ref[pl.ds(row, 2, stride=SUB), :] = stress[:2] - stress[2:3]
        rows_ref[pl.ds(row + 2 * SUB, 3, stride=SUB), :] = stress[3:]
    packed_ref[...] = rows_ref[...].astype(jnp.bfloat16)


def prepare_kernel(slabs, cap, slip_ref, target_ref, source_ref, factor_ref, high_ref, low_ref, weight_ref, sem):
    fetch = pltpu.make_async_copy(source_ref, weight_ref, sem)
    fetch.start()
    segments = slip_ref.shape[1]
    chunks = segments // LANES
    hot = mask(iota((16, segments), 0) == slip_ref[...])
    spot = iota((16, 16), 0) * 16 + iota((16, 16), 1)
    table = jnp.zeros((16, 16), jnp.float32)
    for (row, system), sign in np.ndenumerate(slip_signs()):
        if sign:
            table = jnp.where(spot == row * 16 + system, float(sign), table)
    signs = jnp.dot(table.astype(jnp.bfloat16), hot, preferred_element_type=jnp.float32)
    scale = jnp.where(iota((16, 1), 0) < 8, np.float32(1 / np.sqrt(6.0)), np.float32(1 / np.sqrt(2.0)))
    factor_ref[...] = signs * scale

    target = target_ref[...] ^ lax.axis_index("slab")
    upto = mask(iota((LANES, LANES), 0) <= iota((LANES, LANES), 1))
    ones = jnp.ones((LANES, LANES), jnp.bfloat16)
    before = mask(iota((chunks, chunks), 1) < iota((chunks, chunks), 0))
    slot = target * cap
    for t in range(slabs):
        here = mask(target == t)
        inside = jnp.dot(here, upto, preferred_element_type=jnp.float32)
        total = jnp.dot(here, ones, preferred_element_type=jnp.float32)
        ahead = jnp.dot(before, total.astype(jnp.bfloat16), preferred_element_type=jnp.float32)
        rank = (inside + ahead).astype(jnp.int32) - 1
        slot = slot + jnp.where(target == t, rank, 0)
    high = slot // LANES
    low = slot % LANES
    rows = slabs * cap // LANES
    for r in range(chunks):
        at = pl.ds(r * LANES, LANES)
        high_ref[:, at] = mask(iota((rows, LANES), 0) == high[r : r + 1, :])
        low_ref[:, at] = mask(iota((LANES, LANES), 0) == low[r : r + 1, :])
    fetch.wait()


def glide_kernel(group, slabs, *refs):
    place_ref, mobility_ref, position_ref, factor_ref, high_ref, low_ref, weight_ref = refs[:7]
    stress_refs = refs[7 : 7 + group]
    term_ref = refs[7 + group]
    keep_ref, send_ref = refs[8 + group : 10 + group]
    tiles_ref, step_ref, code_ref, slot_ref, move_ref = refs[10 + group :]
    blocks = place_ref.shape[0]
    rows = stress_refs[0].shape[0]
    for k in range(group):
        tiles_ref[k, :rows, :] = stress_refs[k][...].astype(jnp.float32)

    span = PACK * SEGB
    part = iota((SUB, span), 1) // SEGB
    real = iota((SUB, span), 0) < NR
    for g in range(blocks // PACK):
        tiles = []
        for j in range(PACK):
            spot = place_ref[g * PACK + j]
            tiles.append(tiles_ref[spot // FIELD, pl.ds(spot % FIELD, SUB, stride=SUB), :])
        stress = jnp.concatenate(tiles, axis=0).astype(jnp.bfloat16)
        at = pl.ds(g * span, span)
        crossed = lax.dot_general(stress, weight_ref[at, :], CONTRACT_LANES, preferred_element_type=jnp.float32)
        sampled = crossed[:SUB]
        for j in range(1, PACK):
            sampled = jnp.where(part == j, crossed[j * SUB : (j + 1) * SUB], sampled)
        factors = factor_ref[:SUB, at]
        resolved = jnp.sum(jnp.where(real, factors * sampled, 0.0), axis=0, keepdims=True)
        step = glide_time * mobility_ref[:, at] * resolved
        step_ref[:, at] = step
        term_ref[:, at] = step * factors

    step = step_ref[...]
    high = high_ref[...]
    slot_rows = high.shape[0]
    deep = slot_rows // slabs
    for c in range(4):
        value = step if c == 3 else position_ref[c : c + 1, :] + factor_ref[8 + c : 9 + c, :] * step
        code_ref[c * slot_rows : (c + 1) * slot_rows, :] = high * value.astype(jnp.bfloat16)
    slot_ref[...] = lax.dot_general(code_ref[...], low_ref[...], CONTRACT_LANES, preferred_element_type=jnp.float32)
    for t in range(slabs):
        for c in range(4):
            source = c * slot_rows + t * deep
            move_ref[(t * 4 + c) * deep : (t * 4 + c + 1) * deep, :] = slot_ref[source : source + deep, :]
    half = keep_ref.shape[0]
    keep_ref[...] = move_ref[:half, :].astype(keep_ref.dtype)
    send_ref[...] = move_ref[half:, :].astype(send_ref.dtype)


def spread_kernel(group, *refs):
    place_ref, term_ref, weight_ref, kept_ref = refs[:4]
    sent_refs = refs[4 : 3 + group]
    dense_ref, spread_ref = refs[3 + group :]
    blocks = place_ref.shape[0]
    span = PACK * SEGB
    part = iota((SUB, span), 1) // SEGB
    dense_ref[...] = jnp.zeros_like(dense_ref)
    for g in range(blocks // PACK):
        at = pl.ds(g * span, span)
        term = term_ref[:, at]
        term = jnp.concatenate([jnp.where(part == j, term, 0.0) for j in range(PACK)], axis=0).astype(jnp.bfloat16)
        spread_ref[g * PACK * SUB : (g + 1) * PACK * SUB, :] = jnp.dot(term, weight_ref[at, :], preferred_element_type=jnp.float32)
    for j in range(blocks):
        spot = place_ref[j]
        at = pl.ds(spot % FIELD, NR, stride=SUB)
        dense_ref[spot // FIELD, at, :] = dense_ref[spot // FIELD, at, :] + spread_ref[j * SUB : j * SUB + NR, :]
    kept_ref[...] = dense_ref[0]
    for k in range(1, group):
        sent_refs[k - 1][...] = dense_ref[k].astype(jnp.bfloat16)


def gather_kernel(chunk, picks, *refs):
    for k, (which, place) in enumerate(picks):
        refs[-1][k * chunk : (k + 1) * chunk, :] = refs[which][place * chunk : (place + 1) * chunk, :]


def finish_kernel(group, slabs, picks, *refs):
    kept_ref = refs[0]
    got_refs = refs[1:group]
    moved_refs = refs[group:-4]
    distortion_ref, arrived_ref, sum_ref, slot_ref = refs[-4:]
    total = kept_ref[...]
    for ref in got_refs:
        total = total + ref[...].astype(jnp.float32)
    sum_ref[...] = total
    for block in range(distortion_ref.shape[1] // LANES):
        row = block // SUB * NR * SUB + block % SUB
        part = sum_ref[pl.ds(row, NR, stride=SUB), :]
        at = slice(block * LANES, (block + 1) * LANES)
        distortion_ref[:2, at] = part[:2]
        distortion_ref[2:3, at] = -(part[:1] + part[1:2])
        distortion_ref[3:, at] = part[2:]
    rows = slot_ref.shape[1]
    deep = rows // 4
    for source, (which, place) in picks.items():
        slot_ref[source] = moved_refs[which][place * rows : (place + 1) * rows, :].astype(jnp.float32)
    me = lax.axis_index("slab")
    for s in range(slabs):
        for b in range(deep):
            lane = (s * deep + b) * LANES
            arrived_ref[:, lane : lane + LANES] = slot_ref[me ^ s, pl.ds(b, 4, stride=deep), :]


def body(
    stress, interp_weight, block_owner, block_local, slip_system, mobility, position, target_slab
):
    group = lax.axis_size("grp")
    slabs = lax.axis_size("slab")
    segments = slip_system.shape[0]
    voxels = stress.shape[1]
    cap = 2 * segments // slabs
    slot_rows = slabs * cap // LANES
    f32, bf16 = jnp.float32, jnp.bfloat16
    shape = jax.ShapeDtypeStruct
    params = pltpu.CompilerParams(vmem_limit_bytes=48 * 1024 * 1024)

    def swap(x, k):
        return lax.ppermute(x, "grp", [(i, i ^ k) for i in range(group)])

    peers = sorted(range(1, group), key=lambda k: -bin(k).count("1"))
    blocks = block_local.shape[0]

    def still(x):
        return pltpu.with_memory_space_constraint(x, pltpu.HBM)

    packed, place = pl.pallas_call(
        pack_kernel,
        out_shape=(shape((NR * voxels // LANES, LANES), bf16), shape((1, blocks), jnp.int32)),
        in_specs=[HBM] * 3,
        out_specs=[VMEM] * 2,
        scratch_shapes=[
            pltpu.VMEM(stress.shape, bf16),
            pltpu.VMEM((NR * voxels // LANES, LANES), f32),
            pltpu.VMEM((2, 1, blocks), jnp.int32),
            pltpu.SemaphoreType.DMA((3,)),
        ],
        compiler_params=params,
        name="pack",
    )(still(stress), still(block_owner.reshape(1, blocks)), still(block_local.reshape(1, blocks)))
    place = place.reshape(blocks)
    parts = {k: swap(packed, k) for k in peers}
    parts[0] = packed

    factor, high, low, weight = pl.pallas_call(
        functools.partial(prepare_kernel, slabs, cap),
        out_shape=(
            shape((16, segments), f32),
            shape((slot_rows, segments), bf16),
            shape((LANES, segments), bf16),
            shape((segments, BLK), bf16),
        ),
        in_specs=[VMEM] * 2 + [HBM],
        out_specs=[VMEM] * 4,
        scratch_shapes=[pltpu.SemaphoreType.DMA],
        compiler_params=params,
        name="prepare",
    )(
        slip_system.reshape(1, segments),
        target_slab.reshape(segments // LANES, LANES),
        still(interp_weight.reshape(segments, BLK)),
    )

    tile_shape = (group, packed.shape[0] + (SUB - NR) * SUB, LANES)
    chunk = 4 * slot_rows // slabs
    term, keep, send = pl.pallas_call(
        functools.partial(glide_kernel, group, slabs),
        out_shape=(shape((SUB, segments), f32),) + (shape((slabs // 2 * chunk, LANES), bf16),) * 2,
        in_specs=[SMEM] + [VMEM] * (6 + group),
        out_specs=[VMEM] * 3,
        scratch_shapes=[
            pltpu.VMEM(tile_shape, f32),
            pltpu.VMEM((1, segments), f32),
            pltpu.VMEM((4 * slot_rows, segments), bf16),
            pltpu.VMEM((4 * slot_rows, LANES), f32),
            pltpu.VMEM((4 * slot_rows, LANES), f32),
        ],
        compiler_params=params,
        name="glide",
    )(
        place,
        mobility.reshape(1, segments),
        position,
        factor,
        high,
        low,
        weight,
        *[parts[k] for k in range(group)],
    )

    def hop(x, k):
        return lax.ppermute(x, "slab", [(i, i ^ k) for i in range(slabs)])

    bit = slabs // 2
    arrays = [keep, hop(send, bit)]
    held = {(r, s * bit): (s, r) for r in range(bit) for s in range(2)}
    while bit > 1:
        bit //= 2
        leaving = {key: at for key, at in sorted(held.items(), key=lambda item: item[0][::-1]) if key[0] & bit}
        send = pl.pallas_call(
            functools.partial(gather_kernel, chunk, tuple(leaving.values())),
            out_shape=shape((len(leaving) * chunk, LANES), bf16),
            in_specs=[VMEM] * len(arrays),
            out_specs=VMEM,
            compiler_params=params,
            name="gather",
        )(*arrays)
        for k, key in enumerate(leaving):
            del held[key]
            held[key[0] ^ bit, key[1] | bit] = (len(arrays), k)
        arrays.append(hop(send, bit))

    kept, *sent = pl.pallas_call(
        functools.partial(spread_kernel, group),
        out_shape=(shape(packed.shape, f32),) + (shape(packed.shape, bf16),) * (group - 1),
        in_specs=[SMEM] + [VMEM] * 2,
        out_specs=[VMEM] * group,
        scratch_shapes=[
            pltpu.VMEM((group,) + packed.shape, f32),
            pltpu.VMEM((segments // SEGB * SUB, LANES), f32),
        ],
        compiler_params=params,
        name="spread",
    )(place, term, weight)
    got = [swap(sent[k - 1], k) for k in peers]
    return pl.pallas_call(
        functools.partial(finish_kernel, group, slabs, {s: at for (_, s), at in held.items()}),
        out_shape=(shape((NC, voxels), f32), shape((4, slabs * cap), f32)),
        in_specs=[VMEM] * (group + len(arrays)),
        out_specs=[VMEM] * 2,
        scratch_shapes=[
            pltpu.VMEM(packed.shape, f32),
            pltpu.VMEM((slabs, chunk, LANES), f32),
        ],
        compiler_params=params,
        name="finish",
    )(kept, *got, *arrays)


def solution(mesh):
    placed = (
        P(None, ("slab", "grp")),
        P(("slab", "grp"), None, None),
        P(("slab", "grp"), None),
        P(("slab", "grp")),
        P(("slab", "grp")),
        P(("slab", "grp")),
        P(None, ("slab", "grp")),
        P(("slab", "grp"), None),
    )
    return jax.shard_map(
        body,
        mesh=mesh,
        in_specs=placed,
        out_specs=(P(None, ("slab", "grp")), P(None, ("slab", "grp"))),
        check_vma=False,
    )
```

time: 27.6 us -> 25.9 us (0.938)
  local copies, waits for them, and re-layouts: 4.98 us -> 0.02 us
  waiting for transfers between devices: 2.86 us -> 6.54 us
  starting transfers between devices: 13.2 us -> 12.4 us
  Pallas kernels: 5.48 us -> 6.04 us
    unnamed x24 -> x8, local copies, waits for them, and re-layouts: 3.19 us -> 0.02 us
    ppermute x5 -> x3, waiting for transfers between devices: 0.84 us -> 3.52 us  [hop(): return lax.ppermute(x, 'slab', [(i, i ^ k) for i in range(slabs)])]
    pallas_call x1 -> x4, Pallas kernels: 0.84 us -> 1.94 us  [the longest x1 1.02 us: body(): pl.pallas_call(pack_kernel, out_shape=(shape((NR * voxels // LANES, LANES...]
    reshape x1 -> x0, local copies, waits for them, and re-layouts: 1.08 us -> none  [body(): packed = stress.reshape(NC * SUB, voxels // SUB)]
    ppermute x6, waiting for transfers between devices: 2.02 us -> 3.02 us  [swap(): return lax.ppermute(x, 'grp', [(i, i ^ k) for i in range(group)])]
    ppermute x5 -> x3, starting transfers between devices: 5.01 us -> 4.24 us  [hop(): return lax.ppermute(x, 'slab', [(i, i ^ k) for i in range(slabs)])]
    slice x5 -> x0, local copies, waits for them, and re-layouts: 0.71 us -> none  [body(): across = hop(jnp.concatenate([x[chunk:] for x in far], axis=0), 1)]
    pallas_call x1, Pallas kernels: 1.42 us -> 1.13 us  [body(): pl.pallas_call(functools.partial(spread_kernel, group), out_shape=(shape(...]
  transfers between devices with their start and end apart: 11 -> 9, of which waited for: 5 -> 5; matrix products, arithmetic and copies ran while one was open for 0% -> 0% of each run, Pallas kernels for 10% -> 9%
where the time goes in v3:
time: 25.9 us; the launch traced here: 25.7 us
  starting transfers between devices  12.4 us (48%)
  waiting for transfers between devices  6.54 us (25%)
  Pallas kernels  6.04 us (23%)
  between operations  0.71 us (3%)
    ppermute x6, starting transfers between devices, swap(): return lax.ppermute(x, 'grp', [(i, i ^ k) for i in range(group)])  8.16 us
    ppermute x3, starting transfers between devices, hop(): return lax.ppermute(x, 'slab', [(i, i ^ k) for i in range(slabs)])  4.24 us
    ppermute x3, waiting for transfers between devices, hop(): return lax.ppermute(x, 'slab', [(i, i ^ k) for i in range(slabs)])  3.52 us
    ppermute x6, waiting for transfers between devices, swap(): return lax.ppermute(x, 'grp', [(i, i ^ k) for i in range(group)])  3.02 us
    pallas_call x1, Pallas kernels, body(): pl.pallas_call(functools.partial(glide_kernel, group, slabs), out_shape=(...  1.7 us
    pallas_call x1, Pallas kernels, body(): pl.pallas_call(functools.partial(prepare_kernel, slabs, cap), out_shape=(...  1.27 us
    pallas_call x1, Pallas kernels, body(): pl.pallas_call(functools.partial(spread_kernel, group), out_shape=(shape(...  1.13 us
    pallas_call x1, Pallas kernels, body(): pl.pallas_call(pack_kernel, out_shape=(shape((NR * voxels // LANES, LANES...  1.02 us
  transfers between devices with their start and end apart: 9, of which 5 were waited for; matrix products, arithmetic and copies ran while one was open for 0% of the time, Pallas kernels for 9%

profile of v3, /device:TPU:0, one launch (start us, length us, event | category | flops | bytes accessed | tf_op | source)
XLA Modules:
  0.0 25.7 jit_solution(3859589831799168468)
XLA Ops:
  0.6 0.0 copy-start.1
  0.6 0.0 copy-start.2
  0.7 1.0 %pack.1 = (bf16[320,128]{1,0:T(8,128)(2,1)S(1)}, s32[1,64]{1,0:T(1,128)S(1)}) custom-call(bf16[6,8192]{1,0:T(8,128)(2,1)} %source_ref.1, s32[1,64]{1,0:T(1,128)} %bitcast.13, s32[1,64]{1,0:T(1,128)} %bitcast.14), custom_call_target="tpu_custom_call" | custom-call | tf_op jit(solution)/shard_map/pack/pallas_call | solution.py:232
  1.7 4.0 %collective-permute-start.2 = (bf16[320,128]{1,0:T(8,128)(2,1)S(1)}, bf16[320,128]{1,0:T(8,128)(2,1)S(1)}, u32[]{:S(2)}, u32[]{:S(2)}) collective-permute-start(bf16[320,128]{1,0:T(8,128)(2,1)S(1)} %get-tuple-element.20.refs_7_), channel_id=1, source_target_pairs={{0,3},{1,2},{2,1},{3,0},{4,7},{5,6},{6,5},{7,4},{8,11},{9,10},{10,... | collective-permute-start | bytes 245768 | tf_op jit(solution)/shard_map/ppermute | solution.py:224
  5.6 0.5 %collective-permute-start.1 = (bf16[320,128]{1,0:T(8,128)(2,1)S(1)}, bf16[320,128]{1,0:T(8,128)(2,1)S(1)}, u32[]{:S(2)}, u32[]{:S(2)}) collective-permute-start(bf16[320,128]{1,0:T(8,128)(2,1)S(1)} %get-tuple-element.20.refs_7_), channel_id=1, source_target_pairs={{0,2},{1,3},{2,0},{3,1},{4,6},{5,7},{6,4},{7,5},{8,10},{9,11},{10,... | collective-permute-start | bytes 245768 | tf_op jit(solution)/shard_map/ppermute | solution.py:224
  6.1 0.1 collective-permute-start
  6.3 0.0 copy-done.1
  6.3 0.0 copy-done.2
  6.3 0.0 copy-start
  6.3 0.0 copy-start.3
  6.3 1.3 %prepare.1 = (f32[16,4096]{1,0:T(8,128)S(1)}, bf16[64,4096]{1,0:T(8,128)(2,1)S(1)}, bf16[128,4096]{1,0:T(8,128)(2,1)S(1)}, bf16[4096,128]{1,0:T(8,128)(2,1)S(1)}) custom-call(s32[1,4096]{1,0:T(1,128)S(1)} %bitcast.7, s32[32,128]{1,0:T(8,128)S(1)} %bitcast.8, bf16[4096,128]{1,0:T(8,128)(2,1)} %bitcast.12), custom_call_target="tpu_custom_call" | custom-call | tf_op jit(solution)/shard_map/prepare/pallas_call | solution.py:250
  7.6 0.6 %collective-permute-done.2.refs_10_ = bf16[320,128]{1,0:T(8,128)(2,1)S(1)} collective-permute-done((bf16[320,128]{1,0:T(8,128)(2,1)S(1)}, bf16[320,128]{1,0:T(8,128)(2,1)S(1)}, u32[]{:S(2)}, u32[]{:S(2)}) %collective-permute-start.2) | collective-permute-done | bytes 81952 | tf_op jit(solution)/shard_map/ppermute | solution.py:224
  8.2 1.9 %collective-permute-done.1.refs_9_ = bf16[320,128]{1,0:T(8,128)(2,1)S(1)} collective-permute-done((bf16[320,128]{1,0:T(8,128)(2,1)S(1)}, bf16[320,128]{1,0:T(8,128)(2,1)S(1)}, u32[]{:S(2)}, u32[]{:S(2)}) %collective-permute-start.1) | collective-permute-done | bytes 81952 | tf_op jit(solution)/shard_map/ppermute | solution.py:224
  10.1 0.5 %collective-permute-done.refs_8_ = bf16[320,128]{1,0:T(8,128)(2,1)S(1)} collective-permute-done((bf16[320,128]{1,0:T(8,128)(2,1)S(1)}, bf16[320,128]{1,0:T(8,128)(2,1)S(1)}, u32[]{:S(2)}, u32[]{:S(2)}) %collective-permute-start) | collective-permute-done | bytes 81952 | tf_op jit(solution)/shard_map/ppermute | solution.py:224
  10.6 0.0 copy-done
  10.6 0.0 copy-done.3
  10.6 1.7 %glide.1 = (f32[8,4096]{1,0:T(8,128)S(1)}, bf16[128,128]{1,0:T(8,128)(2,1)S(1)}, bf16[128,128]{1,0:T(8,128)(2,1)S(1)}) custom-call(s32[64]{0:T(128)S(1)} %bitcast.10, f32[1,4096]{1,0:T(1,128)S(1)} %bitcast.9, f32[3,4096]{1,0:T(4,128)S(1)} %copy-done, f32[16,4096]{1,0:T(8,128)S(1)} %get-tuple-element.16.refs_3_, ...), custom_call_target="tpu_custom_call" | custom-call | tf_op jit(solution)/shard_map/glide/pallas_call | solution.py:271
  12.3 2.7 %collective-permute-start.6 = (bf16[128,128]{1,0:T(8,128)(2,1)S(1)}, bf16[128,128]{1,0:T(8,128)(2,1)S(1)}, u32[]{:S(2)}, u32[]{:S(2)}) collective-permute-start(bf16[128,128]{1,0:T(8,128)(2,1)S(1)} %get-tuple-element.27), channel_id=1, source_target_pairs={{0,16},{4,20},{8,24},{12,28},{16,0},{20,4},{24,8},{28,12},{1,17},{... | collective-permute-start | bytes 98312 | tf_op jit(solution)/shard_map/ppermute | solution.py:297
  15.0 1.1 %spread.1 = (f32[320,128]{1,0:T(8,128)S(1)}, bf16[320,128]{1,0:T(8,128)(2,1)S(1)}, bf16[320,128]{1,0:T(8,128)(2,1)S(1)}, bf16[320,128]{1,0:T(8,128)(2,1)S(1)}) custom-call(s32[64]{0:T(128)S(1)} %bitcast.11, f32[8,4096]{1,0:T(8,128)S(1)} %get-tuple-element.21.refs_1_, bf16[4096,128]{1,0:T(8,128)(2,1)S(1)} %get-tuple-element.19.refs_6_.refs_2_), custom_call_target="tpu_custom_call" | custom-call | tf_op jit(solution)/shard_map/spread/pallas_call | solution.py:318
  16.1 1.6 %collective-permute-start.3 = (bf16[320,128]{1,0:T(8,128)(2,1)S(1)}, bf16[320,128]{1,0:T(8,128)(2,1)S(1)}, u32[]{:S(2)}, u32[]{:S(2)}) collective-permute-start(bf16[320,128]{1,0:T(8,128)(2,1)S(1)} %get-tuple-element.23), channel_id=1, source_target_pairs={{0,3},{1,2},{2,1},{3,0},{4,7},{5,6},{6,5},{7,4},{8,11},{9,10},{10,... | collective-permute-start | bytes 245768 | tf_op jit(solution)/shard_map/ppermute | solution.py:224
  17.7 1.5 %collective-permute-start.4 = (bf16[320,128]{1,0:T(8,128)(2,1)S(1)}, bf16[320,128]{1,0:T(8,128)(2,1)S(1)}, u32[]{:S(2)}, u32[]{:S(2)}) collective-permute-start(bf16[320,128]{1,0:T(8,128)(2,1)S(1)} %get-tuple-element.24), channel_id=1, source_target_pairs={{0,1},{1,0},{2,3},{3,2},{4,5},{5,4},{6,7},{7,6},{8,9},{9,8},{10,11... | collective-permute-start | bytes 245768 | tf_op jit(solution)/shard_map/ppermute | solution.py:224
  19.1 0.5 %collective-permute-start.5 = (bf16[320,128]{1,0:T(8,128)(2,1)S(1)}, bf16[320,128]{1,0:T(8,128)(2,1)S(1)}, u32[]{:S(2)}, u32[]{:S(2)}) collective-permute-start(bf16[320,128]{1,0:T(8,128)(2,1)S(1)} %get-tuple-element.25), channel_id=1, source_target_pairs={{0,2},{1,3},{2,0},{3,1},{4,6},{5,7},{6,4},{7,5},{8,10},{9,11},{10,... | collective-permute-start | bytes 245768 | tf_op jit(solution)/shard_map/ppermute | solution.py:224
  19.6 0.0 collective-permute-done.6.refs_1_.refs_5_
  19.7 1.6 %collective-permute-start.7 = (bf16[128,128]{1,0:T(8,128)(2,1)S(1)}, bf16[128,128]{1,0:T(8,128)(2,1)S(1)}, u32[]{:S(2)}, u32[]{:S(2)}) collective-permute-start(bf16[128,128]{1,0:T(8,128)(2,1)S(1)} %gather.2), channel_id=1, source_target_pairs={{0,8},{4,12},{8,0},{12,4},{16,24},{20,28},{24,16},{28,20},{1,9},{5... | collective-permute-start | bytes 98312 | tf_op jit(solution)/shard_map/ppermute | solution.py:297
  21.2 2.3 %collective-permute-done.7.refs_2_.refs_6_ = bf16[128,128]{1,0:T(8,128)(2,1)S(1)} collective-permute-done((bf16[128,128]{1,0:T(8,128)(2,1)S(1)}, bf16[128,128]{1,0:T(8,128)(2,1)S(1)}, u32[]{:S(2)}, u32[]{:S(2)}) %collective-permute-start.7) | collective-permute-done | bytes 32800 | tf_op jit(solution)/shard_map/ppermute | solution.py:297
  23.6 0.0 collective-permute-start.8
  23.6 0.0 collective-permute-done.3.refs_1_
  23.6 0.0 collective-permute-done.4.refs_2_
  23.6 0.0 collective-permute-done.5.refs_3_
  23.6 1.2 %collective-permute-done.8.refs_7_ = bf16[128,128]{1,0:T(8,128)(2,1)S(1)} collective-permute-done((bf16[128,128]{1,0:T(8,128)(2,1)S(1)}, bf16[128,128]{1,0:T(8,128)(2,1)S(1)}, u32[]{:S(2)}, u32[]{:S(2)}) %collective-permute-start.8) | collective-permute-done | bytes 32800 | tf_op jit(solution)/shard_map/ppermute | solution.py:297
  24.8 0.9 %finish.1 = (f32[6,8192]{1,0:T(8,128)}, f32[4,8192]{1,0:T(4,128)}) custom-call(f32[320,128]{1,0:T(8,128)S(1)} %get-tuple-element.22.refs_0_, bf16[320,128]{1,0:T(8,128)(2,1)S(1)} %collective-permute-done.3.refs_1_, bf16[320,128]{1,0:T(8,128)(2,1)S(1)} %collective-permute-done.4.refs_2_, bf16[320,128]{1,0:T(8,128)(2,1)S(1)} %collective-permute-done.5.refs_3_, ...), custom_call_target="tpu_custom_call" | custom-call | tf_op jit(solution)/shard_map/finish/pallas_call | solution.py:331
  (2 shorter events, 0.0 us)
Async XLA Ops:
  0.6 5.7 %copy-start.1 = (s32[4096]{0:T(1024)S(1)}, s32[4096]{0:T(1024)}, u32[]{:S(2)}) copy-start(s32[4096]{0:T(1024)} %param.12) | copy-start | bytes 49156
  0.6 5.6 %copy-start.2 = (s32[4096,1]{0,1:T(1,128)S(1)}, s32[4096,1]{0,1:T(1,128)}, u32[]{:S(2)}) copy-start(s32[4096,1]{0,1:T(1,128)} %param.15) | copy-start | bytes 49156
  1.7 6.5 %collective-permute-start.2 = (bf16[320,128]{1,0:T(8,128)(2,1)S(1)}, bf16[320,128]{1,0:T(8,128)(2,1)S(1)}, u32[]{:S(2)}, u32[]{:S(2)}) collective-permute-start(bf16[320,128]{1,0:T(8,128)(2,1)S(1)} %get-tuple-element.20.refs_7_), channel_id=1, source_target_pairs={{0,3},{1,2},{2,1},{3,0},{4,7},{5,6},{6,5},{7,4},{8,11},{9,10},{10,... | collective-permute-start | bytes 245768 | tf_op jit(solution)/shard_map/ppermute | solution.py:224
  5.6 4.4 %collective-permute-start.1 = (bf16[320,128]{1,0:T(8,128)(2,1)S(1)}, bf16[320,128]{1,0:T(8,128)(2,1)S(1)}, u32[]{:S(2)}, u32[]{:S(2)}) collective-permute-start(bf16[320,128]{1,0:T(8,128)(2,1)S(1)} %get-tuple-element.20.refs_7_), channel_id=1, source_target_pairs={{0,2},{1,3},{2,0},{3,1},{4,6},{5,7},{6,4},{7,5},{8,10},{9,11},{10,... | collective-permute-start | bytes 245768 | tf_op jit(solution)/shard_map/ppermute | solution.py:224
  6.1 4.4 %collective-permute-start = (bf16[320,128]{1,0:T(8,128)(2,1)S(1)}, bf16[320,128]{1,0:T(8,128)(2,1)S(1)}, u32[]{:S(2)}, u32[]{:S(2)}) collective-permute-start(bf16[320,128]{1,0:T(8,128)(2,1)S(1)} %get-tuple-element.20.refs_7_), channel_id=1, source_target_pairs={{0,1},{1,0},{2,3},{3,2},{4,5},{5,4},{6,7},{7,6},{8,9},{9,8},{10,11... | collective-permute-start | bytes 245768 | tf_op jit(solution)/shard_map/ppermute | solution.py:224
  6.3 4.3 %copy-start = (f32[3,4096]{1,0:T(4,128)S(1)}, f32[3,4096]{1,0:T(4,128)}, u32[]{:S(2)}) copy-start(f32[3,4096]{1,0:T(4,128)} %refs_2_.1) | copy-start | bytes 147460
  6.3 4.3 %copy-start.3 = (f32[4096]{0:T(1024)S(1)}, f32[4096]{0:T(1024)}, u32[]{:S(2)}) copy-start(f32[4096]{0:T(1024)} %param.13) | copy-start | bytes 49156
  12.3 7.3 %collective-permute-start.6 = (bf16[128,128]{1,0:T(8,128)(2,1)S(1)}, bf16[128,128]{1,0:T(8,128)(2,1)S(1)}, u32[]{:S(2)}, u32[]{:S(2)}) collective-permute-start(bf16[128,128]{1,0:T(8,128)(2,1)S(1)} %get-tuple-element.27), channel_id=1, source_target_pairs={{0,16},{4,20},{8,24},{12,28},{16,0},{20,4},{24,8},{28,12},{1,17},{... | collective-permute-start | bytes 98312 | tf_op jit(solution)/shard_map/ppermute | solution.py:297
  16.1 7.5 %collective-permute-start.3 = (bf16[320,128]{1,0:T(8,128)(2,1)S(1)}, bf16[320,128]{1,0:T(8,128)(2,1)S(1)}, u32[]{:S(2)}, u32[]{:S(2)}) collective-permute-start(bf16[320,128]{1,0:T(8,128)(2,1)S(1)} %get-tuple-element.23), channel_id=1, source_target_pairs={{0,3},{1,2},{2,1},{3,0},{4,7},{5,6},{6,5},{7,4},{8,11},{9,10},{10,... | collective-permute-start | bytes 245768 | tf_op jit(solution)/shard_map/ppermute | solution.py:224
  17.7 5.9 %collective-permute-start.4 = (bf16[320,128]{1,0:T(8,128)(2,1)S(1)}, bf16[320,128]{1,0:T(8,128)(2,1)S(1)}, u32[]{:S(2)}, u32[]{:S(2)}) collective-permute-start(bf16[320,128]{1,0:T(8,128)(2,1)S(1)} %get-tuple-element.24), channel_id=1, source_target_pairs={{0,1},{1,0},{2,3},{3,2},{4,5},{5,4},{6,7},{7,6},{8,9},{9,8},{10,11... | collective-permute-start | bytes 245768 | tf_op jit(solution)/shard_map/ppermute | solution.py:224
  19.1 4.4 %collective-permute-start.5 = (bf16[320,128]{1,0:T(8,128)(2,1)S(1)}, bf16[320,128]{1,0:T(8,128)(2,1)S(1)}, u32[]{:S(2)}, u32[]{:S(2)}) collective-permute-start(bf16[320,128]{1,0:T(8,128)(2,1)S(1)} %get-tuple-element.25), channel_id=1, source_target_pairs={{0,2},{1,3},{2,0},{3,1},{4,6},{5,7},{6,4},{7,5},{8,10},{9,11},{10,... | collective-permute-start | bytes 245768 | tf_op jit(solution)/shard_map/ppermute | solution.py:224
  19.7 3.9 %collective-permute-start.7 = (bf16[128,128]{1,0:T(8,128)(2,1)S(1)}, bf16[128,128]{1,0:T(8,128)(2,1)S(1)}, u32[]{:S(2)}, u32[]{:S(2)}) collective-permute-start(bf16[128,128]{1,0:T(8,128)(2,1)S(1)} %gather.2), channel_id=1, source_target_pairs={{0,8},{4,12},{8,0},{12,4},{16,24},{20,28},{24,16},{28,20},{1,9},{5... | collective-permute-start | bytes 98312 | tf_op jit(solution)/shard_map/ppermute | solution.py:297
  23.6 1.2 %collective-permute-start.8 = (bf16[128,128]{1,0:T(8,128)(2,1)S(1)}, bf16[128,128]{1,0:T(8,128)(2,1)S(1)}, u32[]{:S(2)}, u32[]{:S(2)}) collective-permute-start(bf16[128,128]{1,0:T(8,128)(2,1)S(1)} %gather.3), channel_id=1, source_target_pairs={{0,4},{4,0},{8,12},{12,8},{16,20},{20,16},{24,28},{28,24},{1,5},{5... | collective-permute-start | bytes 98312 | tf_op jit(solution)/shard_map/ppermute | solution.py:297

commit v4 on v3

--- a/solution.py
+++ b/solution.py
@@ -16,12 +16,10 @@
 LANES = 128
 SUB = 8
 PACK = 4
-FIELD = 1 << 16
 
 glide_time = 0.5
 
 VMEM = pl.BlockSpec(memory_space=pltpu.VMEM)
-SMEM = pl.BlockSpec(memory_space=pltpu.SMEM)
 HBM = pl.BlockSpec(memory_space=pltpu.HBM)
 CONTRACT_LANES = (((1,), (1,)), ((), ()))
 
@@ -58,17 +56,19 @@
         copy.start()
     for copy in copies:
         copy.wait()
-    local = block_ref[1]
-    place_ref[...] = (block_ref[0] ^ lax.axis_index("grp")) * FIELD + local // SUB * (NR * SUB) + local % SUB
-    for block in range(stress_ref.shape[1] // LANES):
+    blocks = stress_ref.shape[1] // LANES
+    place_ref[...] = (block_ref[0] ^ lax.axis_index("grp")) * blocks + block_ref[1]
+    for block in range(blocks):
         stress = stress_ref[:, block * LANES : (block + 1) * LANES].astype(jnp.float32)
-        row = block // SUB * NR * SUB + block % SUB
-        rows_ref[pl.ds(row, 2, stride=SUB), :] = stress[:2] - stress[2:3]
-        rows_ref[pl.ds(row + 2 * SUB, 3, stride=SUB), :] = stress[3:]
+        rows_ref[pl.ds(block, 2, stride=blocks), :] = stress[:2] - stress[2:3]
+        rows_ref[pl.ds(block + 2 * blocks, 3, stride=blocks), :] = stress[3:]
     packed_ref[...] = rows_ref[...].astype(jnp.bfloat16)
 
 
-def prepare_kernel(slabs, cap, slip_ref, target_ref, source_ref, factor_ref, high_ref, low_ref, weight_ref, sem):
+def prepare_kernel(slabs, cap, *refs):
+    slip_ref, target_ref, place_ref, position_ref, source_ref = refs[:5]
+    factor_ref, high_ref, low_ref, pick_ref, put_ref, start_ref, course_ref, weight_ref = refs[5:13]
+    code_ref, sem = refs[13:]
     fetch = pltpu.make_async_copy(source_ref, weight_ref, sem)
     fetch.start()
     segments = slip_ref.shape[1]
@@ -81,7 +81,13 @@
             table = jnp.where(spot == row * 16 + system, float(sign), table)
     signs = jnp.dot(table.astype(jnp.bfloat16), hot, preferred_element_type=jnp.float32)
     scale = jnp.where(iota((16, 1), 0) < 8, np.float32(1 / np.sqrt(6.0)), np.float32(1 / np.sqrt(2.0)))
-    factor_ref[...] = signs * scale
+    factors = signs * scale
+    factor_ref[...] = factors[:SUB]
+    blocks, choices = pick_ref.shape
+    place = jnp.concatenate([place_ref[...], place_ref[...]], axis=1)
+    put = jnp.where(iota((choices, 2 * blocks), 0) == place, 1.0, 0.0)
+    put_ref[...] = put.astype(jnp.bfloat16)
+    pick_ref[...] = put.T[:blocks].astype(jnp.bfloat16)
 
     target = target_ref[...] ^ lax.axis_index("slab")
     upto = mask(iota((LANES, LANES), 0) <= iota((LANES, LANES), 1))
@@ -102,19 +108,30 @@
         at = pl.ds(r * LANES, LANES)
         high_ref[:, at] = mask(iota((rows, LANES), 0) == high[r : r + 1, :])
         low_ref[:, at] = mask(iota((LANES, LANES), 0) == low[r : r + 1, :])
+    codes = high_ref[...]
+    for c in range(3):
+        code_ref[c * rows : (c + 1) * rows, :] = codes * position_ref[c : c + 1, :].astype(jnp.bfloat16)
+        code_ref[(3 + c) * rows : (4 + c) * rows, :] = codes * signs[8 + c : 9 + c, :].astype(jnp.bfloat16)
+    slots = lax.dot_general(code_ref[...], low_ref[...], CONTRACT_LANES, preferred_element_type=jnp.float32)
+    start_ref[...] = slots[: 3 * rows]
+    course_ref[...] = slots[3 * rows :] * np.float32(1 / np.sqrt(2.0))
     fetch.wait()
 
 
-def glide_kernel(group, slabs, *refs):
-    place_ref, mobility_ref, position_ref, factor_ref, high_ref, low_ref, weight_ref = refs[:7]
-    stress_refs = refs[7 : 7 + group]
-    term_ref = refs[7 + group]
-    keep_ref, send_ref = refs[8 + group : 10 + group]
-    tiles_ref, step_ref, code_ref, slot_ref, move_ref = refs[10 + group :]
-    blocks = place_ref.shape[0]
-    rows = stress_refs[0].shape[0]
-    for k in range(group):
-        tiles_ref[k, :rows, :] = stress_refs[k][...].astype(jnp.float32)
+def glide_kernel(order, slabs, *refs):
+    pick_ref, mobility_ref, factor_ref, high_ref, low_ref, start_ref, course_ref, weight_ref = refs[:8]
+    group = len(order)
+    stress_refs = [refs[8 + order.index(k)] for k in range(group)]
+    term_ref = refs[8 + group]
+    keep_ref, send_ref = refs[9 + group : 11 + group]
+    tiles_ref, step_ref, move_ref = refs[11 + group :]
+    blocks = pick_ref.shape[0]
+    held = stress_refs[0].shape[0] // NR
+    for c in range(NR):
+        stress = jnp.concatenate([ref[c * held : (c + 1) * held, :] for ref in stress_refs], axis=0)
+        picked = jnp.dot(pick_ref[...], stress, preferred_element_type=jnp.float32)
+        for j in range(0, blocks, SUB):
+            tiles_ref[(j + c) * SUB : (j + c + 1) * SUB, :] = picked[j : j + SUB]
 
     span = PACK * SEGB
     part = iota((SUB, span), 1) // SEGB
@@ -122,15 +139,15 @@
     for g in range(blocks // PACK):
         tiles = []
         for j in range(PACK):
-            spot = place_ref[g * PACK + j]
-            tiles.append(tiles_ref[spot // FIELD, pl.ds(spot % FIELD, SUB, stride=SUB), :])
+            block = g * PACK + j
+            tiles.append(tiles_ref[pl.ds(block // SUB * SUB * SUB + block % SUB, SUB, stride=SUB), :])
         stress = jnp.concatenate(tiles, axis=0).astype(jnp.bfloat16)
         at = pl.ds(g * span, span)
         crossed = lax.dot_general(stress, weight_ref[at, :], CONTRACT_LANES, preferred_element_type=jnp.float32)
         sampled = crossed[:SUB]
         for j in range(1, PACK):
             sampled = jnp.where(part == j, crossed[j * SUB : (j + 1) * SUB], sampled)
-        factors = factor_ref[:SUB, at]
+        factors = factor_ref[:, at]
         resolved = jnp.sum(jnp.where(real, factors * sampled, 0.0), axis=0, keepdims=True)
         step = glide_time * mobility_ref[:, at] * resolved
         step_ref[:, at] = step
@@ -140,39 +157,42 @@
     high = high_ref[...]
     slot_rows = high.shape[0]
     deep = slot_rows // slabs
+    step = lax.dot_general(high * step.astype(jnp.bfloat16), low_ref[...], CONTRACT_LANES, preferred_element_type=jnp.float32)
     for c in range(4):
-        value = step if c == 3 else position_ref[c : c + 1, :] + factor_ref[8 + c : 9 + c, :] * step
-        code_ref[c * slot_rows : (c + 1) * slot_rows, :] = high * value.astype(jnp.bfloat16)
-    slot_ref[...] = lax.dot_general(code_ref[...], low_ref[...], CONTRACT_LANES, preferred_element_type=jnp.float32)
-    for t in range(slabs):
-        for c in range(4):
-            source = c * slot_rows + t * deep
-            move_ref[(t * 4 + c) * deep : (t * 4 + c + 1) * deep, :] = slot_ref[source : source + deep, :]
+        value = step
+        if c < 3:
+            at = slice(c * slot_rows, (c + 1) * slot_rows)
+            value = start_ref[at, :] + course_ref[at, :] * step
+        for t in range(slabs):
+            row = (t * 4 + c) * deep
+            move_ref[row : row + deep, :] = value[t * deep : (t + 1) * deep]
     half = keep_ref.shape[0]
     keep_ref[...] = move_ref[:half, :].astype(keep_ref.dtype)
     send_ref[...] = move_ref[half:, :].astype(send_ref.dtype)
 
 
 def spread_kernel(group, *refs):
-    place_ref, term_ref, weight_ref, kept_ref = refs[:4]
+    put_ref, term_ref, weight_ref, kept_ref = refs[:4]
     sent_refs = refs[4 : 3 + group]
-    dense_ref, spread_ref = refs[3 + group :]
-    blocks = place_ref.shape[0]
+    spread_ref = refs[3 + group]
+    blocks = put_ref.shape[1] // 2
+    held = kept_ref.shape[0] // NR
     span = PACK * SEGB
     part = iota((SUB, span), 1) // SEGB
-    dense_ref[...] = jnp.zeros_like(dense_ref)
     for g in range(blocks // PACK):
         at = pl.ds(g * span, span)
         term = term_ref[:, at]
         term = jnp.concatenate([jnp.where(part == j, term, 0.0) for j in range(PACK)], axis=0).astype(jnp.bfloat16)
         spread_ref[g * PACK * SUB : (g + 1) * PACK * SUB, :] = jnp.dot(term, weight_ref[at, :], preferred_element_type=jnp.float32)
-    for j in range(blocks):
-        spot = place_ref[j]
-        at = pl.ds(spot % FIELD, NR, stride=SUB)
-        dense_ref[spot // FIELD, at, :] = dense_ref[spot // FIELD, at, :] + spread_ref[j * SUB : j * SUB + NR, :]
-    kept_ref[...] = dense_ref[0]
-    for k in range(1, group):
-        sent_refs[k - 1][...] = dense_ref[k].astype(jnp.bfloat16)
+    for c in range(NR):
+        spread = spread_ref[pl.ds(c, blocks, stride=SUB), :]
+        rounded = spread.astype(jnp.bfloat16)
+        rest = (spread - rounded.astype(jnp.float32)).astype(jnp.bfloat16)
+        dense = jnp.dot(put_ref[...], jnp.concatenate([rounded, rest], axis=0), preferred_element_type=jnp.float32)
+        rows = slice(c * held, (c + 1) * held)
+        kept_ref[rows, :] = dense[:held]
+        for k in range(1, group):
+            sent_refs[k - 1][rows, :] = dense[k * held : (k + 1) * held].astype(jnp.bfloat16)
 
 
 def gather_kernel(chunk, picks, *refs):
@@ -188,10 +208,12 @@
     total = kept_ref[...]
     for ref in got_refs:
         total = total + ref[...].astype(jnp.float32)
-    sum_ref[...] = total
+    held = total.shape[0] // NR
+    for c in range(NR):
+        for b in range(0, held, SUB):
+            sum_ref[b * NR + c * SUB : b * NR + (c + 1) * SUB, :] = total[c * held + b : c * held + b + SUB]
     for block in range(distortion_ref.shape[1] // LANES):
-        row = block // SUB * NR * SUB + block % SUB
-        part = sum_ref[pl.ds(row, NR, stride=SUB), :]
+        part = sum_ref[pl.ds(block // SUB * NR * SUB + block % SUB, NR, stride=SUB), :]
         at = slice(block * LANES, (block + 1) * LANES)
         distortion_ref[:2, at] = part[:2]
         distortion_ref[2:3, at] = -(part[:1] + part[1:2])
@@ -243,54 +265,59 @@
         compiler_params=params,
         name="pack",
     )(still(stress), still(block_owner.reshape(1, blocks)), still(block_local.reshape(1, blocks)))
-    place = place.reshape(blocks)
     parts = {k: swap(packed, k) for k in peers}
     parts[0] = packed
-
-    factor, high, low, weight = pl.pallas_call(
+    order = [0, *peers]
+
+    slot_shape = (3 * slot_rows, LANES)
+    factor, high, low, pick, put, start, course, weight = pl.pallas_call(
         functools.partial(prepare_kernel, slabs, cap),
         out_shape=(
-            shape((16, segments), f32),
+            shape((SUB, segments), f32),
             shape((slot_rows, segments), bf16),
             shape((LANES, segments), bf16),
+            shape((blocks, group * voxels // BLK), bf16),
+            shape((group * voxels // BLK, 2 * blocks), bf16),
+            shape(slot_shape, f32),
+            shape(slot_shape, f32),
             shape((segments, BLK), bf16),
         ),
-        in_specs=[VMEM] * 2 + [HBM],
-        out_specs=[VMEM] * 4,
-        scratch_shapes=[pltpu.SemaphoreType.DMA],
+        in_specs=[VMEM] * 4 + [HBM],
+        out_specs=[VMEM] * 8,
+        scratch_shapes=[pltpu.VMEM((6 * slot_rows, segments), bf16), pltpu.SemaphoreType.DMA],
         compiler_params=params,
         name="prepare",
     )(
         slip_system.reshape(1, segments),
         target_slab.reshape(segments // LANES, LANES),
+        place,
+        position,
         still(interp_weight.reshape(segments, BLK)),
     )
 
-    tile_shape = (group, packed.shape[0] + (SUB - NR) * SUB, LANES)
     chunk = 4 * slot_rows // slabs
     term, keep, send = pl.pallas_call(
-        functools.partial(glide_kernel, group, slabs),
+        functools.partial(glide_kernel, order, slabs),
         out_shape=(shape((SUB, segments), f32),) + (shape((slabs // 2 * chunk, LANES), bf16),) * 2,
-        in_specs=[SMEM] + [VMEM] * (6 + group),
+        in_specs=[VMEM] * (8 + group),
         out_specs=[VMEM] * 3,
         scratch_shapes=[
-            pltpu.VMEM(tile_shape, f32),
+            pltpu.VMEM((SUB * blocks, LANES), f32),
             pltpu.VMEM((1, segments), f32),
-            pltpu.VMEM((4 * slot_rows, segments), bf16),
-            pltpu.VMEM((4 * slot_rows, LANES), f32),
             pltpu.VMEM((4 * slot_rows, LANES), f32),
         ],
         compiler_params=params,
         name="glide",
     )(
-        place,
+        pick,
         mobility.reshape(1, segments),
-        position,
         factor,
         high,
         low,
+        start,
+        course,
         weight,
-        *[parts[k] for k in range(group)],
+        *[parts[k] for k in order],
     )
 
     def hop(x, k):
@@ -318,15 +345,12 @@
     kept, *sent = pl.pallas_call(
         functools.partial(spread_kernel, group),
         out_shape=(shape(packed.shape, f32),) + (shape(packed.shape, bf16),) * (group - 1),
-        in_specs=[SMEM] + [VMEM] * 2,
+        in_specs=[VMEM] * 3,
         out_specs=[VMEM] * group,
-        scratch_shapes=[
-            pltpu.VMEM((group,) + packed.shape, f32),
-            pltpu.VMEM((segments // SEGB * SUB, LANES), f32),
-        ],
+        scratch_shapes=[pltpu.VMEM((blocks * SUB, LANES), f32)],
         compiler_params=params,
         name="spread",
-    )(place, term, weight)
+    )(put, term, weight)
     got = [swap(sent[k - 1], k) for k in peers]
     return pl.pallas_call(
         functools.partial(finish_kernel, group, slabs, {s: at for (_, s), at in held.items()}),

time: 25.9 us -> 24.9 us (0.961)
  waiting for transfers between devices: 6.54 us -> 5.01 us
  Pallas kernels: 6.04 us -> 6.54 us
    pallas_call x1, Pallas kernels: 1.27 us -> 2.82 us  [body(): pl.pallas_call(functools.partial(prepare_kernel, slabs, cap), out_shape=(...]
    ppermute x6, waiting for transfers between devices: 3.02 us -> 1.49 us  [swap(): return lax.ppermute(x, 'grp', [(i, i ^ k) for i in range(group)])]
    pallas_call x1, Pallas kernels: 1.13 us -> 0.53 us  [body(): pl.pallas_call(functools.partial(spread_kernel, group), out_shape=(shape(...]
    pallas_call x1, Pallas kernels: 1.7 us -> 1.18 us  [body(): pl.pallas_call(functools.partial(glide_kernel, order, slabs), out_shape=(...]
  transfers between devices with their start and end apart: 9 -> 9, of which waited for: 5 -> 4; matrix products, arithmetic and copies ran while one was open for 0% -> 0% of each run, Pallas kernels for 9% -> 14%
where the time goes in v4:
time: 24.9 us; the launch traced here: 24.7 us
  starting transfers between devices  12.4 us (50%)
  Pallas kernels  6.54 us (26%)
  waiting for transfers between devices  5.01 us (20%)
  between operations  0.73 us (3%)
    ppermute x6, starting transfers between devices, swap(): return lax.ppermute(x, 'grp', [(i, i ^ k) for i in range(group)])  8.16 us
    ppermute x3, starting transfers between devices, hop(): return lax.ppermute(x, 'slab', [(i, i ^ k) for i in range(slabs)])  4.23 us
    ppermute x3, waiting for transfers between devices, hop(): return lax.ppermute(x, 'slab', [(i, i ^ k) for i in range(slabs)])  3.53 us
    pallas_call x1, Pallas kernels, body(): pl.pallas_call(functools.partial(prepare_kernel, slabs, cap), out_shape=(...  2.82 us
    ppermute x6, waiting for transfers between devices, swap(): return lax.ppermute(x, 'grp', [(i, i ^ k) for i in range(group)])  1.49 us
    pallas_call x1, Pallas kernels, body(): pl.pallas_call(functools.partial(glide_kernel, order, slabs), out_shape=(...  1.18 us
    pallas_call x1, Pallas kernels, body(): pl.pallas_call(pack_kernel, out_shape=(shape((NR * voxels // LANES, LANES...  1.09 us
    pallas_call x1, Pallas kernels, body(): pl.pallas_call(functools.partial(finish_kernel, group, slabs, {s: at for...  0.91 us
  transfers between devices with their start and end apart: 9, of which 4 were waited for; matrix products, arithmetic and copies ran while one was open for 0% of the time, Pallas kernels for 14%

profile of v4, /device:TPU:0, one launch (start us, length us, event | category | flops | bytes accessed | tf_op | source)
XLA Modules:
  0.0 24.7 jit_solution(5088891777890682073)
XLA Ops:
  0.6 0.0 copy-start
  0.6 0.0 copy-start.1
  0.7 0.0 copy-start.2
  0.7 1.1 %pack.1 = (bf16[320,128]{1,0:T(8,128)(2,1)S(1)}, s32[1,64]{1,0:T(1,128)S(1)}) custom-call(bf16[6,8192]{1,0:T(8,128)(2,1)} %source_ref.1, s32[1,64]{1,0:T(1,128)} %bitcast.10, s32[1,64]{1,0:T(1,128)} %bitcast.11), custom_call_target="tpu_custom_call" | custom-call | tf_op jit(solution)/shard_map/pack/pallas_call | solution.py:254
  1.8 4.0 %collective-permute-start = (bf16[320,128]{1,0:T(8,128)(2,1)S(1)}, bf16[320,128]{1,0:T(8,128)(2,1)S(1)}, u32[]{:S(2)}, u32[]{:S(2)}) collective-permute-start(bf16[320,128]{1,0:T(8,128)(2,1)S(1)} %get-tuple-element.28.refs_8_), channel_id=1, source_target_pairs={{0,3},{1,2},{2,1},{3,0},{4,7},{5,6},{6,5},{7,4},{8,11},{9,10},{10,... | collective-permute-start | bytes 245768 | tf_op jit(solution)/shard_map/ppermute | solution.py:246
  5.7 0.5 %collective-permute-start.1 = (bf16[320,128]{1,0:T(8,128)(2,1)S(1)}, bf16[320,128]{1,0:T(8,128)(2,1)S(1)}, u32[]{:S(2)}, u32[]{:S(2)}) collective-permute-start(bf16[320,128]{1,0:T(8,128)(2,1)S(1)} %get-tuple-element.28.refs_8_), channel_id=1, source_target_pairs={{0,1},{1,0},{2,3},{3,2},{4,5},{5,4},{6,7},{7,6},{8,9},{9,8},{10,11... | collective-permute-start | bytes 245768 | tf_op jit(solution)/shard_map/ppermute | solution.py:246
  6.3 0.1 collective-permute-start.2
  6.4 0.0 copy-done
  6.4 0.0 copy-done.1
  6.4 0.0 copy-done.2
  6.4 0.0 copy-start.3
  6.4 2.8 %prepare.1 = (f32[8,4096]{1,0:T(8,128)S(1)}, bf16[64,4096]{1,0:T(8,128)(2,1)S(1)}, bf16[128,4096]{1,0:T(8,128)(2,1)S(1)}, bf16[64,256]{1,0:T(8,128)(2,1)S(1)}, b...) custom-call(s32[1,4096]{1,0:T(1,128)S(1)} %bitcast.6, ...), custom_call_target="tpu_custom_call" | custom-call | tf_op jit(solution)/shard_map/prepare/pallas_call | solution.py:273
  9.2 0.0 collective-permute-done.refs_9_
  9.2 1.2 %collective-permute-done.1.refs_10_ = bf16[320,128]{1,0:T(8,128)(2,1)S(1)} collective-permute-done((bf16[320,128]{1,0:T(8,128)(2,1)S(1)}, bf16[320,128]{1,0:T(8,128)(2,1)S(1)}, u32[]{:S(2)}, u32[]{:S(2)}) %collective-permute-start.1) | collective-permute-done | bytes 81952 | tf_op jit(solution)/shard_map/ppermute | solution.py:246
  10.4 0.3 %collective-permute-done.2.refs_11_ = bf16[320,128]{1,0:T(8,128)(2,1)S(1)} collective-permute-done((bf16[320,128]{1,0:T(8,128)(2,1)S(1)}, bf16[320,128]{1,0:T(8,128)(2,1)S(1)}, u32[]{:S(2)}, u32[]{:S(2)}) %collective-permute-start.2) | collective-permute-done | bytes 81952 | tf_op jit(solution)/shard_map/ppermute | solution.py:246
  10.7 0.0 copy-done.3
  10.7 1.2 %glide.1 = (f32[8,4096]{1,0:T(8,128)S(1)}, bf16[128,128]{1,0:T(8,128)(2,1)S(1)}, bf16[128,128]{1,0:T(8,128)(2,1)S(1)}) custom-call(bf16[64,256]{1,0:T(8,128)(2,1)S(1)} %get-tuple-element.21.refs_0_, f32[1,4096]{1,0:T(1,128)S(1)} %bitcast.8, f32[8,4096]{1,0:T(8,128)S(1)} %get-tuple-element.22.refs_2_, bf16[64,4096]{1,0:T(8,128)(2,1)S(1)} %get-tuple-element.23.refs_3_, ...), custom_call_target="tpu_custom_call" | custom-call | tf_op jit(solution)/shard_map/glide/pallas_call | solution.py:299
  11.9 2.7 %collective-permute-start.6 = (bf16[128,128]{1,0:T(8,128)(2,1)S(1)}, bf16[128,128]{1,0:T(8,128)(2,1)S(1)}, u32[]{:S(2)}, u32[]{:S(2)}) collective-permute-start(bf16[128,128]{1,0:T(8,128)(2,1)S(1)} %get-tuple-element.35), channel_id=1, source_target_pairs={{0,16},{4,20},{8,24},{12,28},{16,0},{20,4},{24,8},{28,12},{1,17},{... | collective-permute-start | bytes 98312 | tf_op jit(solution)/shard_map/ppermute | solution.py:324
  14.5 0.5 %spread.1 = (f32[320,128]{1,0:T(8,128)S(1)}, bf16[320,128]{1,0:T(8,128)(2,1)S(1)}, bf16[320,128]{1,0:T(8,128)(2,1)S(1)}, bf16[320,128]{1,0:T(8,128)(2,1)S(1)}) custom-call(bf16[256,128]{1,0:T(8,128)(2,1)S(1)} %get-tuple-element.20.refs_0_, f32[8,4096]{1,0:T(8,128)S(1)} %get-tuple-element.29.refs_1_, bf16[4096,128]{1,0:T(8,128)(2,1)S(1)} %get-tuple-element.27.refs_7_.refs_2_), custom_call_target="tpu_custom_call" | custom-call | tf_op jit(solution)/shard_map/spread/pallas_call | solution.py:345
  15.1 1.9 %collective-permute-start.3 = (bf16[320,128]{1,0:T(8,128)(2,1)S(1)}, bf16[320,128]{1,0:T(8,128)(2,1)S(1)}, u32[]{:S(2)}, u32[]{:S(2)}) collective-permute-start(bf16[320,128]{1,0:T(8,128)(2,1)S(1)} %get-tuple-element.31), channel_id=1, source_target_pairs={{0,3},{1,2},{2,1},{3,0},{4,7},{5,6},{6,5},{7,4},{8,11},{9,10},{10,... | collective-permute-start | bytes 245768 | tf_op jit(solution)/shard_map/ppermute | solution.py:246
  17.0 0.5 %collective-permute-start.4 = (bf16[320,128]{1,0:T(8,128)(2,1)S(1)}, bf16[320,128]{1,0:T(8,128)(2,1)S(1)}, u32[]{:S(2)}, u32[]{:S(2)}) collective-permute-start(bf16[320,128]{1,0:T(8,128)(2,1)S(1)} %get-tuple-element.32), channel_id=1, source_target_pairs={{0,1},{1,0},{2,3},{3,2},{4,5},{5,4},{6,7},{7,6},{8,9},{9,8},{10,11... | collective-permute-start | bytes 245768 | tf_op jit(solution)/shard_map/ppermute | solution.py:246
  17.5 1.1 %collective-permute-start.5 = (bf16[320,128]{1,0:T(8,128)(2,1)S(1)}, bf16[320,128]{1,0:T(8,128)(2,1)S(1)}, u32[]{:S(2)}, u32[]{:S(2)}) collective-permute-start(bf16[320,128]{1,0:T(8,128)(2,1)S(1)} %get-tuple-element.33), channel_id=1, source_target_pairs={{0,2},{1,3},{2,0},{3,1},{4,6},{5,7},{6,4},{7,5},{8,10},{9,11},{10,... | collective-permute-start | bytes 245768 | tf_op jit(solution)/shard_map/ppermute | solution.py:246
  18.6 0.0 collective-permute-done.6.refs_1_.refs_5_
  18.6 1.6 %collective-permute-start.7 = (bf16[128,128]{1,0:T(8,128)(2,1)S(1)}, bf16[128,128]{1,0:T(8,128)(2,1)S(1)}, u32[]{:S(2)}, u32[]{:S(2)}) collective-permute-start(bf16[128,128]{1,0:T(8,128)(2,1)S(1)} %gather.2), channel_id=1, source_target_pairs={{0,8},{4,12},{8,0},{12,4},{16,24},{20,28},{24,16},{28,20},{1,9},{5... | collective-permute-start | bytes 98312 | tf_op jit(solution)/shard_map/ppermute | solution.py:324
  20.2 2.3 %collective-permute-done.7.refs_2_.refs_6_ = bf16[128,128]{1,0:T(8,128)(2,1)S(1)} collective-permute-done((bf16[128,128]{1,0:T(8,128)(2,1)S(1)}, bf16[128,128]{1,0:T(8,128)(2,1)S(1)}, u32[]{:S(2)}, u32[]{:S(2)}) %collective-permute-start.7) | collective-permute-done | bytes 32800 | tf_op jit(solution)/shard_map/ppermute | solution.py:324
  22.6 0.0 collective-permute-start.8
  22.6 0.0 collective-permute-done.3.refs_1_
  22.6 0.0 collective-permute-done.4.refs_2_
  22.6 0.0 collective-permute-done.5.refs_3_
  22.6 1.2 %collective-permute-done.8.refs_7_ = bf16[128,128]{1,0:T(8,128)(2,1)S(1)} collective-permute-done((bf16[128,128]{1,0:T(8,128)(2,1)S(1)}, bf16[128,128]{1,0:T(8,128)(2,1)S(1)}, u32[]{:S(2)}, u32[]{:S(2)}) %collective-permute-start.8) | collective-permute-done | bytes 32800 | tf_op jit(solution)/shard_map/ppermute | solution.py:324
  23.8 0.9 %finish.1 = (f32[6,8192]{1,0:T(8,128)}, f32[4,8192]{1,0:T(4,128)}) custom-call(f32[320,128]{1,0:T(8,128)S(1)} %get-tuple-element.30.refs_0_, bf16[320,128]{1,0:T(8,128)(2,1)S(1)} %collective-permute-done.3.refs_1_, bf16[320,128]{1,0:T(8,128)(2,1)S(1)} %collective-permute-done.4.refs_2_, bf16[320,128]{1,0:T(8,128)(2,1)S(1)} %collective-permute-done.5.refs_3_, ...), custom_call_target="tpu_custom_call" | custom-call | tf_op jit(solution)/shard_map/finish/pallas_call | solution.py:355
  (2 shorter events, 0.0 us)
Async XLA Ops:
  0.6 5.7 %copy-start = (f32[3,4096]{1,0:T(4,128)S(1)}, f32[3,4096]{1,0:T(4,128)}, u32[]{:S(2)}) copy-start(f32[3,4096]{1,0:T(4,128)} %refs_3_.1) | copy-start | bytes 147460
  0.6 5.7 %copy-start.1 = (s32[4096]{0:T(1024)S(1)}, s32[4096]{0:T(1024)}, u32[]{:S(2)}) copy-start(s32[4096]{0:T(1024)} %param.12) | copy-start | bytes 49156
  0.7 5.7 %copy-start.2 = (s32[4096,1]{0,1:T(1,128)S(1)}, s32[4096,1]{0,1:T(1,128)}, u32[]{:S(2)}) copy-start(s32[4096,1]{0,1:T(1,128)} %param.15) | copy-start | bytes 49156
  1.8 7.5 %collective-permute-start = (bf16[320,128]{1,0:T(8,128)(2,1)S(1)}, bf16[320,128]{1,0:T(8,128)(2,1)S(1)}, u32[]{:S(2)}, u32[]{:S(2)}) collective-permute-start(bf16[320,128]{1,0:T(8,128)(2,1)S(1)} %get-tuple-element.28.refs_8_), channel_id=1, source_target_pairs={{0,3},{1,2},{2,1},{3,0},{4,7},{5,6},{6,5},{7,4},{8,11},{9,10},{10,... | collective-permute-start | bytes 245768 | tf_op jit(solution)/shard_map/ppermute | solution.py:246
  5.7 4.7 %collective-permute-start.1 = (bf16[320,128]{1,0:T(8,128)(2,1)S(1)}, bf16[320,128]{1,0:T(8,128)(2,1)S(1)}, u32[]{:S(2)}, u32[]{:S(2)}) collective-permute-start(bf16[320,128]{1,0:T(8,128)(2,1)S(1)} %get-tuple-element.28.refs_8_), channel_id=1, source_target_pairs={{0,1},{1,0},{2,3},{3,2},{4,5},{5,4},{6,7},{7,6},{8,9},{9,8},{10,11... | collective-permute-start | bytes 245768 | tf_op jit(solution)/shard_map/ppermute | solution.py:246
  6.3 4.4 %collective-permute-start.2 = (bf16[320,128]{1,0:T(8,128)(2,1)S(1)}, bf16[320,128]{1,0:T(8,128)(2,1)S(1)}, u32[]{:S(2)}, u32[]{:S(2)}) collective-permute-start(bf16[320,128]{1,0:T(8,128)(2,1)S(1)} %get-tuple-element.28.refs_8_), channel_id=1, source_target_pairs={{0,2},{1,3},{2,0},{3,1},{4,6},{5,7},{6,4},{7,5},{8,10},{9,11},{10,... | collective-permute-start | bytes 245768 | tf_op jit(solution)/shard_map/ppermute | solution.py:246
  6.4 4.3 %copy-start.3 = (f32[4096]{0:T(1024)S(1)}, f32[4096]{0:T(1024)}, u32[]{:S(2)}) copy-start(f32[4096]{0:T(1024)} %param.13) | copy-start | bytes 49156
  11.9 6.8 %collective-permute-start.6 = (bf16[128,128]{1,0:T(8,128)(2,1)S(1)}, bf16[128,128]{1,0:T(8,128)(2,1)S(1)}, u32[]{:S(2)}, u32[]{:S(2)}) collective-permute-start(bf16[128,128]{1,0:T(8,128)(2,1)S(1)} %get-tuple-element.35), channel_id=1, source_target_pairs={{0,16},{4,20},{8,24},{12,28},{16,0},{20,4},{24,8},{28,12},{1,17},{... | collective-permute-start | bytes 98312 | tf_op jit(solution)/shard_map/ppermute | solution.py:324
  15.1 7.5 %collective-permute-start.3 = (bf16[320,128]{1,0:T(8,128)(2,1)S(1)}, bf16[320,128]{1,0:T(8,128)(2,1)S(1)}, u32[]{:S(2)}, u32[]{:S(2)}) collective-permute-start(bf16[320,128]{1,0:T(8,128)(2,1)S(1)} %get-tuple-element.31), channel_id=1, source_target_pairs={{0,3},{1,2},{2,1},{3,0},{4,7},{5,6},{6,5},{7,4},{8,11},{9,10},{10,... | collective-permute-start | bytes 245768 | tf_op jit(solution)/shard_map/ppermute | solution.py:246
  17.0 5.6 %collective-permute-start.4 = (bf16[320,128]{1,0:T(8,128)(2,1)S(1)}, bf16[320,128]{1,0:T(8,128)(2,1)S(1)}, u32[]{:S(2)}, u32[]{:S(2)}) collective-permute-start(bf16[320,128]{1,0:T(8,128)(2,1)S(1)} %get-tuple-element.32), channel_id=1, source_target_pairs={{0,1},{1,0},{2,3},{3,2},{4,5},{5,4},{6,7},{7,6},{8,9},{9,8},{10,11... | collective-permute-start | bytes 245768 | tf_op jit(solution)/shard_map/ppermute | solution.py:246
  17.5 5.0 %collective-permute-start.5 = (bf16[320,128]{1,0:T(8,128)(2,1)S(1)}, bf16[320,128]{1,0:T(8,128)(2,1)S(1)}, u32[]{:S(2)}, u32[]{:S(2)}) collective-permute-start(bf16[320,128]{1,0:T(8,128)(2,1)S(1)} %get-tuple-element.33), channel_id=1, source_target_pairs={{0,2},{1,3},{2,0},{3,1},{4,6},{5,7},{6,4},{7,5},{8,10},{9,11},{10,... | collective-permute-start | bytes 245768 | tf_op jit(solution)/shard_map/ppermute | solution.py:246
  18.6 3.9 %collective-permute-start.7 = (bf16[128,128]{1,0:T(8,128)(2,1)S(1)}, bf16[128,128]{1,0:T(8,128)(2,1)S(1)}, u32[]{:S(2)}, u32[]{:S(2)}) collective-permute-start(bf16[128,128]{1,0:T(8,128)(2,1)S(1)} %gather.2), channel_id=1, source_target_pairs={{0,8},{4,12},{8,0},{12,4},{16,24},{20,28},{24,16},{28,20},{1,9},{5... | collective-permute-start | bytes 98312 | tf_op jit(solution)/shard_map/ppermute | solution.py:324
  22.6 1.2 %collective-permute-start.8 = (bf16[128,128]{1,0:T(8,128)(2,1)S(1)}, bf16[128,128]{1,0:T(8,128)(2,1)S(1)}, u32[]{:S(2)}, u32[]{:S(2)}) collective-permute-start(bf16[128,128]{1,0:T(8,128)(2,1)S(1)} %gather.3), channel_id=1, source_target_pairs={{0,4},{4,0},{8,12},{12,8},{16,20},{20,16},{24,28},{28,24},{1,5},{5... | collective-permute-start | bytes 98312 | tf_op jit(solution)/shard_map/ppermute | solution.py:324

commit v5 on v4

--- a/solution.py
+++ b/solution.py
@@ -15,7 +15,7 @@
 SEGB = 64
 LANES = 128
 SUB = 8
-PACK = 4
+PACK = 8
 
 glide_time = 0.5
 
@@ -60,35 +60,18 @@
     place_ref[...] = (block_ref[0] ^ lax.axis_index("grp")) * blocks + block_ref[1]
     for block in range(blocks):
         stress = stress_ref[:, block * LANES : (block + 1) * LANES].astype(jnp.float32)
-        rows_ref[pl.ds(block, 2, stride=blocks), :] = stress[:2] - stress[2:3]
-        rows_ref[pl.ds(block + 2 * blocks, 3, stride=blocks), :] = stress[3:]
-    packed_ref[...] = rows_ref[...].astype(jnp.bfloat16)
-
-
-def prepare_kernel(slabs, cap, *refs):
-    slip_ref, target_ref, place_ref, position_ref, source_ref = refs[:5]
-    factor_ref, high_ref, low_ref, pick_ref, put_ref, start_ref, course_ref, weight_ref = refs[5:13]
-    code_ref, sem = refs[13:]
+        row = block // SUB * NR * SUB + block % SUB
+        rows_ref[pl.ds(row, 2, stride=SUB), :] = stress[:2] - stress[2:3]
+        rows_ref[pl.ds(row + 2 * SUB, 3, stride=SUB), :] = stress[3:]
+    for c in range(NR):
+        pieces = [rows_ref[b * NR + c * SUB : b * NR + (c + 1) * SUB, :] for b in range(0, blocks, SUB)]
+        packed_ref[c * blocks : (c + 1) * blocks, :] = jnp.concatenate(pieces, axis=0).astype(jnp.bfloat16)
+
+
+def code_kernel(slabs, cap, target_ref, source_ref, high_ref, low_ref, weight_ref, sem):
     fetch = pltpu.make_async_copy(source_ref, weight_ref, sem)
     fetch.start()
-    segments = slip_ref.shape[1]
-    chunks = segments // LANES
-    hot = mask(iota((16, segments), 0) == slip_ref[...])
-    spot = iota((16, 16), 0) * 16 + iota((16, 16), 1)
-    table = jnp.zeros((16, 16), jnp.float32)
-    for (row, system), sign in np.ndenumerate(slip_signs()):
-        if sign:
-            table = jnp.where(spot == row * 16 + system, float(sign), table)
-    signs = jnp.dot(table.astype(jnp.bfloat16), hot, preferred_element_type=jnp.float32)
-    scale = jnp.where(iota((16, 1), 0) < 8, np.float32(1 / np.sqrt(6.0)), np.float32(1 / np.sqrt(2.0)))
-    factors = signs * scale
-    factor_ref[...] = factors[:SUB]
-    blocks, choices = pick_ref.shape
-    place = jnp.concatenate([place_ref[...], place_ref[...]], axis=1)
-    put = jnp.where(iota((choices, 2 * blocks), 0) == place, 1.0, 0.0)
-    put_ref[...] = put.astype(jnp.bfloat16)
-    pick_ref[...] = put.T[:blocks].astype(jnp.bfloat16)
-
+    chunks = target_ref.shape[0]
     target = target_ref[...] ^ lax.axis_index("slab")
     upto = mask(iota((LANES, LANES), 0) <= iota((LANES, LANES), 1))
     ones = jnp.ones((LANES, LANES), jnp.bfloat16)
@@ -108,14 +91,34 @@
         at = pl.ds(r * LANES, LANES)
         high_ref[:, at] = mask(iota((rows, LANES), 0) == high[r : r + 1, :])
         low_ref[:, at] = mask(iota((LANES, LANES), 0) == low[r : r + 1, :])
+    fetch.wait()
+
+
+def prepare_kernel(*refs):
+    slip_ref, place_ref, position_ref, high_ref, low_ref = refs[:5]
+    factor_ref, pick_ref, put_ref, start_ref, course_ref, code_ref = refs[5:]
+    segments = slip_ref.shape[1]
+    hot = mask(iota((16, segments), 0) == slip_ref[...])
+    spot = iota((16, 16), 0) * 16 + iota((16, 16), 1)
+    table = jnp.zeros((16, 16), jnp.float32)
+    for (row, system), sign in np.ndenumerate(slip_signs()):
+        if sign:
+            table = jnp.where(spot == row * 16 + system, float(sign), table)
+    signs = jnp.dot(table.astype(jnp.bfloat16), hot, preferred_element_type=jnp.float32)
+    factor_ref[...] = signs[:SUB] * np.float32(1 / np.sqrt(6.0))
+    blocks, choices = pick_ref.shape
+    place = jnp.concatenate([place_ref[...], place_ref[...]], axis=1)
+    put = jnp.where(iota((choices, 2 * blocks), 0) == place, 1.0, 0.0)
+    put_ref[...] = put.astype(jnp.bfloat16)
+    pick_ref[...] = put.T[:blocks].astype(jnp.bfloat16)
     codes = high_ref[...]
+    rows = codes.shape[0]
     for c in range(3):
         code_ref[c * rows : (c + 1) * rows, :] = codes * position_ref[c : c + 1, :].astype(jnp.bfloat16)
         code_ref[(3 + c) * rows : (4 + c) * rows, :] = codes * signs[8 + c : 9 + c, :].astype(jnp.bfloat16)
     slots = lax.dot_general(code_ref[...], low_ref[...], CONTRACT_LANES, preferred_element_type=jnp.float32)
     start_ref[...] = slots[: 3 * rows]
     course_ref[...] = slots[3 * rows :] * np.float32(1 / np.sqrt(2.0))
-    fetch.wait()
 
 
 def glide_kernel(order, slabs, *refs):
@@ -124,34 +127,27 @@
     stress_refs = [refs[8 + order.index(k)] for k in range(group)]
     term_ref = refs[8 + group]
     keep_ref, send_ref = refs[9 + group : 11 + group]
-    tiles_ref, step_ref, move_ref = refs[11 + group :]
+    step_ref, move_ref = refs[11 + group :]
     blocks = pick_ref.shape[0]
     held = stress_refs[0].shape[0] // NR
+    picked = []
     for c in range(NR):
         stress = jnp.concatenate([ref[c * held : (c + 1) * held, :] for ref in stress_refs], axis=0)
-        picked = jnp.dot(pick_ref[...], stress, preferred_element_type=jnp.float32)
-        for j in range(0, blocks, SUB):
-            tiles_ref[(j + c) * SUB : (j + c + 1) * SUB, :] = picked[j : j + SUB]
+        picked.append(jnp.dot(pick_ref[...], stress, preferred_element_type=jnp.float32))
 
     span = PACK * SEGB
-    part = iota((SUB, span), 1) // SEGB
-    real = iota((SUB, span), 0) < NR
+    mine = iota((PACK, span), 0) == iota((PACK, span), 1) // SEGB
     for g in range(blocks // PACK):
-        tiles = []
-        for j in range(PACK):
-            block = g * PACK + j
-            tiles.append(tiles_ref[pl.ds(block // SUB * SUB * SUB + block % SUB, SUB, stride=SUB), :])
-        stress = jnp.concatenate(tiles, axis=0).astype(jnp.bfloat16)
+        stress = jnp.concatenate([x[g * PACK : (g + 1) * PACK] for x in picked], axis=0).astype(jnp.bfloat16)
         at = pl.ds(g * span, span)
-        crossed = lax.dot_general(stress, weight_ref[at, :], CONTRACT_LANES, preferred_element_type=jnp.float32)
-        sampled = crossed[:SUB]
-        for j in range(1, PACK):
-            sampled = jnp.where(part == j, crossed[j * SUB : (j + 1) * SUB], sampled)
-        factors = factor_ref[:, at]
-        resolved = jnp.sum(jnp.where(real, factors * sampled, 0.0), axis=0, keepdims=True)
+        sampled = lax.dot_general(stress, weight_ref[at, :], CONTRACT_LANES, preferred_element_type=jnp.float32)
+        resolved = sampled[:PACK] * factor_ref[:1, at]
+        for c in range(1, NR):
+            resolved = resolved + sampled[c * PACK : (c + 1) * PACK] * factor_ref[c : c + 1, at]
+        resolved = jnp.sum(jnp.where(mine, resolved, 0.0), axis=0, keepdims=True)
         step = glide_time * mobility_ref[:, at] * resolved
         step_ref[:, at] = step
-        term_ref[:, at] = step * factors
+        term_ref[:, at] = step * factor_ref[:, at]
 
     step = step_ref[...]
     high = high_ref[...]
@@ -174,18 +170,18 @@
 def spread_kernel(group, *refs):
     put_ref, term_ref, weight_ref, kept_ref = refs[:4]
     sent_refs = refs[4 : 3 + group]
-    spread_ref = refs[3 + group]
     blocks = put_ref.shape[1] // 2
     held = kept_ref.shape[0] // NR
     span = PACK * SEGB
-    part = iota((SUB, span), 1) // SEGB
+    mine = iota((PACK, span), 0) == iota((PACK, span), 1) // SEGB
+    parts = []
     for g in range(blocks // PACK):
         at = pl.ds(g * span, span)
-        term = term_ref[:, at]
-        term = jnp.concatenate([jnp.where(part == j, term, 0.0) for j in range(PACK)], axis=0).astype(jnp.bfloat16)
-        spread_ref[g * PACK * SUB : (g + 1) * PACK * SUB, :] = jnp.dot(term, weight_ref[at, :], preferred_element_type=jnp.float32)
+        terms = [jnp.where(mine, term_ref[c : c + 1, at], 0.0) for c in range(NR)]
+        terms = jnp.concatenate(terms, axis=0).astype(jnp.bfloat16)
+        parts.append(jnp.dot(terms, weight_ref[at, :], preferred_element_type=jnp.float32))
     for c in range(NR):
-        spread = spread_ref[pl.ds(c, blocks, stride=SUB), :]
+        spread = jnp.concatenate([x[c * PACK : (c + 1) * PACK] for x in parts], axis=0)
         rounded = spread.astype(jnp.bfloat16)
         rest = (spread - rounded.astype(jnp.float32)).astype(jnp.bfloat16)
         dense = jnp.dot(put_ref[...], jnp.concatenate([rounded, rest], axis=0), preferred_element_type=jnp.float32)
@@ -200,11 +196,9 @@
         refs[-1][k * chunk : (k + 1) * chunk, :] = refs[which][place * chunk : (place + 1) * chunk, :]
 
 
-def finish_kernel(group, slabs, picks, *refs):
-    kept_ref = refs[0]
-    got_refs = refs[1:group]
-    moved_refs = refs[group:-4]
-    distortion_ref, arrived_ref, sum_ref, slot_ref = refs[-4:]
+def total_kernel(*refs):
+    kept_ref, got_refs = refs[0], refs[1:-2]
+    distortion_ref, sum_ref = refs[-2:]
     total = kept_ref[...]
     for ref in got_refs:
         total = total + ref[...].astype(jnp.float32)
@@ -212,12 +206,17 @@
     for c in range(NR):
         for b in range(0, held, SUB):
             sum_ref[b * NR + c * SUB : b * NR + (c + 1) * SUB, :] = total[c * held + b : c * held + b + SUB]
-    for block in range(distortion_ref.shape[1] // LANES):
+    for block in range(held):
         part = sum_ref[pl.ds(block // SUB * NR * SUB + block % SUB, NR, stride=SUB), :]
         at = slice(block * LANES, (block + 1) * LANES)
         distortion_ref[:2, at] = part[:2]
         distortion_ref[2:3, at] = -(part[:1] + part[1:2])
         distortion_ref[3:, at] = part[2:]
+
+
+def arrive_kernel(slabs, picks, *refs):
+    moved_refs = refs[:-2]
+    arrived_ref, slot_ref = refs[-2:]
     rows = slot_ref.shape[1]
     deep = rows // 4
     for source, (which, place) in picks.items():
@@ -270,30 +269,34 @@
     order = [0, *peers]
 
     slot_shape = (3 * slot_rows, LANES)
-    factor, high, low, pick, put, start, course, weight = pl.pallas_call(
-        functools.partial(prepare_kernel, slabs, cap),
+    high, low, weight = pl.pallas_call(
+        functools.partial(code_kernel, slabs, cap),
+        out_shape=(
+            shape((slot_rows, segments), bf16),
+            shape((LANES, segments), bf16),
+            shape((segments, BLK), bf16),
+        ),
+        in_specs=[VMEM, HBM],
+        out_specs=[VMEM] * 3,
+        scratch_shapes=[pltpu.SemaphoreType.DMA],
+        compiler_params=params,
+        name="code",
+    )(target_slab.reshape(segments // LANES, LANES), still(interp_weight.reshape(segments, BLK)))
+    factor, pick, put, start, course = pl.pallas_call(
+        prepare_kernel,
         out_shape=(
             shape((SUB, segments), f32),
-            shape((slot_rows, segments), bf16),
-            shape((LANES, segments), bf16),
             shape((blocks, group * voxels // BLK), bf16),
             shape((group * voxels // BLK, 2 * blocks), bf16),
             shape(slot_shape, f32),
             shape(slot_shape, f32),
-            shape((segments, BLK), bf16),
         ),
-        in_specs=[VMEM] * 4 + [HBM],
-        out_specs=[VMEM] * 8,
-        scratch_shapes=[pltpu.VMEM((6 * slot_rows, segments), bf16), pltpu.SemaphoreType.DMA],
+        in_specs=[VMEM] * 5,
+        out_specs=[VMEM] * 5,
+        scratch_shapes=[pltpu.VMEM((6 * slot_rows, segments), bf16)],
         compiler_params=params,
         name="prepare",
-    )(
-        slip_system.reshape(1, segments),
-        target_slab.reshape(segments // LANES, LANES),
-        place,
-        position,
-        still(interp_weight.reshape(segments, BLK)),
-    )
+    )(slip_system.reshape(1, segments), place, position, high, low)
 
     chunk = 4 * slot_rows // slabs
     term, keep, send = pl.pallas_call(
@@ -302,7 +305,6 @@
         in_specs=[VMEM] * (8 + group),
         out_specs=[VMEM] * 3,
         scratch_shapes=[
-            pltpu.VMEM((SUB * blocks, LANES), f32),
             pltpu.VMEM((1, segments), f32),
             pltpu.VMEM((4 * slot_rows, LANES), f32),
         ],
@@ -347,23 +349,29 @@
         out_shape=(shape(packed.shape, f32),) + (shape(packed.shape, bf16),) * (group - 1),
         in_specs=[VMEM] * 3,
         out_specs=[VMEM] * group,
-        scratch_shapes=[pltpu.VMEM((blocks * SUB, LANES), f32)],
         compiler_params=params,
         name="spread",
     )(put, term, weight)
     got = [swap(sent[k - 1], k) for k in peers]
-    return pl.pallas_call(
-        functools.partial(finish_kernel, group, slabs, {s: at for (_, s), at in held.items()}),
-        out_shape=(shape((NC, voxels), f32), shape((4, slabs * cap), f32)),
-        in_specs=[VMEM] * (group + len(arrays)),
-        out_specs=[VMEM] * 2,
-        scratch_shapes=[
-            pltpu.VMEM(packed.shape, f32),
-            pltpu.VMEM((slabs, chunk, LANES), f32),
-        ],
-        compiler_params=params,
-        name="finish",
-    )(kept, *got, *arrays)
+    distortion = pl.pallas_call(
+        total_kernel,
+        out_shape=shape((NC, voxels), f32),
+        in_specs=[VMEM] * group,
+        out_specs=VMEM,
+        scratch_shapes=[pltpu.VMEM(packed.shape, f32)],
+        compiler_params=params,
+        name="total",
+    )(kept, *got)
+    arrived = pl.pallas_call(
+        functools.partial(arrive_kernel, slabs, {s: at for (_, s), at in held.items()}),
+        out_shape=shape((4, slabs * cap), f32),
+        in_specs=[VMEM] * len(arrays),
+        out_specs=VMEM,
+        scratch_shapes=[pltpu.VMEM((slabs, chunk, LANES), f32)],
+        compiler_params=params,
+        name="arrive",
+    )(*arrays)
+    return (distortion, arrived)
 
 
 def solution(mesh):

time: 24.9 us -> 24.4 us (0.980)
  waiting for transfers between devices: 5.01 us -> 4.51 us
    ppermute x3, waiting for transfers between devices: 3.53 us -> 2.67 us  [hop(): return lax.ppermute(x, 'slab', [(i, i ^ k) for i in range(slabs)])]
    ppermute x6, waiting for transfers between devices: 1.49 us -> 1.84 us  [swap(): return lax.ppermute(x, 'grp', [(i, i ^ k) for i in range(group)])]
    pallas_call x2 -> x4, Pallas kernels: 3.73 us -> 3.98 us  [the longest x1 1.34 us: body(): pl.pallas_call(functools.partial(code_kernel, slabs, cap), out_shape=(sha...]
  transfers between devices with their start and end apart: 9 -> 9, of which waited for: 4 -> 4; matrix products, arithmetic and copies ran while one was open for 0% -> 0% of each run, Pallas kernels for 14% -> 16%
where the time goes in v5:
time: 24.4 us; the launch traced here: 24.3 us
  starting transfers between devices  12.4 us (51%)
  Pallas kernels  6.63 us (27%)
  waiting for transfers between devices  4.51 us (18%)
  between operations  0.74 us (3%)
    ppermute x6, starting transfers between devices, swap(): return lax.ppermute(x, 'grp', [(i, i ^ k) for i in range(group)])  8.16 us
    ppermute x3, starting transfers between devices, hop(): return lax.ppermute(x, 'slab', [(i, i ^ k) for i in range(slabs)])  4.25 us
    ppermute x3, waiting for transfers between devices, hop(): return lax.ppermute(x, 'slab', [(i, i ^ k) for i in range(slabs)])  2.67 us
    ppermute x6, waiting for transfers between devices, swap(): return lax.ppermute(x, 'grp', [(i, i ^ k) for i in range(group)])  1.84 us
    pallas_call x1, Pallas kernels, body(): pl.pallas_call(functools.partial(code_kernel, slabs, cap), out_shape=(sha...  1.34 us
    pallas_call x1, Pallas kernels, body(): pl.pallas_call(prepare_kernel, out_shape=(shape((SUB, segments), f32), sh...  1.11 us
    pallas_call x1, Pallas kernels, body(): pl.pallas_call(functools.partial(glide_kernel, order, slabs), out_shape=(...  1.1 us
    pallas_call x1, Pallas kernels, body(): pl.pallas_call(pack_kernel, out_shape=(shape((NR * voxels // LANES, LANES...  1.01 us
  transfers between devices with their start and end apart: 9, of which 4 were waited for; matrix products, arithmetic and copies ran while one was open for 0% of the time, Pallas kernels for 16%

profile of v5, /device:TPU:0, one launch (start us, length us, event | category | flops | bytes accessed | tf_op | source)
XLA Modules:
  0.0 24.3 jit_solution(10123242060275259769)
XLA Ops:
  0.6 0.0 copy-start.1
  0.6 1.0 %pack.1 = (bf16[320,128]{1,0:T(8,128)(2,1)S(1)}, s32[1,64]{1,0:T(1,128)S(1)}) custom-call(bf16[6,8192]{1,0:T(8,128)(2,1)} %source_ref.1, s32[1,64]{1,0:T(1,128)} %bitcast.10, s32[1,64]{1,0:T(1,128)} %bitcast.11), custom_call_target="tpu_custom_call" | custom-call | tf_op jit(solution)/shard_map/pack/pallas_call | solution.py:253
  1.7 4.0 %collective-permute-start = (bf16[320,128]{1,0:T(8,128)(2,1)S(1)}, bf16[320,128]{1,0:T(8,128)(2,1)S(1)}, u32[]{:S(2)}, u32[]{:S(2)}) collective-permute-start(bf16[320,128]{1,0:T(8,128)(2,1)S(1)} %get-tuple-element.28.refs_8_), channel_id=1, source_target_pairs={{0,3},{1,2},{2,1},{3,0},{4,7},{5,6},{6,5},{7,4},{8,11},{9,10},{10,... | collective-permute-start | bytes 245768 | tf_op jit(solution)/shard_map/ppermute | solution.py:245
  5.6 0.5 %collective-permute-start.1 = (bf16[320,128]{1,0:T(8,128)(2,1)S(1)}, bf16[320,128]{1,0:T(8,128)(2,1)S(1)}, u32[]{:S(2)}, u32[]{:S(2)}) collective-permute-start(bf16[320,128]{1,0:T(8,128)(2,1)S(1)} %get-tuple-element.28.refs_8_), channel_id=1, source_target_pairs={{0,1},{1,0},{2,3},{3,2},{4,5},{5,4},{6,7},{7,6},{8,9},{9,8},{10,11... | collective-permute-start | bytes 245768 | tf_op jit(solution)/shard_map/ppermute | solution.py:245
  6.2 0.1 collective-permute-start.2
  6.3 0.0 copy-done.1
  6.3 0.0 copy-start
  6.3 1.3 %code.1 = (bf16[64,4096]{1,0:T(8,128)(2,1)S(1)}, bf16[128,4096]{1,0:T(8,128)(2,1)S(1)}, bf16[4096,128]{1,0:T(8,128)(2,1)S(1)}) custom-call(s32[32,128]{1,0:T(8,128)S(1)} %bitcast.6, bf16[4096,128]{1,0:T(8,128)(2,1)} %bitcast.9), custom_call_target="tpu_custom_call" | custom-call | tf_op jit(solution)/shard_map/code/pallas_call | solution.py:272
  7.6 0.0 copy-done
  7.6 0.0 copy-done.2
  7.6 0.0 copy-start.3
  7.7 1.1 %prepare.1 = (f32[8,4096]{1,0:T(8,128)S(1)}, bf16[64,256]{1,0:T(8,128)(2,1)S(1)}, bf16[256,128]{1,0:T(8,128)(2,1)S(1)}, f32[192,128]{1,0:T(8,128)S(1)}, f32[192,128]{1,0:T(8,128)S(1)}) custom-call(s32[1,4096]{1,0:T(1,128)S(1)} %bitcast.7, s32[1,64]{1,0:T(1,128)S(1)} %get-tuple-element.19.refs_1_, f32[3,4096]{1,0:T(4,128)S(1)} %copy-done, ...), custom_call_target="tpu_custom_call" | custom-call | tf_op jit(solution)/shard_map/prepare/pallas_call | solution.py:285
  8.8 0.0 collective-permute-done.refs_9_
  8.8 1.6 %collective-permute-done.1.refs_10_ = bf16[320,128]{1,0:T(8,128)(2,1)S(1)} collective-permute-done((bf16[320,128]{1,0:T(8,128)(2,1)S(1)}, bf16[320,128]{1,0:T(8,128)(2,1)S(1)}, u32[]{:S(2)}, u32[]{:S(2)}) %collective-permute-start.1) | collective-permute-done | bytes 81952 | tf_op jit(solution)/shard_map/ppermute | solution.py:245
  10.3 0.3 %collective-permute-done.2.refs_11_ = bf16[320,128]{1,0:T(8,128)(2,1)S(1)} collective-permute-done((bf16[320,128]{1,0:T(8,128)(2,1)S(1)}, bf16[320,128]{1,0:T(8,128)(2,1)S(1)}, u32[]{:S(2)}, u32[]{:S(2)}) %collective-permute-start.2) | collective-permute-done | bytes 81952 | tf_op jit(solution)/shard_map/ppermute | solution.py:245
  10.6 0.0 copy-done.3
  10.6 1.1 %glide.1 = (f32[8,4096]{1,0:T(8,128)S(1)}, bf16[128,128]{1,0:T(8,128)(2,1)S(1)}, bf16[128,128]{1,0:T(8,128)(2,1)S(1)}) custom-call(bf16[64,256]{1,0:T(8,128)(2,1)S(1)} %get-tuple-element.23.refs_0_, f32[1,4096]{1,0:T(1,128)S(1)} %bitcast.8, f32[8,4096]{1,0:T(8,128)S(1)} %get-tuple-element.24.refs_2_, bf16[64,4096]{1,0:T(8,128)(2,1)S(1)} %get-tuple-element.20.refs_3_, ...), custom_call_target="tpu_custom_call" | custom-call | tf_op jit(solution)/shard_map/glide/pallas_call | solution.py:302
  11.7 2.7 %collective-permute-start.6 = (bf16[128,128]{1,0:T(8,128)(2,1)S(1)}, bf16[128,128]{1,0:T(8,128)(2,1)S(1)}, u32[]{:S(2)}, u32[]{:S(2)}) collective-permute-start(bf16[128,128]{1,0:T(8,128)(2,1)S(1)} %get-tuple-element.35), channel_id=1, source_target_pairs={{0,16},{4,20},{8,24},{12,28},{16,0},{20,4},{24,8},{28,12},{1,17},{... | collective-permute-start | bytes 98312 | tf_op jit(solution)/shard_map/ppermute | solution.py:326
  14.4 0.5 %spread.1 = (f32[320,128]{1,0:T(8,128)S(1)}, bf16[320,128]{1,0:T(8,128)(2,1)S(1)}, bf16[320,128]{1,0:T(8,128)(2,1)S(1)}, bf16[320,128]{1,0:T(8,128)(2,1)S(1)}) custom-call(bf16[256,128]{1,0:T(8,128)(2,1)S(1)} %get-tuple-element.22.refs_0_, f32[8,4096]{1,0:T(8,128)S(1)} %get-tuple-element.29.refs_1_, bf16[4096,128]{1,0:T(8,128)(2,1)S(1)} %get-tuple-element.27.refs_7_.refs_2_), custom_call_target="tpu_custom_call" | custom-call | tf_op jit(solution)/shard_map/spread/pallas_call | solution.py:347
  14.9 1.9 %collective-permute-start.3 = (bf16[320,128]{1,0:T(8,128)(2,1)S(1)}, bf16[320,128]{1,0:T(8,128)(2,1)S(1)}, u32[]{:S(2)}, u32[]{:S(2)}) collective-permute-start(bf16[320,128]{1,0:T(8,128)(2,1)S(1)} %get-tuple-element.31), channel_id=1, source_target_pairs={{0,3},{1,2},{2,1},{3,0},{4,7},{5,6},{6,5},{7,4},{8,11},{9,10},{10,... | collective-permute-start | bytes 245768 | tf_op jit(solution)/shard_map/ppermute | solution.py:245
  16.8 0.5 %collective-permute-start.4 = (bf16[320,128]{1,0:T(8,128)(2,1)S(1)}, bf16[320,128]{1,0:T(8,128)(2,1)S(1)}, u32[]{:S(2)}, u32[]{:S(2)}) collective-permute-start(bf16[320,128]{1,0:T(8,128)(2,1)S(1)} %get-tuple-element.32), channel_id=1, source_target_pairs={{0,1},{1,0},{2,3},{3,2},{4,5},{5,4},{6,7},{7,6},{8,9},{9,8},{10,11... | collective-permute-start | bytes 245768 | tf_op jit(solution)/shard_map/ppermute | solution.py:245
  17.4 1.1 %collective-permute-start.5 = (bf16[320,128]{1,0:T(8,128)(2,1)S(1)}, bf16[320,128]{1,0:T(8,128)(2,1)S(1)}, u32[]{:S(2)}, u32[]{:S(2)}) collective-permute-start(bf16[320,128]{1,0:T(8,128)(2,1)S(1)} %get-tuple-element.33), channel_id=1, source_target_pairs={{0,2},{1,3},{2,0},{3,1},{4,6},{5,7},{6,4},{7,5},{8,10},{9,11},{10,... | collective-permute-start | bytes 245768 | tf_op jit(solution)/shard_map/ppermute | solution.py:245
  18.5 0.0 collective-permute-done.6.refs_1_
  18.5 1.6 %collective-permute-start.7 = (bf16[128,128]{1,0:T(8,128)(2,1)S(1)}, bf16[128,128]{1,0:T(8,128)(2,1)S(1)}, u32[]{:S(2)}, u32[]{:S(2)}) collective-permute-start(bf16[128,128]{1,0:T(8,128)(2,1)S(1)} %gather.2), channel_id=1, source_target_pairs={{0,8},{4,12},{8,0},{12,4},{16,24},{20,28},{24,16},{28,20},{1,9},{5... | collective-permute-start | bytes 98312 | tf_op jit(solution)/shard_map/ppermute | solution.py:326
  20.1 2.3 %collective-permute-done.7.refs_2_ = bf16[128,128]{1,0:T(8,128)(2,1)S(1)} collective-permute-done((bf16[128,128]{1,0:T(8,128)(2,1)S(1)}, bf16[128,128]{1,0:T(8,128)(2,1)S(1)}, u32[]{:S(2)}, u32[]{:S(2)}) %collective-permute-start.7) | collective-permute-done | bytes 32800 | tf_op jit(solution)/shard_map/ppermute | solution.py:326
  22.4 0.0 collective-permute-start.8
  22.4 0.0 collective-permute-done.3.refs_1_
  22.4 0.0 collective-permute-done.4.refs_2_
  22.4 0.0 collective-permute-done.5.refs_3_
  22.4 0.8 %total.1 = f32[6,8192]{1,0:T(8,128)} custom-call(f32[320,128]{1,0:T(8,128)S(1)} %get-tuple-element.30.refs_0_, bf16[320,128]{1,0:T(8,128)(2,1)S(1)} %collective-permute-done.3.refs_1_, bf16[320,128]{1,0:T(8,128)(2,1)S(1)} %collective-permute-done.4.refs_2_, bf16[320,128]{1,0:T(8,128)(2,1)S(1)} %collective-permute-done.5.refs_3_), custom_call_target="tpu_custom_call" | custom-call | tf_op jit(solution)/shard_map/total/pallas_call | solution.py:356
  23.3 0.3 %collective-permute-done.8.refs_3_ = bf16[128,128]{1,0:T(8,128)(2,1)S(1)} collective-permute-done((bf16[128,128]{1,0:T(8,128)(2,1)S(1)}, bf16[128,128]{1,0:T(8,128)(2,1)S(1)}, u32[]{:S(2)}, u32[]{:S(2)}) %collective-permute-start.8) | collective-permute-done | bytes 32800 | tf_op jit(solution)/shard_map/ppermute | solution.py:326
  23.6 0.7 %arrive.1 = f32[4,8192]{1,0:T(4,128)} custom-call(bf16[128,128]{1,0:T(8,128)(2,1)S(1)} %get-tuple-element.34.refs_0_, bf16[128,128]{1,0:T(8,128)(2,1)S(1)} %collective-permute-done.6.refs_1_, bf16[128,128]{1,0:T(8,128)(2,1)S(1)} %collective-permute-done.7.refs_2_, bf16[128,128]{1,0:T(8,128)(2,1)S(1)} %collective-permute-done.8.refs_3_), custom_call_target="tpu_custom_call" | custom-call | tf_op jit(solution)/shard_map/arrive/pallas_call | solution.py:365
  (3 shorter events, 0.0 us)
Async XLA Ops:
  0.6 5.6 %copy-start.1 = (s32[4096,1]{0,1:T(1,128)S(1)}, s32[4096,1]{0,1:T(1,128)}, u32[]{:S(2)}) copy-start(s32[4096,1]{0,1:T(1,128)} %param.15) | copy-start | bytes 49156
  1.7 7.1 %collective-permute-start = (bf16[320,128]{1,0:T(8,128)(2,1)S(1)}, bf16[320,128]{1,0:T(8,128)(2,1)S(1)}, u32[]{:S(2)}, u32[]{:S(2)}) collective-permute-start(bf16[320,128]{1,0:T(8,128)(2,1)S(1)} %get-tuple-element.28.refs_8_), channel_id=1, source_target_pairs={{0,3},{1,2},{2,1},{3,0},{4,7},{5,6},{6,5},{7,4},{8,11},{9,10},{10,... | collective-permute-start | bytes 245768 | tf_op jit(solution)/shard_map/ppermute | solution.py:245
  5.6 4.7 %collective-permute-start.1 = (bf16[320,128]{1,0:T(8,128)(2,1)S(1)}, bf16[320,128]{1,0:T(8,128)(2,1)S(1)}, u32[]{:S(2)}, u32[]{:S(2)}) collective-permute-start(bf16[320,128]{1,0:T(8,128)(2,1)S(1)} %get-tuple-element.28.refs_8_), channel_id=1, source_target_pairs={{0,1},{1,0},{2,3},{3,2},{4,5},{5,4},{6,7},{7,6},{8,9},{9,8},{10,11... | collective-permute-start | bytes 245768 | tf_op jit(solution)/shard_map/ppermute | solution.py:245
  6.2 4.4 %collective-permute-start.2 = (bf16[320,128]{1,0:T(8,128)(2,1)S(1)}, bf16[320,128]{1,0:T(8,128)(2,1)S(1)}, u32[]{:S(2)}, u32[]{:S(2)}) collective-permute-start(bf16[320,128]{1,0:T(8,128)(2,1)S(1)} %get-tuple-element.28.refs_8_), channel_id=1, source_target_pairs={{0,2},{1,3},{2,0},{3,1},{4,6},{5,7},{6,4},{7,5},{8,10},{9,11},{10,... | collective-permute-start | bytes 245768 | tf_op jit(solution)/shard_map/ppermute | solution.py:245
  6.3 1.4 %copy-start = (f32[3,4096]{1,0:T(4,128)S(1)}, f32[3,4096]{1,0:T(4,128)}, u32[]{:S(2)}) copy-start(f32[3,4096]{1,0:T(4,128)} %refs_2_.1) | copy-start | bytes 147460
  6.3 1.4 %copy-start.2 = (s32[4096]{0:T(1024)S(1)}, s32[4096]{0:T(1024)}, u32[]{:S(2)}) copy-start(s32[4096]{0:T(1024)} %param.12) | copy-start | bytes 49156
  7.6 3.0 %copy-start.3 = (f32[4096]{0:T(1024)S(1)}, f32[4096]{0:T(1024)}, u32[]{:S(2)}) copy-start(f32[4096]{0:T(1024)} %param.13) | copy-start | bytes 49156
  11.7 6.8 %collective-permute-start.6 = (bf16[128,128]{1,0:T(8,128)(2,1)S(1)}, bf16[128,128]{1,0:T(8,128)(2,1)S(1)}, u32[]{:S(2)}, u32[]{:S(2)}) collective-permute-start(bf16[128,128]{1,0:T(8,128)(2,1)S(1)} %get-tuple-element.35), channel_id=1, source_target_pairs={{0,16},{4,20},{8,24},{12,28},{16,0},{20,4},{24,8},{28,12},{1,17},{... | collective-permute-start | bytes 98312 | tf_op jit(solution)/shard_map/ppermute | solution.py:326
  14.9 7.5 %collective-permute-start.3 = (bf16[320,128]{1,0:T(8,128)(2,1)S(1)}, bf16[320,128]{1,0:T(8,128)(2,1)S(1)}, u32[]{:S(2)}, u32[]{:S(2)}) collective-permute-start(bf16[320,128]{1,0:T(8,128)(2,1)S(1)} %get-tuple-element.31), channel_id=1, source_target_pairs={{0,3},{1,2},{2,1},{3,0},{4,7},{5,6},{6,5},{7,4},{8,11},{9,10},{10,... | collective-permute-start | bytes 245768 | tf_op jit(solution)/shard_map/ppermute | solution.py:245
  16.8 5.6 %collective-permute-start.4 = (bf16[320,128]{1,0:T(8,128)(2,1)S(1)}, bf16[320,128]{1,0:T(8,128)(2,1)S(1)}, u32[]{:S(2)}, u32[]{:S(2)}) collective-permute-start(bf16[320,128]{1,0:T(8,128)(2,1)S(1)} %get-tuple-element.32), channel_id=1, source_target_pairs={{0,1},{1,0},{2,3},{3,2},{4,5},{5,4},{6,7},{7,6},{8,9},{9,8},{10,11... | collective-permute-start | bytes 245768 | tf_op jit(solution)/shard_map/ppermute | solution.py:245
  17.4 5.0 %collective-permute-start.5 = (bf16[320,128]{1,0:T(8,128)(2,1)S(1)}, bf16[320,128]{1,0:T(8,128)(2,1)S(1)}, u32[]{:S(2)}, u32[]{:S(2)}) collective-permute-start(bf16[320,128]{1,0:T(8,128)(2,1)S(1)} %get-tuple-element.33), channel_id=1, source_target_pairs={{0,2},{1,3},{2,0},{3,1},{4,6},{5,7},{6,4},{7,5},{8,10},{9,11},{10,... | collective-permute-start | bytes 245768 | tf_op jit(solution)/shard_map/ppermute | solution.py:245
  18.5 3.9 %collective-permute-start.7 = (bf16[128,128]{1,0:T(8,128)(2,1)S(1)}, bf16[128,128]{1,0:T(8,128)(2,1)S(1)}, u32[]{:S(2)}, u32[]{:S(2)}) collective-permute-start(bf16[128,128]{1,0:T(8,128)(2,1)S(1)} %gather.2), channel_id=1, source_target_pairs={{0,8},{4,12},{8,0},{12,4},{16,24},{20,28},{24,16},{28,20},{1,9},{5... | collective-permute-start | bytes 98312 | tf_op jit(solution)/shard_map/ppermute | solution.py:326
  22.4 1.2 %collective-permute-start.8 = (bf16[128,128]{1,0:T(8,128)(2,1)S(1)}, bf16[128,128]{1,0:T(8,128)(2,1)S(1)}, u32[]{:S(2)}, u32[]{:S(2)}) collective-permute-start(bf16[128,128]{1,0:T(8,128)(2,1)S(1)} %gather.3), channel_id=1, source_target_pairs={{0,4},{4,0},{8,12},{12,8},{16,20},{20,16},{24,28},{28,24},{1,5},{5... | collective-permute-start | bytes 98312 | tf_op jit(solution)/shard_map/ppermute | solution.py:326

commit v6 on v5

--- a/solution.py
+++ b/solution.py
@@ -46,7 +46,12 @@
     return jnp.where(condition, 1.0, 0.0).astype(jnp.bfloat16)
 
 
-def pack_kernel(source_ref, owner_ref, local_ref, packed_ref, place_ref, stress_ref, rows_ref, block_ref, sems):
+def turned(index, group):
+    side = group.bit_length() // 2
+    return (index & ((1 << side) - 1)) << side | index >> side
+
+
+def pack_kernel(group, source_ref, owner_ref, local_ref, packed_ref, place_ref, stress_ref, rows_ref, block_ref, sems):
     copies = [
         pltpu.make_async_copy(source_ref, stress_ref, sems.at[0]),
         pltpu.make_async_copy(owner_ref, block_ref.at[0], sems.at[1]),
@@ -57,7 +62,9 @@
     for copy in copies:
         copy.wait()
     blocks = stress_ref.shape[1] // LANES
-    place_ref[...] = (block_ref[0] ^ lax.axis_index("grp")) * blocks + block_ref[1]
+    across = block_ref[0] ^ lax.axis_index("grp")
+    across = jnp.where(lax.axis_index("slab") % 2 == 1, turned(across, group), across)
+    place_ref[...] = across * blocks + block_ref[1]
     for block in range(blocks):
         stress = stress_ref[:, block * LANES : (block + 1) * LANES].astype(jnp.float32)
         row = block // SUB * NR * SUB + block % SUB
@@ -160,7 +167,7 @@
             at = slice(c * slot_rows, (c + 1) * slot_rows)
             value = start_ref[at, :] + course_ref[at, :] * step
         for t in range(slabs):
-            row = (t * 4 + c) * deep
+            row = ((t % 2 * slabs + t) // 2 * 4 + c) * deep
             move_ref[row : row + deep, :] = value[t * deep : (t + 1) * deep]
     half = keep_ref.shape[0]
     keep_ref[...] = move_ref[:half, :].astype(keep_ref.dtype)
@@ -194,6 +201,8 @@
 def gather_kernel(chunk, picks, *refs):
     for k, (which, place) in enumerate(picks):
         refs[-1][k * chunk : (k + 1) * chunk, :] = refs[which][place * chunk : (place + 1) * chunk, :]
+    rest = len(picks) * chunk
+    refs[-1][rest:, :] = jnp.zeros((refs[-1].shape[0] - rest, LANES), refs[-1].dtype)
 
 
 def total_kernel(*refs):
@@ -242,7 +251,9 @@
     params = pltpu.CompilerParams(vmem_limit_bytes=48 * 1024 * 1024)
 
     def swap(x, k):
-        return lax.ppermute(x, "grp", [(i, i ^ k) for i in range(group)])
+        steps = (k, turned(k, group))
+        pairs = [(s * group + g, s * group + (g ^ steps[s % 2])) for s in range(slabs) for g in range(group)]
+        return lax.ppermute(x, ("slab", "grp"), pairs)
 
     peers = sorted(range(1, group), key=lambda k: -bin(k).count("1"))
     blocks = block_local.shape[0]
@@ -251,7 +262,7 @@
         return pltpu.with_memory_space_constraint(x, pltpu.HBM)
 
     packed, place = pl.pallas_call(
-        pack_kernel,
+        functools.partial(pack_kernel, group),
         out_shape=(shape((NR * voxels // LANES, LANES), bf16), shape((1, blocks), jnp.int32)),
         in_specs=[HBM] * 3,
         out_specs=[VMEM] * 2,
@@ -325,25 +336,8 @@
     def hop(x, k):
         return lax.ppermute(x, "slab", [(i, i ^ k) for i in range(slabs)])
 
-    bit = slabs // 2
-    arrays = [keep, hop(send, bit)]
-    held = {(r, s * bit): (s, r) for r in range(bit) for s in range(2)}
-    while bit > 1:
-        bit //= 2
-        leaving = {key: at for key, at in sorted(held.items(), key=lambda item: item[0][::-1]) if key[0] & bit}
-        send = pl.pallas_call(
-            functools.partial(gather_kernel, chunk, tuple(leaving.values())),
-            out_shape=shape((len(leaving) * chunk, LANES), bf16),
-            in_specs=[VMEM] * len(arrays),
-            out_specs=VMEM,
-            compiler_params=params,
-            name="gather",
-        )(*arrays)
-        for k, key in enumerate(leaving):
-            del held[key]
-            held[key[0] ^ bit, key[1] | bit] = (len(arrays), k)
-        arrays.append(hop(send, bit))
-
+    arrays = [keep, hop(send, 1)]
+    held = {(r, s): (s, r // 2) for r in range(0, slabs, 2) for s in range(2)}
     kept, *sent = pl.pallas_call(
         functools.partial(spread_kernel, group),
         out_shape=(shape(packed.shape, f32),) + (shape(packed.shape, bf16),) * (group - 1),
@@ -352,7 +346,27 @@
         compiler_params=params,
         name="spread",
     )(put, term, weight)
+    bit = slabs
+    while bit > 2:
+        bit //= 2
+        leaving = {key: at for key, at in sorted(held.items(), key=lambda item: item[0][::-1]) if key[0] & bit}
+        through = tuple(sent) if bit == slabs // 2 else ()
+        *through, send = pl.pallas_call(
+            functools.partial(gather_kernel, chunk, tuple(leaving.values())),
+            out_shape=tuple(shape(x.shape, x.dtype) for x in through) + (shape((len(leaving) * chunk + 48, LANES), bf16),),
+            in_specs=[VMEM] * (len(arrays) + len(through)),
+            out_specs=[VMEM] * (len(through) + 1),
+            input_output_aliases={len(arrays) + k: k for k in range(len(through))},
+            compiler_params=params,
+            name="gather",
+        )(*arrays, *through)
+        sent = through or sent
+        for k, key in enumerate(leaving):
+            del held[key]
+            held[key[0] ^ bit, key[1] | bit] = (len(arrays), k)
+        arrays.append(hop(send, bit))
     got = [swap(sent[k - 1], k) for k in peers]
+
     distortion = pl.pallas_call(
         total_kernel,
         out_shape=shape((NC, voxels), f32),

time: 24.4 us -> 24.2 us (level)
  waiting for transfers between devices: 4.51 us -> 4.23 us
    ppermute x3, waiting for transfers between devices: 2.67 us -> 0.66 us  [hop(): return lax.ppermute(x, 'slab', [(i, i ^ k) for i in range(slabs)])]
    ppermute x6, waiting for transfers between devices: 1.84 us -> 3.57 us  [swap(): return lax.ppermute(x, ('slab', 'grp'), pairs)]
  transfers between devices with their start and end apart: 9 -> 9, of which waited for: 4 -> 6; matrix products, arithmetic and copies ran while one was open for 0% -> 0% of each run, Pallas kernels for 16% -> 16%
where the time goes in v6:
time: 24.2 us; the launch traced here: 24 us
  starting transfers between devices  12.4 us (51%)
  Pallas kernels  6.65 us (27%)
  waiting for transfers between devices  4.23 us (17%)
  between operations  0.73 us (3%)
    ppermute x6, starting transfers between devices, swap(): return lax.ppermute(x, ('slab', 'grp'), pairs)  8.09 us
    ppermute x3, starting transfers between devices, hop(): return lax.ppermute(x, 'slab', [(i, i ^ k) for i in range(slabs)])  4.3 us
    ppermute x6, waiting for transfers between devices, swap(): return lax.ppermute(x, ('slab', 'grp'), pairs)  3.57 us
    pallas_call x1, Pallas kernels, body(): pl.pallas_call(functools.partial(code_kernel, slabs, cap), out_shape=(sha...  1.34 us
    pallas_call x1, Pallas kernels, body(): pl.pallas_call(functools.partial(glide_kernel, order, slabs), out_shape=(...  1.11 us
    pallas_call x1, Pallas kernels, body(): pl.pallas_call(prepare_kernel, out_shape=(shape((SUB, segments), f32), sh...  1.1 us
    pallas_call x1, Pallas kernels, body(): pl.pallas_call(functools.partial(pack_kernel, group), out_shape=(shape((N...  1.01 us
    pallas_call x1, Pallas kernels, body(): pl.pallas_call(total_kernel, out_shape=shape((NC, voxels), f32), in_specs...  0.83 us
  transfers between devices with their start and end apart: 9, of which 6 were waited for; matrix products, arithmetic and copies ran while one was open for 0% of the time, Pallas kernels for 16%

profile of v6, /device:TPU:0, one launch (start us, length us, event | category | flops | bytes accessed | tf_op | source)
XLA Modules:
  0.0 24.0 jit_solution(16312160639621635080)
XLA Ops:
  0.6 0.0 copy-start.1
  0.6 1.0 %pack.1 = (bf16[320,128]{1,0:T(8,128)(2,1)S(1)}, s32[1,64]{1,0:T(1,128)S(1)}) custom-call(bf16[6,8192]{1,0:T(8,128)(2,1)} %source_ref.1, s32[1,64]{1,0:T(1,128)} %bitcast.10, s32[1,64]{1,0:T(1,128)} %bitcast.11), custom_call_target="tpu_custom_call" | custom-call | tf_op jit(solution)/shard_map/pack/pallas_call | solution.py:264
  1.7 4.0 %collective-permute-start = (bf16[320,128]{1,0:T(8,128)(2,1)S(1)}, bf16[320,128]{1,0:T(8,128)(2,1)S(1)}, u32[]{:S(2)}, u32[]{:S(2)}) collective-permute-start(bf16[320,128]{1,0:T(8,128)(2,1)S(1)} %get-tuple-element.32.refs_8_), channel_id=1, source_target_pairs={{0,3},{1,2},{2,1},{3,0},{4,7},{5,6},{6,5},{7,4},{8,11},{9,10},{10,... | collective-permute-start | bytes 245768 | tf_op jit(solution)/shard_map/ppermute | solution.py:256
  5.6 0.5 %collective-permute-start.1 = (bf16[320,128]{1,0:T(8,128)(2,1)S(1)}, bf16[320,128]{1,0:T(8,128)(2,1)S(1)}, u32[]{:S(2)}, u32[]{:S(2)}) collective-permute-start(bf16[320,128]{1,0:T(8,128)(2,1)S(1)} %get-tuple-element.32.refs_8_), channel_id=1, source_target_pairs={{0,1},{1,0},{2,3},{3,2},{4,6},{5,7},{6,4},{7,5},{8,9},{9,8},{10,11... | collective-permute-start | bytes 245768 | tf_op jit(solution)/shard_map/ppermute | solution.py:256
  6.2 0.1 collective-permute-start.2
  6.3 0.0 copy-done.1
  6.3 0.0 copy-start
  6.3 1.3 %code.1 = (bf16[64,4096]{1,0:T(8,128)(2,1)S(1)}, bf16[128,4096]{1,0:T(8,128)(2,1)S(1)}, bf16[4096,128]{1,0:T(8,128)(2,1)S(1)}) custom-call(s32[32,128]{1,0:T(8,128)S(1)} %bitcast.6, bf16[4096,128]{1,0:T(8,128)(2,1)} %bitcast.9), custom_call_target="tpu_custom_call" | custom-call | tf_op jit(solution)/shard_map/code/pallas_call | solution.py:283
  7.6 0.0 copy-done
  7.6 0.0 copy-done.2
  7.6 0.0 copy-start.3
  7.7 1.1 %prepare.1 = (f32[8,4096]{1,0:T(8,128)S(1)}, bf16[64,256]{1,0:T(8,128)(2,1)S(1)}, bf16[256,128]{1,0:T(8,128)(2,1)S(1)}, f32[192,128]{1,0:T(8,128)S(1)}, f32[192,128]{1,0:T(8,128)S(1)}) custom-call(s32[1,4096]{1,0:T(1,128)S(1)} %bitcast.7, s32[1,64]{1,0:T(1,128)S(1)} %get-tuple-element.23.refs_1_, f32[3,4096]{1,0:T(4,128)S(1)} %copy-done, ...), custom_call_target="tpu_custom_call" | custom-call | tf_op jit(solution)/shard_map/prepare/pallas_call | solution.py:296
  8.8 0.0 collective-permute-done.refs_9_
  8.8 1.6 %collective-permute-done.1.refs_10_ = bf16[320,128]{1,0:T(8,128)(2,1)S(1)} collective-permute-done((bf16[320,128]{1,0:T(8,128)(2,1)S(1)}, bf16[320,128]{1,0:T(8,128)(2,1)S(1)}, u32[]{:S(2)}, u32[]{:S(2)}) %collective-permute-start.1) | collective-permute-done | bytes 81952 | tf_op jit(solution)/shard_map/ppermute | solution.py:256
  10.3 0.3 %collective-permute-done.2.refs_11_ = bf16[320,128]{1,0:T(8,128)(2,1)S(1)} collective-permute-done((bf16[320,128]{1,0:T(8,128)(2,1)S(1)}, bf16[320,128]{1,0:T(8,128)(2,1)S(1)}, u32[]{:S(2)}, u32[]{:S(2)}) %collective-permute-start.2) | collective-permute-done | bytes 81952 | tf_op jit(solution)/shard_map/ppermute | solution.py:256
  10.6 0.0 copy-done.3
  10.6 1.1 %glide.1 = (f32[8,4096]{1,0:T(8,128)S(1)}, bf16[128,128]{1,0:T(8,128)(2,1)S(1)}, bf16[128,128]{1,0:T(8,128)(2,1)S(1)}) custom-call(bf16[64,256]{1,0:T(8,128)(2,1)S(1)} %get-tuple-element.27.refs_0_, f32[1,4096]{1,0:T(1,128)S(1)} %bitcast.8, f32[8,4096]{1,0:T(8,128)S(1)} %get-tuple-element.28.refs_2_, bf16[64,4096]{1,0:T(8,128)(2,1)S(1)} %get-tuple-element.24.refs_3_, ...), custom_call_target="tpu_custom_call" | custom-call | tf_op jit(solution)/shard_map/glide/pallas_call | solution.py:313
  11.7 0.1 collective-permute-start.3
  11.8 0.5 %spread.1 = (f32[320,128]{1,0:T(8,128)S(1)}, bf16[320,128]{1,0:T(8,128)(2,1)S(1)}, bf16[320,128]{1,0:T(8,128)(2,1)S(1)}, bf16[320,128]{1,0:T(8,128)(2,1)S(1)}) custom-call(bf16[256,128]{1,0:T(8,128)(2,1)S(1)} %get-tuple-element.26.refs_0_, f32[8,4096]{1,0:T(8,128)S(1)} %get-tuple-element.33.refs_1_, bf16[4096,128]{1,0:T(8,128)(2,1)S(1)} %get-tuple-element.31.refs_7_.refs_2_), custom_call_target="tpu_custom_call" | custom-call | tf_op jit(solution)/shard_map/spread/pallas_call | solution.py:341
  12.3 0.7 %collective-permute-done.3.refs_1_ = bf16[128,128]{1,0:T(8,128)(2,1)S(1)} collective-permute-done((bf16[128,128]{1,0:T(8,128)(2,1)S(1)}, bf16[128,128]{1,0:T(8,128)(2,1)S(1)}, u32[]{:S(2)}, u32[]{:S(2)}) %collective-permute-start.3) | collective-permute-done | bytes 32800 | tf_op jit(solution)/shard_map/ppermute | solution.py:337
  13.0 2.6 %collective-permute-start.7 = (bf16[176,128]{1,0:T(8,128)(2,1)S(1)}, bf16[176,128]{1,0:T(8,128)(2,1)S(1)}, u32[]{:S(2)}, u32[]{:S(2)}) collective-permute-start(bf16[176,128]{1,0:T(8,128)(2,1)S(1)} %get-tuple-element.43), channel_id=1, source_target_pairs={{0,16},{4,20},{8,24},{12,28},{16,0},{20,4},{24,8},{28,12},{1,17},{... | collective-permute-start | bytes 135176 | tf_op jit(solution)/shard_map/ppermute | solution.py:337
  15.6 1.8 %collective-permute-start.4 = (bf16[320,128]{1,0:T(8,128)(2,1)S(1)}, bf16[320,128]{1,0:T(8,128)(2,1)S(1)}, u32[]{:S(2)}, u32[]{:S(2)}) collective-permute-start(bf16[320,128]{1,0:T(8,128)(2,1)S(1)} %get-tuple-element.40), channel_id=1, source_target_pairs={{0,3},{1,2},{2,1},{3,0},{4,7},{5,6},{6,5},{7,4},{8,11},{9,10},{10,... | collective-permute-start | bytes 245768 | tf_op jit(solution)/shard_map/ppermute | solution.py:256
  17.4 0.6 %collective-permute-start.5 = (bf16[320,128]{1,0:T(8,128)(2,1)S(1)}, bf16[320,128]{1,0:T(8,128)(2,1)S(1)}, u32[]{:S(2)}, u32[]{:S(2)}) collective-permute-start(bf16[320,128]{1,0:T(8,128)(2,1)S(1)} %get-tuple-element.41), channel_id=1, source_target_pairs={{0,1},{1,0},{2,3},{3,2},{4,6},{5,7},{6,4},{7,5},{8,9},{9,8},{10,11... | collective-permute-start | bytes 245768 | tf_op jit(solution)/shard_map/ppermute | solution.py:256
  18.0 1.1 %collective-permute-start.6 = (bf16[320,128]{1,0:T(8,128)(2,1)S(1)}, bf16[320,128]{1,0:T(8,128)(2,1)S(1)}, u32[]{:S(2)}, u32[]{:S(2)}) collective-permute-start(bf16[320,128]{1,0:T(8,128)(2,1)S(1)} %get-tuple-element.42), channel_id=1, source_target_pairs={{0,2},{1,3},{2,0},{3,1},{4,5},{5,4},{6,7},{7,6},{8,10},{9,11},{10,... | collective-permute-start | bytes 245768 | tf_op jit(solution)/shard_map/ppermute | solution.py:256
  19.1 0.0 collective-permute-done.7.refs_2_
  19.1 1.6 %collective-permute-start.8 = (bf16[176,128]{1,0:T(8,128)(2,1)S(1)}, bf16[176,128]{1,0:T(8,128)(2,1)S(1)}, u32[]{:S(2)}, u32[]{:S(2)}) collective-permute-start(bf16[176,128]{1,0:T(8,128)(2,1)S(1)} %gather.3), channel_id=1, source_target_pairs={{0,8},{4,12},{8,0},{12,4},{16,24},{20,28},{24,16},{28,20},{1,9},{5... | collective-permute-start | bytes 135176 | tf_op jit(solution)/shard_map/ppermute | solution.py:337
  20.7 0.4 %collective-permute-done.4.refs_1_ = bf16[320,128]{1,0:T(8,128)(2,1)S(1)} collective-permute-done((bf16[320,128]{1,0:T(8,128)(2,1)S(1)}, bf16[320,128]{1,0:T(8,128)(2,1)S(1)}, u32[]{:S(2)}, u32[]{:S(2)}) %collective-permute-start.4) | collective-permute-done | bytes 81952 | tf_op jit(solution)/shard_map/ppermute | solution.py:256
  21.1 1.1 %collective-permute-done.5.refs_2_ = bf16[320,128]{1,0:T(8,128)(2,1)S(1)} collective-permute-done((bf16[320,128]{1,0:T(8,128)(2,1)S(1)}, bf16[320,128]{1,0:T(8,128)(2,1)S(1)}, u32[]{:S(2)}, u32[]{:S(2)}) %collective-permute-start.5) | collective-permute-done | bytes 81952 | tf_op jit(solution)/shard_map/ppermute | solution.py:256
  22.2 0.3 %collective-permute-done.6.refs_3_ = bf16[320,128]{1,0:T(8,128)(2,1)S(1)} collective-permute-done((bf16[320,128]{1,0:T(8,128)(2,1)S(1)}, bf16[320,128]{1,0:T(8,128)(2,1)S(1)}, u32[]{:S(2)}, u32[]{:S(2)}) %collective-permute-start.6) | collective-permute-done | bytes 81952 | tf_op jit(solution)/shard_map/ppermute | solution.py:256
  22.5 0.8 %total.1 = f32[6,8192]{1,0:T(8,128)} custom-call(f32[320,128]{1,0:T(8,128)S(1)} %get-tuple-element.34.refs_0_, bf16[320,128]{1,0:T(8,128)(2,1)S(1)} %collective-permute-done.4.refs_1_, bf16[320,128]{1,0:T(8,128)(2,1)S(1)} %collective-permute-done.5.refs_2_, bf16[320,128]{1,0:T(8,128)(2,1)S(1)} %collective-permute-done.6.refs_3_), custom_call_target="tpu_custom_call" | custom-call | tf_op jit(solution)/shard_map/total/pallas_call | solution.py:370
  23.3 0.0 collective-permute-done.8.refs_3_
  23.3 0.7 %arrive.1 = f32[4,8192]{1,0:T(4,128)} custom-call(bf16[128,128]{1,0:T(8,128)(2,1)S(1)} %get-tuple-element.35.refs_0_, bf16[128,128]{1,0:T(8,128)(2,1)S(1)} %collective-permute-done.3.refs_1_, bf16[176,128]{1,0:T(8,128)(2,1)S(1)} %collective-permute-done.7.refs_2_, bf16[176,128]{1,0:T(8,128)(2,1)S(1)} %collective-permute-done.8.refs_3_), custom_call_target="tpu_custom_call" | custom-call | tf_op jit(solution)/shard_map/arrive/pallas_call | solution.py:379
  (3 shorter events, 0.0 us)
Async XLA Ops:
  0.6 5.6 %copy-start.1 = (s32[4096,1]{0,1:T(1,128)S(1)}, s32[4096,1]{0,1:T(1,128)}, u32[]{:S(2)}) copy-start(s32[4096,1]{0,1:T(1,128)} %param.15) | copy-start | bytes 49156
  1.7 7.1 %collective-permute-start = (bf16[320,128]{1,0:T(8,128)(2,1)S(1)}, bf16[320,128]{1,0:T(8,128)(2,1)S(1)}, u32[]{:S(2)}, u32[]{:S(2)}) collective-permute-start(bf16[320,128]{1,0:T(8,128)(2,1)S(1)} %get-tuple-element.32.refs_8_), channel_id=1, source_target_pairs={{0,3},{1,2},{2,1},{3,0},{4,7},{5,6},{6,5},{7,4},{8,11},{9,10},{10,... | collective-permute-start | bytes 245768 | tf_op jit(solution)/shard_map/ppermute | solution.py:256
  5.6 4.7 %collective-permute-start.1 = (bf16[320,128]{1,0:T(8,128)(2,1)S(1)}, bf16[320,128]{1,0:T(8,128)(2,1)S(1)}, u32[]{:S(2)}, u32[]{:S(2)}) collective-permute-start(bf16[320,128]{1,0:T(8,128)(2,1)S(1)} %get-tuple-element.32.refs_8_), channel_id=1, source_target_pairs={{0,1},{1,0},{2,3},{3,2},{4,6},{5,7},{6,4},{7,5},{8,9},{9,8},{10,11... | collective-permute-start | bytes 245768 | tf_op jit(solution)/shard_map/ppermute | solution.py:256
  6.2 4.4 %collective-permute-start.2 = (bf16[320,128]{1,0:T(8,128)(2,1)S(1)}, bf16[320,128]{1,0:T(8,128)(2,1)S(1)}, u32[]{:S(2)}, u32[]{:S(2)}) collective-permute-start(bf16[320,128]{1,0:T(8,128)(2,1)S(1)} %get-tuple-element.32.refs_8_), channel_id=1, source_target_pairs={{0,2},{1,3},{2,0},{3,1},{4,5},{5,4},{6,7},{7,6},{8,10},{9,11},{10,... | collective-permute-start | bytes 245768 | tf_op jit(solution)/shard_map/ppermute | solution.py:256
  6.3 1.4 %copy-start = (f32[3,4096]{1,0:T(4,128)S(1)}, f32[3,4096]{1,0:T(4,128)}, u32[]{:S(2)}) copy-start(f32[3,4096]{1,0:T(4,128)} %refs_2_.1) | copy-start | bytes 147460
  6.3 1.4 %copy-start.2 = (s32[4096]{0:T(1024)S(1)}, s32[4096]{0:T(1024)}, u32[]{:S(2)}) copy-start(s32[4096]{0:T(1024)} %param.12) | copy-start | bytes 49156
  7.6 3.0 %copy-start.3 = (f32[4096]{0:T(1024)S(1)}, f32[4096]{0:T(1024)}, u32[]{:S(2)}) copy-start(f32[4096]{0:T(1024)} %param.13) | copy-start | bytes 49156
  11.7 1.3 %collective-permute-start.3 = (bf16[128,128]{1,0:T(8,128)(2,1)S(1)}, bf16[128,128]{1,0:T(8,128)(2,1)S(1)}, u32[]{:S(2)}, u32[]{:S(2)}) collective-permute-start(bf16[128,128]{1,0:T(8,128)(2,1)S(1)} %get-tuple-element.36), channel_id=1, source_target_pairs={{0,4},{4,0},{8,12},{12,8},{16,20},{20,16},{24,28},{28,24},{1,5},{5... | collective-permute-start | bytes 98312 | tf_op jit(solution)/shard_map/ppermute | solution.py:337
  13.0 6.1 %collective-permute-start.7 = (bf16[176,128]{1,0:T(8,128)(2,1)S(1)}, bf16[176,128]{1,0:T(8,128)(2,1)S(1)}, u32[]{:S(2)}, u32[]{:S(2)}) collective-permute-start(bf16[176,128]{1,0:T(8,128)(2,1)S(1)} %get-tuple-element.43), channel_id=1, source_target_pairs={{0,16},{4,20},{8,24},{12,28},{16,0},{20,4},{24,8},{28,12},{1,17},{... | collective-permute-start | bytes 135176 | tf_op jit(solution)/shard_map/ppermute | solution.py:337
  15.6 5.6 %collective-permute-start.4 = (bf16[320,128]{1,0:T(8,128)(2,1)S(1)}, bf16[320,128]{1,0:T(8,128)(2,1)S(1)}, u32[]{:S(2)}, u32[]{:S(2)}) collective-permute-start(bf16[320,128]{1,0:T(8,128)(2,1)S(1)} %get-tuple-element.40), channel_id=1, source_target_pairs={{0,3},{1,2},{2,1},{3,0},{4,7},{5,6},{6,5},{7,4},{8,11},{9,10},{10,... | collective-permute-start | bytes 245768 | tf_op jit(solution)/shard_map/ppermute | solution.py:256
  17.4 4.8 %collective-permute-start.5 = (bf16[320,128]{1,0:T(8,128)(2,1)S(1)}, bf16[320,128]{1,0:T(8,128)(2,1)S(1)}, u32[]{:S(2)}, u32[]{:S(2)}) collective-permute-start(bf16[320,128]{1,0:T(8,128)(2,1)S(1)} %get-tuple-element.41), channel_id=1, source_target_pairs={{0,1},{1,0},{2,3},{3,2},{4,6},{5,7},{6,4},{7,5},{8,9},{9,8},{10,11... | collective-permute-start | bytes 245768 | tf_op jit(solution)/shard_map/ppermute | solution.py:256
  18.0 4.5 %collective-permute-start.6 = (bf16[320,128]{1,0:T(8,128)(2,1)S(1)}, bf16[320,128]{1,0:T(8,128)(2,1)S(1)}, u32[]{:S(2)}, u32[]{:S(2)}) collective-permute-start(bf16[320,128]{1,0:T(8,128)(2,1)S(1)} %get-tuple-element.42), channel_id=1, source_target_pairs={{0,2},{1,3},{2,0},{3,1},{4,5},{5,4},{6,7},{7,6},{8,10},{9,11},{10,... | collective-permute-start | bytes 245768 | tf_op jit(solution)/shard_map/ppermute | solution.py:256
  19.1 4.2 %collective-permute-start.8 = (bf16[176,128]{1,0:T(8,128)(2,1)S(1)}, bf16[176,128]{1,0:T(8,128)(2,1)S(1)}, u32[]{:S(2)}, u32[]{:S(2)}) collective-permute-start(bf16[176,128]{1,0:T(8,128)(2,1)S(1)} %gather.3), channel_id=1, source_target_pairs={{0,8},{4,12},{8,0},{12,4},{16,24},{20,28},{24,16},{28,20},{1,9},{5... | collective-permute-start | bytes 135176 | tf_op jit(solution)/shard_map/ppermute | solution.py:337

commit v7 on v6

--- a/solution.py
+++ b/solution.py
@@ -66,13 +66,16 @@
     across = jnp.where(lax.axis_index("slab") % 2 == 1, turned(across, group), across)
     place_ref[...] = across * blocks + block_ref[1]
     for block in range(blocks):
-        stress = stress_ref[:, block * LANES : (block + 1) * LANES].astype(jnp.float32)
-        row = block // SUB * NR * SUB + block % SUB
-        rows_ref[pl.ds(row, 2, stride=SUB), :] = stress[:2] - stress[2:3]
-        rows_ref[pl.ds(row + 2 * SUB, 3, stride=SUB), :] = stress[3:]
-    for c in range(NR):
-        pieces = [rows_ref[b * NR + c * SUB : b * NR + (c + 1) * SUB, :] for b in range(0, blocks, SUB)]
-        packed_ref[c * blocks : (c + 1) * blocks, :] = jnp.concatenate(pieces, axis=0).astype(jnp.bfloat16)
+        at = pl.ds(block // SUB * NC * SUB + block % SUB, NC, stride=SUB)
+        rows_ref[at, :] = stress_ref[:, block * LANES : (block + 1) * LANES].astype(jnp.float32)
+
+    def component(c):
+        pieces = [rows_ref[b * NC + c * SUB : b * NC + (c + 1) * SUB, :] for b in range(0, blocks, SUB)]
+        return jnp.concatenate(pieces, axis=0)
+
+    xx, yy, zz, yz, xz, xy = [component(c) for c in range(NC)]
+    for c, value in enumerate((xx - zz, yy - zz, yz, xz, xy)):
+        packed_ref[c * blocks : (c + 1) * blocks, :] = value.astype(jnp.bfloat16)
 
 
 def code_kernel(slabs, cap, target_ref, source_ref, high_ref, low_ref, weight_ref, sem):
@@ -92,12 +95,12 @@
         rank = (inside + ahead).astype(jnp.int32) - 1
         slot = slot + jnp.where(target == t, rank, 0)
     high = slot // LANES
-    low = slot % LANES
+    low = (slot % LANES).T
     rows = slabs * cap // LANES
     for r in range(chunks):
         at = pl.ds(r * LANES, LANES)
         high_ref[:, at] = mask(iota((rows, LANES), 0) == high[r : r + 1, :])
-        low_ref[:, at] = mask(iota((LANES, LANES), 0) == low[r : r + 1, :])
+        low_ref[at, :] = mask(iota((LANES, LANES), 1) == low[:, r : r + 1])
     fetch.wait()
 
 
@@ -123,7 +126,7 @@
     for c in range(3):
         code_ref[c * rows : (c + 1) * rows, :] = codes * position_ref[c : c + 1, :].astype(jnp.bfloat16)
         code_ref[(3 + c) * rows : (4 + c) * rows, :] = codes * signs[8 + c : 9 + c, :].astype(jnp.bfloat16)
-    slots = lax.dot_general(code_ref[...], low_ref[...], CONTRACT_LANES, preferred_element_type=jnp.float32)
+    slots = jnp.dot(code_ref[...], low_ref[...], preferred_element_type=jnp.float32)
     start_ref[...] = slots[: 3 * rows]
     course_ref[...] = slots[3 * rows :] * np.float32(1 / np.sqrt(2.0))
 
@@ -160,7 +163,7 @@
     high = high_ref[...]
     slot_rows = high.shape[0]
     deep = slot_rows // slabs
-    step = lax.dot_general(high * step.astype(jnp.bfloat16), low_ref[...], CONTRACT_LANES, preferred_element_type=jnp.float32)
+    step = jnp.dot(high * step.astype(jnp.bfloat16), low_ref[...], preferred_element_type=jnp.float32)
     for c in range(4):
         value = step
         if c < 3:
@@ -212,15 +215,13 @@
     for ref in got_refs:
         total = total + ref[...].astype(jnp.float32)
     held = total.shape[0] // NR
-    for c in range(NR):
+    xx, yy, yz, xz, xy = [total[c * held : (c + 1) * held] for c in range(NR)]
+    for c, value in enumerate((xx, yy, -(xx + yy), yz, xz, xy)):
         for b in range(0, held, SUB):
-            sum_ref[b * NR + c * SUB : b * NR + (c + 1) * SUB, :] = total[c * held + b : c * held + b + SUB]
+            sum_ref[b * NC + c * SUB : b * NC + (c + 1) * SUB, :] = value[b : b + SUB]
     for block in range(held):
-        part = sum_ref[pl.ds(block // SUB * NR * SUB + block % SUB, NR, stride=SUB), :]
         at = slice(block * LANES, (block + 1) * LANES)
-        distortion_ref[:2, at] = part[:2]
-        distortion_ref[2:3, at] = -(part[:1] + part[1:2])
-        distortion_ref[3:, at] = part[2:]
+        distortion_ref[:, at] = sum_ref[pl.ds(block // SUB * NC * SUB + block % SUB, NC, stride=SUB), :]
 
 
 def arrive_kernel(slabs, picks, *refs):
@@ -268,7 +269,7 @@
         out_specs=[VMEM] * 2,
         scratch_shapes=[
             pltpu.VMEM(stress.shape, bf16),
-            pltpu.VMEM((NR * voxels // LANES, LANES), f32),
+            pltpu.VMEM((NC * voxels // LANES, LANES), f32),
             pltpu.VMEM((2, 1, blocks), jnp.int32),
             pltpu.SemaphoreType.DMA((3,)),
         ],
@@ -284,7 +285,7 @@
         functools.partial(code_kernel, slabs, cap),
         out_shape=(
             shape((slot_rows, segments), bf16),
-            shape((LANES, segments), bf16),
+            shape((segments, LANES), bf16),
             shape((segments, BLK), bf16),
         ),
         in_specs=[VMEM, HBM],
@@ -372,7 +373,7 @@
         out_shape=shape((NC, voxels), f32),
         in_specs=[VMEM] * group,
         out_specs=VMEM,
-        scratch_shapes=[pltpu.VMEM(packed.shape, f32)],
+        scratch_shapes=[pltpu.VMEM((NC * voxels // LANES, LANES), f32)],
         compiler_params=params,
         name="total",
     )(kept, *got)

time: 24.2 us -> 23.8 us (0.983)
  waiting for transfers between devices: 4.23 us -> 3.7 us
    ppermute x6, waiting for transfers between devices: 3.57 us -> 3.05 us  [swap(): return lax.ppermute(x, ('slab', 'grp'), pairs)]
    pallas_call x1, Pallas kernels: 1.34 us -> 1.86 us  [body(): pl.pallas_call(functools.partial(code_kernel, slabs, cap), out_shape=(sha...]
    pallas_call x1, Pallas kernels: 1.11 us -> 0.85 us  [body(): pl.pallas_call(functools.partial(glide_kernel, order, slabs), out_shape=(...]
  transfers between devices with their start and end apart: 9 -> 9, of which waited for: 6 -> 6; matrix products, arithmetic and copies ran while one was open for 0% -> 0% of each run, Pallas kernels for 16% -> 18%
where the time goes in v7:
time: 23.8 us; the launch traced here: 23.7 us
  starting transfers between devices  12.4 us (52%)
  Pallas kernels  6.87 us (29%)
  waiting for transfers between devices  3.7 us (16%)
  between operations  0.73 us (3%)
    ppermute x6, starting transfers between devices, swap(): return lax.ppermute(x, ('slab', 'grp'), pairs)  8.09 us
    ppermute x3, starting transfers between devices, hop(): return lax.ppermute(x, 'slab', [(i, i ^ k) for i in range(slabs)])  4.3 us
    ppermute x6, waiting for transfers between devices, swap(): return lax.ppermute(x, ('slab', 'grp'), pairs)  3.05 us
    pallas_call x1, Pallas kernels, body(): pl.pallas_call(functools.partial(code_kernel, slabs, cap), out_shape=(sha...  1.86 us
    pallas_call x1, Pallas kernels, body(): pl.pallas_call(prepare_kernel, out_shape=(shape((SUB, segments), f32), sh...  1.11 us
    pallas_call x1, Pallas kernels, body(): pl.pallas_call(functools.partial(pack_kernel, group), out_shape=(shape((N...  1 us
    pallas_call x1, Pallas kernels, body(): pl.pallas_call(functools.partial(glide_kernel, order, slabs), out_shape=(...  0.85 us
    pallas_call x1, Pallas kernels, body(): pl.pallas_call(total_kernel, out_shape=shape((NC, voxels), f32), in_specs...  0.8 us
  transfers between devices with their start and end apart: 9, of which 6 were waited for; matrix products, arithmetic and copies ran while one was open for 0% of the time, Pallas kernels for 18%

profile of v7, /device:TPU:0, one launch (start us, length us, event | category | flops | bytes accessed | tf_op | source)
XLA Modules:
  0.0 23.7 jit_solution(4233543677381296122)
XLA Ops:
  0.6 0.0 copy-start.1
  0.6 1.0 %pack.1 = (bf16[320,128]{1,0:T(8,128)(2,1)S(1)}, s32[1,64]{1,0:T(1,128)S(1)}) custom-call(bf16[6,8192]{1,0:T(8,128)(2,1)} %source_ref.1, s32[1,64]{1,0:T(1,128)} %bitcast.10, s32[1,64]{1,0:T(1,128)} %bitcast.11), custom_call_target="tpu_custom_call" | custom-call | tf_op jit(solution)/shard_map/pack/pallas_call | solution.py:265
  1.6 4.0 %collective-permute-start = (bf16[320,128]{1,0:T(8,128)(2,1)S(1)}, bf16[320,128]{1,0:T(8,128)(2,1)S(1)}, u32[]{:S(2)}, u32[]{:S(2)}) collective-permute-start(bf16[320,128]{1,0:T(8,128)(2,1)S(1)} %get-tuple-element.32.refs_8_), channel_id=1, source_target_pairs={{0,3},{1,2},{2,1},{3,0},{4,7},{5,6},{6,5},{7,4},{8,11},{9,10},{10,... | collective-permute-start | bytes 245768 | tf_op jit(solution)/shard_map/ppermute | solution.py:257
  5.6 0.5 %collective-permute-start.1 = (bf16[320,128]{1,0:T(8,128)(2,1)S(1)}, bf16[320,128]{1,0:T(8,128)(2,1)S(1)}, u32[]{:S(2)}, u32[]{:S(2)}) collective-permute-start(bf16[320,128]{1,0:T(8,128)(2,1)S(1)} %get-tuple-element.32.refs_8_), channel_id=1, source_target_pairs={{0,1},{1,0},{2,3},{3,2},{4,6},{5,7},{6,4},{7,5},{8,9},{9,8},{10,11... | collective-permute-start | bytes 245768 | tf_op jit(solution)/shard_map/ppermute | solution.py:257
  6.1 0.1 collective-permute-start.2
  6.2 0.0 copy-done.1
  6.3 0.0 copy-start
  6.3 1.9 %code.1 = (bf16[64,4096]{1,0:T(8,128)(2,1)S(1)}, bf16[4096,128]{1,0:T(8,128)(2,1)S(1)}, bf16[4096,128]{1,0:T(8,128)(2,1)S(1)}) custom-call(s32[32,128]{1,0:T(8,128)S(1)} %bitcast.6, bf16[4096,128]{1,0:T(8,128)(2,1)} %bitcast.9), custom_call_target="tpu_custom_call" | custom-call | tf_op jit(solution)/shard_map/code/pallas_call | solution.py:284
  8.1 0.0 copy-done
  8.1 0.0 copy-done.2
  8.1 0.0 copy-start.3
  8.2 1.1 %prepare.1 = (f32[8,4096]{1,0:T(8,128)S(1)}, bf16[64,256]{1,0:T(8,128)(2,1)S(1)}, bf16[256,128]{1,0:T(8,128)(2,1)S(1)}, f32[192,128]{1,0:T(8,128)S(1)}, f32[192,128]{1,0:T(8,128)S(1)}) custom-call(s32[1,4096]{1,0:T(1,128)S(1)} %bitcast.7, s32[1,64]{1,0:T(1,128)S(1)} %get-tuple-element.23.refs_1_, f32[3,4096]{1,0:T(4,128)S(1)} %copy-done, ...), custom_call_target="tpu_custom_call" | custom-call | tf_op jit(solution)/shard_map/prepare/pallas_call | solution.py:297
  9.3 0.0 collective-permute-done.refs_9_
  9.3 1.0 %collective-permute-done.1.refs_10_ = bf16[320,128]{1,0:T(8,128)(2,1)S(1)} collective-permute-done((bf16[320,128]{1,0:T(8,128)(2,1)S(1)}, bf16[320,128]{1,0:T(8,128)(2,1)S(1)}, u32[]{:S(2)}, u32[]{:S(2)}) %collective-permute-start.1) | collective-permute-done | bytes 81952 | tf_op jit(solution)/shard_map/ppermute | solution.py:257
  10.3 0.3 %collective-permute-done.2.refs_11_ = bf16[320,128]{1,0:T(8,128)(2,1)S(1)} collective-permute-done((bf16[320,128]{1,0:T(8,128)(2,1)S(1)}, bf16[320,128]{1,0:T(8,128)(2,1)S(1)}, u32[]{:S(2)}, u32[]{:S(2)}) %collective-permute-start.2) | collective-permute-done | bytes 81952 | tf_op jit(solution)/shard_map/ppermute | solution.py:257
  10.6 0.0 copy-done.3
  10.6 0.9 %glide.1 = (f32[8,4096]{1,0:T(8,128)S(1)}, bf16[128,128]{1,0:T(8,128)(2,1)S(1)}, bf16[128,128]{1,0:T(8,128)(2,1)S(1)}) custom-call(bf16[64,256]{1,0:T(8,128)(2,1)S(1)} %get-tuple-element.27.refs_0_, f32[1,4096]{1,0:T(1,128)S(1)} %bitcast.8, f32[8,4096]{1,0:T(8,128)S(1)} %get-tuple-element.28.refs_2_, bf16[64,4096]{1,0:T(8,128)(2,1)S(1)} %get-tuple-element.24.refs_3_, ...), custom_call_target="tpu_custom_call" | custom-call | tf_op jit(solution)/shard_map/glide/pallas_call | solution.py:314
  11.4 0.1 collective-permute-start.3
  11.5 0.5 %spread.1 = (f32[320,128]{1,0:T(8,128)S(1)}, bf16[320,128]{1,0:T(8,128)(2,1)S(1)}, bf16[320,128]{1,0:T(8,128)(2,1)S(1)}, bf16[320,128]{1,0:T(8,128)(2,1)S(1)}) custom-call(bf16[256,128]{1,0:T(8,128)(2,1)S(1)} %get-tuple-element.26.refs_0_, f32[8,4096]{1,0:T(8,128)S(1)} %get-tuple-element.33.refs_1_, bf16[4096,128]{1,0:T(8,128)(2,1)S(1)} %get-tuple-element.31.refs_7_.refs_2_), custom_call_target="tpu_custom_call" | custom-call | tf_op jit(solution)/shard_map/spread/pallas_call | solution.py:342
  12.1 0.6 %collective-permute-done.3.refs_1_ = bf16[128,128]{1,0:T(8,128)(2,1)S(1)} collective-permute-done((bf16[128,128]{1,0:T(8,128)(2,1)S(1)}, bf16[128,128]{1,0:T(8,128)(2,1)S(1)}, u32[]{:S(2)}, u32[]{:S(2)}) %collective-permute-start.3) | collective-permute-done | bytes 32800 | tf_op jit(solution)/shard_map/ppermute | solution.py:338
  12.7 2.6 %collective-permute-start.7 = (bf16[176,128]{1,0:T(8,128)(2,1)S(1)}, bf16[176,128]{1,0:T(8,128)(2,1)S(1)}, u32[]{:S(2)}, u32[]{:S(2)}) collective-permute-start(bf16[176,128]{1,0:T(8,128)(2,1)S(1)} %get-tuple-element.43), channel_id=1, source_target_pairs={{0,16},{4,20},{8,24},{12,28},{16,0},{20,4},{24,8},{28,12},{1,17},{... | collective-permute-start | bytes 135176 | tf_op jit(solution)/shard_map/ppermute | solution.py:338
  15.3 1.8 %collective-permute-start.4 = (bf16[320,128]{1,0:T(8,128)(2,1)S(1)}, bf16[320,128]{1,0:T(8,128)(2,1)S(1)}, u32[]{:S(2)}, u32[]{:S(2)}) collective-permute-start(bf16[320,128]{1,0:T(8,128)(2,1)S(1)} %get-tuple-element.40), channel_id=1, source_target_pairs={{0,3},{1,2},{2,1},{3,0},{4,7},{5,6},{6,5},{7,4},{8,11},{9,10},{10,... | collective-permute-start | bytes 245768 | tf_op jit(solution)/shard_map/ppermute | solution.py:257
  17.1 0.6 %collective-permute-start.5 = (bf16[320,128]{1,0:T(8,128)(2,1)S(1)}, bf16[320,128]{1,0:T(8,128)(2,1)S(1)}, u32[]{:S(2)}, u32[]{:S(2)}) collective-permute-start(bf16[320,128]{1,0:T(8,128)(2,1)S(1)} %get-tuple-element.41), channel_id=1, source_target_pairs={{0,1},{1,0},{2,3},{3,2},{4,6},{5,7},{6,4},{7,5},{8,9},{9,8},{10,11... | collective-permute-start | bytes 245768 | tf_op jit(solution)/shard_map/ppermute | solution.py:257
  17.7 1.1 %collective-permute-start.6 = (bf16[320,128]{1,0:T(8,128)(2,1)S(1)}, bf16[320,128]{1,0:T(8,128)(2,1)S(1)}, u32[]{:S(2)}, u32[]{:S(2)}) collective-permute-start(bf16[320,128]{1,0:T(8,128)(2,1)S(1)} %get-tuple-element.42), channel_id=1, source_target_pairs={{0,2},{1,3},{2,0},{3,1},{4,5},{5,4},{6,7},{7,6},{8,10},{9,11},{10,... | collective-permute-start | bytes 245768 | tf_op jit(solution)/shard_map/ppermute | solution.py:257
  18.8 0.0 collective-permute-done.7.refs_2_
  18.8 1.6 %collective-permute-start.8 = (bf16[176,128]{1,0:T(8,128)(2,1)S(1)}, bf16[176,128]{1,0:T(8,128)(2,1)S(1)}, u32[]{:S(2)}, u32[]{:S(2)}) collective-permute-start(bf16[176,128]{1,0:T(8,128)(2,1)S(1)} %gather.3), channel_id=1, source_target_pairs={{0,8},{4,12},{8,0},{12,4},{16,24},{20,28},{24,16},{28,20},{1,9},{5... | collective-permute-start | bytes 135176 | tf_op jit(solution)/shard_map/ppermute | solution.py:338
  20.5 0.4 %collective-permute-done.4.refs_1_ = bf16[320,128]{1,0:T(8,128)(2,1)S(1)} collective-permute-done((bf16[320,128]{1,0:T(8,128)(2,1)S(1)}, bf16[320,128]{1,0:T(8,128)(2,1)S(1)}, u32[]{:S(2)}, u32[]{:S(2)}) %collective-permute-start.4) | collective-permute-done | bytes 81952 | tf_op jit(solution)/shard_map/ppermute | solution.py:257
  20.9 1.1 %collective-permute-done.5.refs_2_ = bf16[320,128]{1,0:T(8,128)(2,1)S(1)} collective-permute-done((bf16[320,128]{1,0:T(8,128)(2,1)S(1)}, bf16[320,128]{1,0:T(8,128)(2,1)S(1)}, u32[]{:S(2)}, u32[]{:S(2)}) %collective-permute-start.5) | collective-permute-done | bytes 81952 | tf_op jit(solution)/shard_map/ppermute | solution.py:257
  21.9 0.3 %collective-permute-done.6.refs_3_ = bf16[320,128]{1,0:T(8,128)(2,1)S(1)} collective-permute-done((bf16[320,128]{1,0:T(8,128)(2,1)S(1)}, bf16[320,128]{1,0:T(8,128)(2,1)S(1)}, u32[]{:S(2)}, u32[]{:S(2)}) %collective-permute-start.6) | collective-permute-done | bytes 81952 | tf_op jit(solution)/shard_map/ppermute | solution.py:257
  22.2 0.8 %total.1 = f32[6,8192]{1,0:T(8,128)} custom-call(f32[320,128]{1,0:T(8,128)S(1)} %get-tuple-element.34.refs_0_, bf16[320,128]{1,0:T(8,128)(2,1)S(1)} %collective-permute-done.4.refs_1_, bf16[320,128]{1,0:T(8,128)(2,1)S(1)} %collective-permute-done.5.refs_2_, bf16[320,128]{1,0:T(8,128)(2,1)S(1)} %collective-permute-done.6.refs_3_), custom_call_target="tpu_custom_call" | custom-call | tf_op jit(solution)/shard_map/total/pallas_call | solution.py:371
  23.0 0.0 collective-permute-done.8.refs_3_
  23.0 0.7 %arrive.1 = f32[4,8192]{1,0:T(4,128)} custom-call(bf16[128,128]{1,0:T(8,128)(2,1)S(1)} %get-tuple-element.35.refs_0_, bf16[128,128]{1,0:T(8,128)(2,1)S(1)} %collective-permute-done.3.refs_1_, bf16[176,128]{1,0:T(8,128)(2,1)S(1)} %collective-permute-done.7.refs_2_, bf16[176,128]{1,0:T(8,128)(2,1)S(1)} %collective-permute-done.8.refs_3_), custom_call_target="tpu_custom_call" | custom-call | tf_op jit(solution)/shard_map/arrive/pallas_call | solution.py:380
  (3 shorter events, 0.0 us)
Async XLA Ops:
  0.6 5.6 %copy-start.1 = (s32[4096,1]{0,1:T(1,128)S(1)}, s32[4096,1]{0,1:T(1,128)}, u32[]{:S(2)}) copy-start(s32[4096,1]{0,1:T(1,128)} %param.15) | copy-start | bytes 49156
  1.6 7.6 %collective-permute-start = (bf16[320,128]{1,0:T(8,128)(2,1)S(1)}, bf16[320,128]{1,0:T(8,128)(2,1)S(1)}, u32[]{:S(2)}, u32[]{:S(2)}) collective-permute-start(bf16[320,128]{1,0:T(8,128)(2,1)S(1)} %get-tuple-element.32.refs_8_), channel_id=1, source_target_pairs={{0,3},{1,2},{2,1},{3,0},{4,7},{5,6},{6,5},{7,4},{8,11},{9,10},{10,... | collective-permute-start | bytes 245768 | tf_op jit(solution)/shard_map/ppermute | solution.py:257
  5.6 4.7 %collective-permute-start.1 = (bf16[320,128]{1,0:T(8,128)(2,1)S(1)}, bf16[320,128]{1,0:T(8,128)(2,1)S(1)}, u32[]{:S(2)}, u32[]{:S(2)}) collective-permute-start(bf16[320,128]{1,0:T(8,128)(2,1)S(1)} %get-tuple-element.32.refs_8_), channel_id=1, source_target_pairs={{0,1},{1,0},{2,3},{3,2},{4,6},{5,7},{6,4},{7,5},{8,9},{9,8},{10,11... | collective-permute-start | bytes 245768 | tf_op jit(solution)/shard_map/ppermute | solution.py:257
  6.1 4.4 %collective-permute-start.2 = (bf16[320,128]{1,0:T(8,128)(2,1)S(1)}, bf16[320,128]{1,0:T(8,128)(2,1)S(1)}, u32[]{:S(2)}, u32[]{:S(2)}) collective-permute-start(bf16[320,128]{1,0:T(8,128)(2,1)S(1)} %get-tuple-element.32.refs_8_), channel_id=1, source_target_pairs={{0,2},{1,3},{2,0},{3,1},{4,5},{5,4},{6,7},{7,6},{8,10},{9,11},{10,... | collective-permute-start | bytes 245768 | tf_op jit(solution)/shard_map/ppermute | solution.py:257
  6.3 1.9 %copy-start = (f32[3,4096]{1,0:T(4,128)S(1)}, f32[3,4096]{1,0:T(4,128)}, u32[]{:S(2)}) copy-start(f32[3,4096]{1,0:T(4,128)} %refs_2_.1) | copy-start | bytes 147460
  6.3 1.9 %copy-start.2 = (s32[4096]{0:T(1024)S(1)}, s32[4096]{0:T(1024)}, u32[]{:S(2)}) copy-start(s32[4096]{0:T(1024)} %param.12) | copy-start | bytes 49156
  8.1 2.4 %copy-start.3 = (f32[4096]{0:T(1024)S(1)}, f32[4096]{0:T(1024)}, u32[]{:S(2)}) copy-start(f32[4096]{0:T(1024)} %param.13) | copy-start | bytes 49156
  11.4 1.3 %collective-permute-start.3 = (bf16[128,128]{1,0:T(8,128)(2,1)S(1)}, bf16[128,128]{1,0:T(8,128)(2,1)S(1)}, u32[]{:S(2)}, u32[]{:S(2)}) collective-permute-start(bf16[128,128]{1,0:T(8,128)(2,1)S(1)} %get-tuple-element.36), channel_id=1, source_target_pairs={{0,4},{4,0},{8,12},{12,8},{16,20},{20,16},{24,28},{28,24},{1,5},{5... | collective-permute-start | bytes 98312 | tf_op jit(solution)/shard_map/ppermute | solution.py:338
  12.7 6.1 %collective-permute-start.7 = (bf16[176,128]{1,0:T(8,128)(2,1)S(1)}, bf16[176,128]{1,0:T(8,128)(2,1)S(1)}, u32[]{:S(2)}, u32[]{:S(2)}) collective-permute-start(bf16[176,128]{1,0:T(8,128)(2,1)S(1)} %get-tuple-element.43), channel_id=1, source_target_pairs={{0,16},{4,20},{8,24},{12,28},{16,0},{20,4},{24,8},{28,12},{1,17},{... | collective-permute-start | bytes 135176 | tf_op jit(solution)/shard_map/ppermute | solution.py:338
  15.3 5.6 %collective-permute-start.4 = (bf16[320,128]{1,0:T(8,128)(2,1)S(1)}, bf16[320,128]{1,0:T(8,128)(2,1)S(1)}, u32[]{:S(2)}, u32[]{:S(2)}) collective-permute-start(bf16[320,128]{1,0:T(8,128)(2,1)S(1)} %get-tuple-element.40), channel_id=1, source_target_pairs={{0,3},{1,2},{2,1},{3,0},{4,7},{5,6},{6,5},{7,4},{8,11},{9,10},{10,... | collective-permute-start | bytes 245768 | tf_op jit(solution)/shard_map/ppermute | solution.py:257
  17.1 4.8 %collective-permute-start.5 = (bf16[320,128]{1,0:T(8,128)(2,1)S(1)}, bf16[320,128]{1,0:T(8,128)(2,1)S(1)}, u32[]{:S(2)}, u32[]{:S(2)}) collective-permute-start(bf16[320,128]{1,0:T(8,128)(2,1)S(1)} %get-tuple-element.41), channel_id=1, source_target_pairs={{0,1},{1,0},{2,3},{3,2},{4,6},{5,7},{6,4},{7,5},{8,9},{9,8},{10,11... | collective-permute-start | bytes 245768 | tf_op jit(solution)/shard_map/ppermute | solution.py:257
  17.7 4.5 %collective-permute-start.6 = (bf16[320,128]{1,0:T(8,128)(2,1)S(1)}, bf16[320,128]{1,0:T(8,128)(2,1)S(1)}, u32[]{:S(2)}, u32[]{:S(2)}) collective-permute-start(bf16[320,128]{1,0:T(8,128)(2,1)S(1)} %get-tuple-element.42), channel_id=1, source_target_pairs={{0,2},{1,3},{2,0},{3,1},{4,5},{5,4},{6,7},{7,6},{8,10},{9,11},{10,... | collective-permute-start | bytes 245768 | tf_op jit(solution)/shard_map/ppermute | solution.py:257
  18.8 4.2 %collective-permute-start.8 = (bf16[176,128]{1,0:T(8,128)(2,1)S(1)}, bf16[176,128]{1,0:T(8,128)(2,1)S(1)}, u32[]{:S(2)}, u32[]{:S(2)}) collective-permute-start(bf16[176,128]{1,0:T(8,128)(2,1)S(1)} %gather.3), channel_id=1, source_target_pairs={{0,8},{4,12},{8,0},{12,4},{16,24},{20,28},{24,16},{28,20},{1,9},{5... | collective-permute-start | bytes 135176 | tf_op jit(solution)/shard_map/ppermute | solution.py:338

commit v8 on v7

--- a/solution.py
+++ b/solution.py
@@ -78,7 +78,7 @@
         packed_ref[c * blocks : (c + 1) * blocks, :] = value.astype(jnp.bfloat16)
 
 
-def code_kernel(slabs, cap, target_ref, source_ref, high_ref, low_ref, weight_ref, sem):
+def code_kernel(slabs, cap, target_ref, source_ref, high_ref, low_ref, weight_ref, across_ref, sem):
     fetch = pltpu.make_async_copy(source_ref, weight_ref, sem)
     fetch.start()
     chunks = target_ref.shape[0]
@@ -102,6 +102,12 @@
         high_ref[:, at] = mask(iota((rows, LANES), 0) == high[r : r + 1, :])
         low_ref[at, :] = mask(iota((LANES, LANES), 1) == low[:, r : r + 1])
     fetch.wait()
+    unit = mask(iota((LANES, LANES), 0) == iota((LANES, LANES), 1))
+    span = PACK * SEGB
+    for g in range(weight_ref.shape[0] // span):
+        at = pl.ds(g * span, span)
+        turn = lax.dot_general(unit, weight_ref[at, :], CONTRACT_LANES, preferred_element_type=jnp.float32)
+        across_ref[:, at] = turn.astype(jnp.bfloat16)
 
 
 def prepare_kernel(*refs):
@@ -132,7 +138,7 @@
 
 
 def glide_kernel(order, slabs, *refs):
-    pick_ref, mobility_ref, factor_ref, high_ref, low_ref, start_ref, course_ref, weight_ref = refs[:8]
+    pick_ref, mobility_ref, factor_ref, high_ref, low_ref, start_ref, course_ref, across_ref = refs[:8]
     group = len(order)
     stress_refs = [refs[8 + order.index(k)] for k in range(group)]
     term_ref = refs[8 + group]
@@ -150,7 +156,7 @@
     for g in range(blocks // PACK):
         stress = jnp.concatenate([x[g * PACK : (g + 1) * PACK] for x in picked], axis=0).astype(jnp.bfloat16)
         at = pl.ds(g * span, span)
-        sampled = lax.dot_general(stress, weight_ref[at, :], CONTRACT_LANES, preferred_element_type=jnp.float32)
+        sampled = jnp.dot(stress, across_ref[:, at], preferred_element_type=jnp.float32)
         resolved = sampled[:PACK] * factor_ref[:1, at]
         for c in range(1, NR):
             resolved = resolved + sampled[c * PACK : (c + 1) * PACK] * factor_ref[c : c + 1, at]
@@ -278,18 +284,19 @@
     )(still(stress), still(block_owner.reshape(1, blocks)), still(block_local.reshape(1, blocks)))
     parts = {k: swap(packed, k) for k in peers}
     parts[0] = packed
-    order = [0, *peers]
+    order = [0, *peers[::-1]]
 
     slot_shape = (3 * slot_rows, LANES)
-    high, low, weight = pl.pallas_call(
+    high, low, weight, weight_across = pl.pallas_call(
         functools.partial(code_kernel, slabs, cap),
         out_shape=(
             shape((slot_rows, segments), bf16),
             shape((segments, LANES), bf16),
             shape((segments, BLK), bf16),
+            shape((BLK, segments), bf16),
         ),
         in_specs=[VMEM, HBM],
-        out_specs=[VMEM] * 3,
+        out_specs=[VMEM] * 4,
         scratch_shapes=[pltpu.SemaphoreType.DMA],
         compiler_params=params,
         name="code",
@@ -330,7 +337,7 @@
         low,
         start,
         course,
-        weight,
+        weight_across,
         *[parts[k] for k in order],
     )
 

time: 23.8 us -> 23.7 us (level)
  transfers between devices with their start and end apart: 9 -> 9, of which waited for: 6 -> 6; matrix products, arithmetic and copies ran while one was open for 0% -> 0% of each run, Pallas kernels for 18% -> 19%
where the time goes in v8:
time: 23.7 us; the launch traced here: 23.5 us
  starting transfers between devices  12.4 us (52%)
  Pallas kernels  6.9 us (29%)
  waiting for transfers between devices  3.49 us (15%)
  between operations  0.73 us (3%)
    ppermute x6, starting transfers between devices, swap(): return lax.ppermute(x, ('slab', 'grp'), pairs)  8.09 us
    ppermute x3, starting transfers between devices, hop(): return lax.ppermute(x, 'slab', [(i, i ^ k) for i in range(slabs)])  4.3 us
    ppermute x6, waiting for transfers between devices, swap(): return lax.ppermute(x, ('slab', 'grp'), pairs)  2.84 us
    pallas_call x1, Pallas kernels, body(): pl.pallas_call(functools.partial(code_kernel, slabs, cap), out_shape=(sha...  2.07 us
    pallas_call x1, Pallas kernels, body(): pl.pallas_call(prepare_kernel, out_shape=(shape((SUB, segments), f32), sh...  1.1 us
    pallas_call x1, Pallas kernels, body(): pl.pallas_call(functools.partial(pack_kernel, group), out_shape=(shape((N...  1 us
    pallas_call x1, Pallas kernels, body(): pl.pallas_call(total_kernel, out_shape=shape((NC, voxels), f32), in_specs...  0.8 us
    pallas_call x1, Pallas kernels, body(): pl.pallas_call(functools.partial(arrive_kernel, slabs, {s: at for (_, s),...  0.7 us
  transfers between devices with their start and end apart: 9, of which 6 were waited for; matrix products, arithmetic and copies ran while one was open for 0% of the time, Pallas kernels for 19%

profile of v8, /device:TPU:0, one launch (start us, length us, event | category | flops | bytes accessed | tf_op | source)
XLA Modules:
  0.0 23.5 jit_solution(16513579379992970268)
XLA Ops:
  0.6 0.0 copy-start.1
  0.6 1.0 %pack.1 = (bf16[320,128]{1,0:T(8,128)(2,1)S(1)}, s32[1,64]{1,0:T(1,128)S(1)}) custom-call(bf16[6,8192]{1,0:T(8,128)(2,1)} %source_ref.1, s32[1,64]{1,0:T(1,128)} %bitcast.10, s32[1,64]{1,0:T(1,128)} %bitcast.11), custom_call_target="tpu_custom_call" | custom-call | tf_op jit(solution)/shard_map/pack/pallas_call | solution.py:271
  1.6 4.0 %collective-permute-start.2 = (bf16[320,128]{1,0:T(8,128)(2,1)S(1)}, bf16[320,128]{1,0:T(8,128)(2,1)S(1)}, u32[]{:S(2)}, u32[]{:S(2)}) collective-permute-start(bf16[320,128]{1,0:T(8,128)(2,1)S(1)} %get-tuple-element.33.refs_8_), channel_id=1, source_target_pairs={{0,3},{1,2},{2,1},{3,0},{4,7},{5,6},{6,5},{7,4},{8,11},{9,10},{10,... | collective-permute-start | bytes 245768 | tf_op jit(solution)/shard_map/ppermute | solution.py:263
  5.6 0.5 %collective-permute-start.1 = (bf16[320,128]{1,0:T(8,128)(2,1)S(1)}, bf16[320,128]{1,0:T(8,128)(2,1)S(1)}, u32[]{:S(2)}, u32[]{:S(2)}) collective-permute-start(bf16[320,128]{1,0:T(8,128)(2,1)S(1)} %get-tuple-element.33.refs_8_), channel_id=1, source_target_pairs={{0,1},{1,0},{2,3},{3,2},{4,6},{5,7},{6,4},{7,5},{8,9},{9,8},{10,11... | collective-permute-start | bytes 245768 | tf_op jit(solution)/shard_map/ppermute | solution.py:263
  6.1 0.1 collective-permute-start
  6.2 0.0 copy-done.1
  6.3 0.0 copy-start
  6.3 2.1 %code.1 = (bf16[64,4096]{1,0:T(8,128)(2,1)S(1)}, bf16[4096,128]{1,0:T(8,128)(2,1)S(1)}, bf16[4096,128]{1,0:T(8,128)(2,1)S(1)}, bf16[128,4096]{1,0:T(8,128)(2,1)S(1)}) custom-call(s32[32,128]{1,0:T(8,128)S(1)} %bitcast.6, bf16[4096,128]{1,0:T(8,128)(2,1)} %bitcast.9), custom_call_target="tpu_custom_call" | custom-call | tf_op jit(solution)/shard_map/code/pallas_call | solution.py:290
  8.3 0.0 copy-done
  8.3 0.0 copy-done.2
  8.4 0.0 copy-start.3
  8.4 1.1 %prepare.1 = (f32[8,4096]{1,0:T(8,128)S(1)}, bf16[64,256]{1,0:T(8,128)(2,1)S(1)}, bf16[256,128]{1,0:T(8,128)(2,1)S(1)}, f32[192,128]{1,0:T(8,128)S(1)}, f32[192,128]{1,0:T(8,128)S(1)}) custom-call(s32[1,4096]{1,0:T(1,128)S(1)} %bitcast.7, s32[1,64]{1,0:T(1,128)S(1)} %get-tuple-element.24.refs_1_, f32[3,4096]{1,0:T(4,128)S(1)} %copy-done, ...), custom_call_target="tpu_custom_call" | custom-call | tf_op jit(solution)/shard_map/prepare/pallas_call | solution.py:304
  9.5 0.0 collective-permute-done.2.refs_11_
  9.5 0.8 %collective-permute-done.1.refs_10_ = bf16[320,128]{1,0:T(8,128)(2,1)S(1)} collective-permute-done((bf16[320,128]{1,0:T(8,128)(2,1)S(1)}, bf16[320,128]{1,0:T(8,128)(2,1)S(1)}, u32[]{:S(2)}, u32[]{:S(2)}) %collective-permute-start.1) | collective-permute-done | bytes 81952 | tf_op jit(solution)/shard_map/ppermute | solution.py:263
  10.3 0.3 %collective-permute-done.refs_9_ = bf16[320,128]{1,0:T(8,128)(2,1)S(1)} collective-permute-done((bf16[320,128]{1,0:T(8,128)(2,1)S(1)}, bf16[320,128]{1,0:T(8,128)(2,1)S(1)}, u32[]{:S(2)}, u32[]{:S(2)}) %collective-permute-start) | collective-permute-done | bytes 81952 | tf_op jit(solution)/shard_map/ppermute | solution.py:263
  10.6 0.0 copy-done.3
  10.6 0.7 %glide.1 = (f32[8,4096]{1,0:T(8,128)S(1)}, bf16[128,128]{1,0:T(8,128)(2,1)S(1)}, bf16[128,128]{1,0:T(8,128)(2,1)S(1)}) custom-call(bf16[64,256]{1,0:T(8,128)(2,1)S(1)} %get-tuple-element.28.refs_0_, f32[1,4096]{1,0:T(1,128)S(1)} %bitcast.8, f32[8,4096]{1,0:T(8,128)S(1)} %get-tuple-element.29.refs_2_, bf16[64,4096]{1,0:T(8,128)(2,1)S(1)} %get-tuple-element.25.refs_3_, ...), custom_call_target="tpu_custom_call" | custom-call | tf_op jit(solution)/shard_map/glide/pallas_call | solution.py:321
  11.3 0.1 collective-permute-start.3
  11.3 0.5 %spread.1 = (f32[320,128]{1,0:T(8,128)S(1)}, bf16[320,128]{1,0:T(8,128)(2,1)S(1)}, bf16[320,128]{1,0:T(8,128)(2,1)S(1)}, bf16[320,128]{1,0:T(8,128)(2,1)S(1)}) custom-call(bf16[256,128]{1,0:T(8,128)(2,1)S(1)} %get-tuple-element.27.refs_0_, f32[8,4096]{1,0:T(8,128)S(1)} %get-tuple-element.34.refs_1_, bf16[4096,128]{1,0:T(8,128)(2,1)S(1)} %get-tuple-element.35.refs_2_), custom_call_target="tpu_custom_call" | custom-call | tf_op jit(solution)/shard_map/spread/pallas_call | solution.py:349
  11.9 0.7 %collective-permute-done.3.refs_1_ = bf16[128,128]{1,0:T(8,128)(2,1)S(1)} collective-permute-done((bf16[128,128]{1,0:T(8,128)(2,1)S(1)}, bf16[128,128]{1,0:T(8,128)(2,1)S(1)}, u32[]{:S(2)}, u32[]{:S(2)}) %collective-permute-start.3) | collective-permute-done | bytes 32800 | tf_op jit(solution)/shard_map/ppermute | solution.py:345
  12.5 2.6 %collective-permute-start.7 = (bf16[176,128]{1,0:T(8,128)(2,1)S(1)}, bf16[176,128]{1,0:T(8,128)(2,1)S(1)}, u32[]{:S(2)}, u32[]{:S(2)}) collective-permute-start(bf16[176,128]{1,0:T(8,128)(2,1)S(1)} %get-tuple-element.45), channel_id=1, source_target_pairs={{0,16},{4,20},{8,24},{12,28},{16,0},{20,4},{24,8},{28,12},{1,17},{... | collective-permute-start | bytes 135176 | tf_op jit(solution)/shard_map/ppermute | solution.py:345
  15.1 1.8 %collective-permute-start.4 = (bf16[320,128]{1,0:T(8,128)(2,1)S(1)}, bf16[320,128]{1,0:T(8,128)(2,1)S(1)}, u32[]{:S(2)}, u32[]{:S(2)}) collective-permute-start(bf16[320,128]{1,0:T(8,128)(2,1)S(1)} %get-tuple-element.42), channel_id=1, source_target_pairs={{0,3},{1,2},{2,1},{3,0},{4,7},{5,6},{6,5},{7,4},{8,11},{9,10},{10,... | collective-permute-start | bytes 245768 | tf_op jit(solution)/shard_map/ppermute | solution.py:263
  16.9 0.6 %collective-permute-start.5 = (bf16[320,128]{1,0:T(8,128)(2,1)S(1)}, bf16[320,128]{1,0:T(8,128)(2,1)S(1)}, u32[]{:S(2)}, u32[]{:S(2)}) collective-permute-start(bf16[320,128]{1,0:T(8,128)(2,1)S(1)} %get-tuple-element.43), channel_id=1, source_target_pairs={{0,1},{1,0},{2,3},{3,2},{4,6},{5,7},{6,4},{7,5},{8,9},{9,8},{10,11... | collective-permute-start | bytes 245768 | tf_op jit(solution)/shard_map/ppermute | solution.py:263
  17.5 1.1 %collective-permute-start.6 = (bf16[320,128]{1,0:T(8,128)(2,1)S(1)}, bf16[320,128]{1,0:T(8,128)(2,1)S(1)}, u32[]{:S(2)}, u32[]{:S(2)}) collective-permute-start(bf16[320,128]{1,0:T(8,128)(2,1)S(1)} %get-tuple-element.44), channel_id=1, source_target_pairs={{0,2},{1,3},{2,0},{3,1},{4,5},{5,4},{6,7},{7,6},{8,10},{9,11},{10,... | collective-permute-start | bytes 245768 | tf_op jit(solution)/shard_map/ppermute | solution.py:263
  18.6 0.0 collective-permute-done.7.refs_2_
  18.6 1.6 %collective-permute-start.8 = (bf16[176,128]{1,0:T(8,128)(2,1)S(1)}, bf16[176,128]{1,0:T(8,128)(2,1)S(1)}, u32[]{:S(2)}, u32[]{:S(2)}) collective-permute-start(bf16[176,128]{1,0:T(8,128)(2,1)S(1)} %gather.3), channel_id=1, source_target_pairs={{0,8},{4,12},{8,0},{12,4},{16,24},{20,28},{24,16},{28,20},{1,9},{5... | collective-permute-start | bytes 135176 | tf_op jit(solution)/shard_map/ppermute | solution.py:345
  20.3 0.4 %collective-permute-done.4.refs_1_ = bf16[320,128]{1,0:T(8,128)(2,1)S(1)} collective-permute-done((bf16[320,128]{1,0:T(8,128)(2,1)S(1)}, bf16[320,128]{1,0:T(8,128)(2,1)S(1)}, u32[]{:S(2)}, u32[]{:S(2)}) %collective-permute-start.4) | collective-permute-done | bytes 81952 | tf_op jit(solution)/shard_map/ppermute | solution.py:263
  20.7 1.1 %collective-permute-done.5.refs_2_ = bf16[320,128]{1,0:T(8,128)(2,1)S(1)} collective-permute-done((bf16[320,128]{1,0:T(8,128)(2,1)S(1)}, bf16[320,128]{1,0:T(8,128)(2,1)S(1)}, u32[]{:S(2)}, u32[]{:S(2)}) %collective-permute-start.5) | collective-permute-done | bytes 81952 | tf_op jit(solution)/shard_map/ppermute | solution.py:263
  21.8 0.3 %collective-permute-done.6.refs_3_ = bf16[320,128]{1,0:T(8,128)(2,1)S(1)} collective-permute-done((bf16[320,128]{1,0:T(8,128)(2,1)S(1)}, bf16[320,128]{1,0:T(8,128)(2,1)S(1)}, u32[]{:S(2)}, u32[]{:S(2)}) %collective-permute-start.6) | collective-permute-done | bytes 81952 | tf_op jit(solution)/shard_map/ppermute | solution.py:263
  22.0 0.8 %total.1 = f32[6,8192]{1,0:T(8,128)} custom-call(f32[320,128]{1,0:T(8,128)S(1)} %get-tuple-element.36.refs_0_, bf16[320,128]{1,0:T(8,128)(2,1)S(1)} %collective-permute-done.4.refs_1_, bf16[320,128]{1,0:T(8,128)(2,1)S(1)} %collective-permute-done.5.refs_2_, bf16[320,128]{1,0:T(8,128)(2,1)S(1)} %collective-permute-done.6.refs_3_), custom_call_target="tpu_custom_call" | custom-call | tf_op jit(solution)/shard_map/total/pallas_call | solution.py:378
  22.8 0.0 collective-permute-done.8.refs_3_
  22.8 0.7 %arrive.1 = f32[4,8192]{1,0:T(4,128)} custom-call(bf16[128,128]{1,0:T(8,128)(2,1)S(1)} %get-tuple-element.37.refs_0_, bf16[128,128]{1,0:T(8,128)(2,1)S(1)} %collective-permute-done.3.refs_1_, bf16[176,128]{1,0:T(8,128)(2,1)S(1)} %collective-permute-done.7.refs_2_, bf16[176,128]{1,0:T(8,128)(2,1)S(1)} %collective-permute-done.8.refs_3_), custom_call_target="tpu_custom_call" | custom-call | tf_op jit(solution)/shard_map/arrive/pallas_call | solution.py:387
  (3 shorter events, 0.0 us)
Async XLA Ops:
  0.6 5.6 %copy-start.1 = (s32[4096,1]{0,1:T(1,128)S(1)}, s32[4096,1]{0,1:T(1,128)}, u32[]{:S(2)}) copy-start(s32[4096,1]{0,1:T(1,128)} %param.15) | copy-start | bytes 49156
  1.6 7.8 %collective-permute-start.2 = (bf16[320,128]{1,0:T(8,128)(2,1)S(1)}, bf16[320,128]{1,0:T(8,128)(2,1)S(1)}, u32[]{:S(2)}, u32[]{:S(2)}) collective-permute-start(bf16[320,128]{1,0:T(8,128)(2,1)S(1)} %get-tuple-element.33.refs_8_), channel_id=1, source_target_pairs={{0,3},{1,2},{2,1},{3,0},{4,7},{5,6},{6,5},{7,4},{8,11},{9,10},{10,... | collective-permute-start | bytes 245768 | tf_op jit(solution)/shard_map/ppermute | solution.py:263
  5.6 4.7 %collective-permute-start.1 = (bf16[320,128]{1,0:T(8,128)(2,1)S(1)}, bf16[320,128]{1,0:T(8,128)(2,1)S(1)}, u32[]{:S(2)}, u32[]{:S(2)}) collective-permute-start(bf16[320,128]{1,0:T(8,128)(2,1)S(1)} %get-tuple-element.33.refs_8_), channel_id=1, source_target_pairs={{0,1},{1,0},{2,3},{3,2},{4,6},{5,7},{6,4},{7,5},{8,9},{9,8},{10,11... | collective-permute-start | bytes 245768 | tf_op jit(solution)/shard_map/ppermute | solution.py:263
  6.1 4.4 %collective-permute-start = (bf16[320,128]{1,0:T(8,128)(2,1)S(1)}, bf16[320,128]{1,0:T(8,128)(2,1)S(1)}, u32[]{:S(2)}, u32[]{:S(2)}) collective-permute-start(bf16[320,128]{1,0:T(8,128)(2,1)S(1)} %get-tuple-element.33.refs_8_), channel_id=1, source_target_pairs={{0,2},{1,3},{2,0},{3,1},{4,5},{5,4},{6,7},{7,6},{8,10},{9,11},{10,... | collective-permute-start | bytes 245768 | tf_op jit(solution)/shard_map/ppermute | solution.py:263
  6.3 2.1 %copy-start = (f32[3,4096]{1,0:T(4,128)S(1)}, f32[3,4096]{1,0:T(4,128)}, u32[]{:S(2)}) copy-start(f32[3,4096]{1,0:T(4,128)} %refs_2_.1) | copy-start | bytes 147460
  6.3 2.1 %copy-start.2 = (s32[4096]{0:T(1024)S(1)}, s32[4096]{0:T(1024)}, u32[]{:S(2)}) copy-start(s32[4096]{0:T(1024)} %param.12) | copy-start | bytes 49156
  8.4 2.2 %copy-start.3 = (f32[4096]{0:T(1024)S(1)}, f32[4096]{0:T(1024)}, u32[]{:S(2)}) copy-start(f32[4096]{0:T(1024)} %param.13) | copy-start | bytes 49156
  11.3 1.3 %collective-permute-start.3 = (bf16[128,128]{1,0:T(8,128)(2,1)S(1)}, bf16[128,128]{1,0:T(8,128)(2,1)S(1)}, u32[]{:S(2)}, u32[]{:S(2)}) collective-permute-start(bf16[128,128]{1,0:T(8,128)(2,1)S(1)} %get-tuple-element.38), channel_id=1, source_target_pairs={{0,4},{4,0},{8,12},{12,8},{16,20},{20,16},{24,28},{28,24},{1,5},{5... | collective-permute-start | bytes 98312 | tf_op jit(solution)/shard_map/ppermute | solution.py:345
  12.5 6.1 %collective-permute-start.7 = (bf16[176,128]{1,0:T(8,128)(2,1)S(1)}, bf16[176,128]{1,0:T(8,128)(2,1)S(1)}, u32[]{:S(2)}, u32[]{:S(2)}) collective-permute-start(bf16[176,128]{1,0:T(8,128)(2,1)S(1)} %get-tuple-element.45), channel_id=1, source_target_pairs={{0,16},{4,20},{8,24},{12,28},{16,0},{20,4},{24,8},{28,12},{1,17},{... | collective-permute-start | bytes 135176 | tf_op jit(solution)/shard_map/ppermute | solution.py:345
  15.1 5.6 %collective-permute-start.4 = (bf16[320,128]{1,0:T(8,128)(2,1)S(1)}, bf16[320,128]{1,0:T(8,128)(2,1)S(1)}, u32[]{:S(2)}, u32[]{:S(2)}) collective-permute-start(bf16[320,128]{1,0:T(8,128)(2,1)S(1)} %get-tuple-element.42), channel_id=1, source_target_pairs={{0,3},{1,2},{2,1},{3,0},{4,7},{5,6},{6,5},{7,4},{8,11},{9,10},{10,... | collective-permute-start | bytes 245768 | tf_op jit(solution)/shard_map/ppermute | solution.py:263
  16.9 4.8 %collective-permute-start.5 = (bf16[320,128]{1,0:T(8,128)(2,1)S(1)}, bf16[320,128]{1,0:T(8,128)(2,1)S(1)}, u32[]{:S(2)}, u32[]{:S(2)}) collective-permute-start(bf16[320,128]{1,0:T(8,128)(2,1)S(1)} %get-tuple-element.43), channel_id=1, source_target_pairs={{0,1},{1,0},{2,3},{3,2},{4,6},{5,7},{6,4},{7,5},{8,9},{9,8},{10,11... | collective-permute-start | bytes 245768 | tf_op jit(solution)/shard_map/ppermute | solution.py:263
  17.5 4.5 %collective-permute-start.6 = (bf16[320,128]{1,0:T(8,128)(2,1)S(1)}, bf16[320,128]{1,0:T(8,128)(2,1)S(1)}, u32[]{:S(2)}, u32[]{:S(2)}) collective-permute-start(bf16[320,128]{1,0:T(8,128)(2,1)S(1)} %get-tuple-element.44), channel_id=1, source_target_pairs={{0,2},{1,3},{2,0},{3,1},{4,5},{5,4},{6,7},{7,6},{8,10},{9,11},{10,... | collective-permute-start | bytes 245768 | tf_op jit(solution)/shard_map/ppermute | solution.py:263
  18.6 4.2 %collective-permute-start.8 = (bf16[176,128]{1,0:T(8,128)(2,1)S(1)}, bf16[176,128]{1,0:T(8,128)(2,1)S(1)}, u32[]{:S(2)}, u32[]{:S(2)}) collective-permute-start(bf16[176,128]{1,0:T(8,128)(2,1)S(1)} %gather.3), channel_id=1, source_target_pairs={{0,8},{4,12},{8,0},{12,4},{16,24},{20,28},{24,16},{28,20},{1,9},{5... | collective-permute-start | bytes 135176 | tf_op jit(solution)/shard_map/ppermute | solution.py:345

commit v9 on v8

--- a/solution.py
+++ b/solution.py
@@ -141,9 +141,7 @@
     pick_ref, mobility_ref, factor_ref, high_ref, low_ref, start_ref, course_ref, across_ref = refs[:8]
     group = len(order)
     stress_refs = [refs[8 + order.index(k)] for k in range(group)]
-    term_ref = refs[8 + group]
-    keep_ref, send_ref = refs[9 + group : 11 + group]
-    step_ref, move_ref = refs[11 + group :]
+    step_ref, keep_ref, send_ref, move_ref = refs[8 + group :]
     blocks = pick_ref.shape[0]
     held = stress_refs[0].shape[0] // NR
     picked = []
@@ -163,7 +161,6 @@
         resolved = jnp.sum(jnp.where(mine, resolved, 0.0), axis=0, keepdims=True)
         step = glide_time * mobility_ref[:, at] * resolved
         step_ref[:, at] = step
-        term_ref[:, at] = step * factor_ref[:, at]
 
     step = step_ref[...]
     high = high_ref[...]
@@ -184,8 +181,8 @@
 
 
 def spread_kernel(group, *refs):
-    put_ref, term_ref, weight_ref, kept_ref = refs[:4]
-    sent_refs = refs[4 : 3 + group]
+    put_ref, step_ref, factor_ref, weight_ref, kept_ref = refs[:5]
+    sent_refs = refs[5:]
     blocks = put_ref.shape[1] // 2
     held = kept_ref.shape[0] // NR
     span = PACK * SEGB
@@ -193,7 +190,7 @@
     parts = []
     for g in range(blocks // PACK):
         at = pl.ds(g * span, span)
-        terms = [jnp.where(mine, term_ref[c : c + 1, at], 0.0) for c in range(NR)]
+        terms = [jnp.where(mine, step_ref[:, at] * factor_ref[c : c + 1, at], 0.0) for c in range(NR)]
         terms = jnp.concatenate(terms, axis=0).astype(jnp.bfloat16)
         parts.append(jnp.dot(terms, weight_ref[at, :], preferred_element_type=jnp.float32))
     for c in range(NR):
@@ -318,15 +315,12 @@
     )(slip_system.reshape(1, segments), place, position, high, low)
 
     chunk = 4 * slot_rows // slabs
-    term, keep, send = pl.pallas_call(
+    step, keep, send = pl.pallas_call(
         functools.partial(glide_kernel, order, slabs),
-        out_shape=(shape((SUB, segments), f32),) + (shape((slabs // 2 * chunk, LANES), bf16),) * 2,
+        out_shape=(shape((1, segments), f32),) + (shape((slabs // 2 * chunk, LANES), bf16),) * 2,
         in_specs=[VMEM] * (8 + group),
         out_specs=[VMEM] * 3,
-        scratch_shapes=[
-            pltpu.VMEM((1, segments), f32),
-            pltpu.VMEM((4 * slot_rows, LANES), f32),
-        ],
+        scratch_shapes=[pltpu.VMEM((4 * slot_rows, LANES), f32)],
         compiler_params=params,
         name="glide",
     )(
@@ -349,11 +343,11 @@
     kept, *sent = pl.pallas_call(
         functools.partial(spread_kernel, group),
         out_shape=(shape(packed.shape, f32),) + (shape(packed.shape, bf16),) * (group - 1),
-        in_specs=[VMEM] * 3,
+        in_specs=[VMEM] * 4,
         out_specs=[VMEM] * group,
         compiler_params=params,
         name="spread",
-    )(put, term, weight)
+    )(put, step, factor, weight)
     bit = slabs
     while bit > 2:
         bit //= 2

time: 23.7 us -> 23.7 us (level)
  no operation moved by 1% of the time
where the time goes in v9:
time: 23.7 us; the launch traced here: 23.5 us
  starting transfers between devices  12.4 us (52%)
  Pallas kernels  6.88 us (29%)
  waiting for transfers between devices  3.49 us (15%)
  between operations  0.73 us (3%)
    ppermute x6, starting transfers between devices, swap(): return lax.ppermute(x, ('slab', 'grp'), pairs)  8.09 us
    ppermute x3, starting transfers between devices, hop(): return lax.ppermute(x, 'slab', [(i, i ^ k) for i in range(slabs)])  4.3 us
    ppermute x6, waiting for transfers between devices, swap(): return lax.ppermute(x, ('slab', 'grp'), pairs)  2.83 us
    pallas_call x1, Pallas kernels, body(): pl.pallas_call(functools.partial(code_kernel, slabs, cap), out_shape=(sha...  2.07 us
    pallas_call x1, Pallas kernels, body(): pl.pallas_call(prepare_kernel, out_shape=(shape((SUB, segments), f32), sh...  1.11 us
    pallas_call x1, Pallas kernels, body(): pl.pallas_call(functools.partial(pack_kernel, group), out_shape=(shape((N...  1 us
    pallas_call x1, Pallas kernels, body(): pl.pallas_call(total_kernel, out_shape=shape((NC, voxels), f32), in_specs...  0.8 us
    pallas_call x1, Pallas kernels, body(): pl.pallas_call(functools.partial(arrive_kernel, slabs, {s: at for (_, s),...  0.7 us
  transfers between devices with their start and end apart: 9, of which 6 were waited for; matrix products, arithmetic and copies ran while one was open for 0% of the time, Pallas kernels for 19%

profile of v9, /device:TPU:0, one launch (start us, length us, event | category | flops | bytes accessed | tf_op | source)
XLA Modules:
  0.0 23.5 jit_solution(16184947416665844084)
XLA Ops:
  0.6 0.0 copy-start.1
  0.6 1.0 %pack.1 = (bf16[320,128]{1,0:T(8,128)(2,1)S(1)}, s32[1,64]{1,0:T(1,128)S(1)}) custom-call(bf16[6,8192]{1,0:T(8,128)(2,1)} %source_ref.1, s32[1,64]{1,0:T(1,128)} %bitcast.10, s32[1,64]{1,0:T(1,128)} %bitcast.11), custom_call_target="tpu_custom_call" | custom-call | tf_op jit(solution)/shard_map/pack/pallas_call | solution.py:268
  1.6 4.0 %collective-permute-start.2 = (bf16[320,128]{1,0:T(8,128)(2,1)S(1)}, bf16[320,128]{1,0:T(8,128)(2,1)S(1)}, u32[]{:S(2)}, u32[]{:S(2)}) collective-permute-start(bf16[320,128]{1,0:T(8,128)(2,1)S(1)} %get-tuple-element.33.refs_8_), channel_id=1, source_target_pairs={{0,3},{1,2},{2,1},{3,0},{4,7},{5,6},{6,5},{7,4},{8,11},{9,10},{10,... | collective-permute-start | bytes 245768 | tf_op jit(solution)/shard_map/ppermute | solution.py:260
  5.6 0.5 %collective-permute-start.1 = (bf16[320,128]{1,0:T(8,128)(2,1)S(1)}, bf16[320,128]{1,0:T(8,128)(2,1)S(1)}, u32[]{:S(2)}, u32[]{:S(2)}) collective-permute-start(bf16[320,128]{1,0:T(8,128)(2,1)S(1)} %get-tuple-element.33.refs_8_), channel_id=1, source_target_pairs={{0,1},{1,0},{2,3},{3,2},{4,6},{5,7},{6,4},{7,5},{8,9},{9,8},{10,11... | collective-permute-start | bytes 245768 | tf_op jit(solution)/shard_map/ppermute | solution.py:260
  6.1 0.1 collective-permute-start
  6.2 0.0 copy-done.1
  6.3 0.0 copy-start
  6.3 2.1 %code.1 = (bf16[64,4096]{1,0:T(8,128)(2,1)S(1)}, bf16[4096,128]{1,0:T(8,128)(2,1)S(1)}, bf16[4096,128]{1,0:T(8,128)(2,1)S(1)}, bf16[128,4096]{1,0:T(8,128)(2,1)S(1)}) custom-call(s32[32,128]{1,0:T(8,128)S(1)} %bitcast.6, bf16[4096,128]{1,0:T(8,128)(2,1)} %bitcast.9), custom_call_target="tpu_custom_call" | custom-call | tf_op jit(solution)/shard_map/code/pallas_call | solution.py:287
  8.3 0.0 copy-done
  8.3 0.0 copy-done.2
  8.4 0.0 copy-start.3
  8.4 1.1 %prepare.1 = (f32[8,4096]{1,0:T(8,128)S(1)}, bf16[64,256]{1,0:T(8,128)(2,1)S(1)}, bf16[256,128]{1,0:T(8,128)(2,1)S(1)}, f32[192,128]{1,0:T(8,128)S(1)}, f32[192,128]{1,0:T(8,128)S(1)}) custom-call(s32[1,4096]{1,0:T(1,128)S(1)} %bitcast.7, s32[1,64]{1,0:T(1,128)S(1)} %get-tuple-element.24.refs_1_, f32[3,4096]{1,0:T(4,128)S(1)} %copy-done, ...), custom_call_target="tpu_custom_call" | custom-call | tf_op jit(solution)/shard_map/prepare/pallas_call | solution.py:301
  9.5 0.0 collective-permute-done.2.refs_11_
  9.5 0.8 %collective-permute-done.1.refs_10_ = bf16[320,128]{1,0:T(8,128)(2,1)S(1)} collective-permute-done((bf16[320,128]{1,0:T(8,128)(2,1)S(1)}, bf16[320,128]{1,0:T(8,128)(2,1)S(1)}, u32[]{:S(2)}, u32[]{:S(2)}) %collective-permute-start.1) | collective-permute-done | bytes 81952 | tf_op jit(solution)/shard_map/ppermute | solution.py:260
  10.3 0.3 %collective-permute-done.refs_9_ = bf16[320,128]{1,0:T(8,128)(2,1)S(1)} collective-permute-done((bf16[320,128]{1,0:T(8,128)(2,1)S(1)}, bf16[320,128]{1,0:T(8,128)(2,1)S(1)}, u32[]{:S(2)}, u32[]{:S(2)}) %collective-permute-start) | collective-permute-done | bytes 81952 | tf_op jit(solution)/shard_map/ppermute | solution.py:260
  10.6 0.0 copy-done.3
  10.6 0.7 %glide.1 = (f32[1,4096]{1,0:T(1,128)S(1)}, bf16[128,128]{1,0:T(8,128)(2,1)S(1)}, bf16[128,128]{1,0:T(8,128)(2,1)S(1)}) custom-call(bf16[64,256]{1,0:T(8,128)(2,1)S(1)} %get-tuple-element.28.refs_0_, f32[1,4096]{1,0:T(1,128)S(1)} %bitcast.8, f32[8,4096]{1,0:T(8,128)S(1)} %get-tuple-element.29.refs_2_, bf16[64,4096]{1,0:T(8,128)(2,1)S(1)} %get-tuple-element.25.refs_3_, ...), custom_call_target="tpu_custom_call" | custom-call | tf_op jit(solution)/shard_map/glide/pallas_call | solution.py:318
  11.2 0.1 collective-permute-start.3
  11.3 0.5 %spread.1 = (f32[320,128]{1,0:T(8,128)S(1)}, bf16[320,128]{1,0:T(8,128)(2,1)S(1)}, bf16[320,128]{1,0:T(8,128)(2,1)S(1)}, bf16[320,128]{1,0:T(8,128)(2,1)S(1)}) custom-call(bf16[256,128]{1,0:T(8,128)(2,1)S(1)} %get-tuple-element.27.refs_0_, f32[1,4096]{1,0:T(1,128)S(1)} %get-tuple-element.34.refs_1_, f32[8,4096]{1,0:T(8,128)S(1)} %get-tuple-element.29.refs_2_, ...), custom_call_target="tpu_custom_call" | custom-call | tf_op jit(solution)/shard_map/spread/pallas_call | solution.py:343
  11.9 0.7 %collective-permute-done.3.refs_1_ = bf16[128,128]{1,0:T(8,128)(2,1)S(1)} collective-permute-done((bf16[128,128]{1,0:T(8,128)(2,1)S(1)}, bf16[128,128]{1,0:T(8,128)(2,1)S(1)}, u32[]{:S(2)}, u32[]{:S(2)}) %collective-permute-start.3) | collective-permute-done | bytes 32800 | tf_op jit(solution)/shard_map/ppermute | solution.py:339
  12.5 2.6 %collective-permute-start.7 = (bf16[176,128]{1,0:T(8,128)(2,1)S(1)}, bf16[176,128]{1,0:T(8,128)(2,1)S(1)}, u32[]{:S(2)}, u32[]{:S(2)}) collective-permute-start(bf16[176,128]{1,0:T(8,128)(2,1)S(1)} %get-tuple-element.45), channel_id=1, source_target_pairs={{0,16},{4,20},{8,24},{12,28},{16,0},{20,4},{24,8},{28,12},{1,17},{... | collective-permute-start | bytes 135176 | tf_op jit(solution)/shard_map/ppermute | solution.py:339
  15.1 1.8 %collective-permute-start.4 = (bf16[320,128]{1,0:T(8,128)(2,1)S(1)}, bf16[320,128]{1,0:T(8,128)(2,1)S(1)}, u32[]{:S(2)}, u32[]{:S(2)}) collective-permute-start(bf16[320,128]{1,0:T(8,128)(2,1)S(1)} %get-tuple-element.42), channel_id=1, source_target_pairs={{0,3},{1,2},{2,1},{3,0},{4,7},{5,6},{6,5},{7,4},{8,11},{9,10},{10,... | collective-permute-start | bytes 245768 | tf_op jit(solution)/shard_map/ppermute | solution.py:260
  16.9 0.6 %collective-permute-start.5 = (bf16[320,128]{1,0:T(8,128)(2,1)S(1)}, bf16[320,128]{1,0:T(8,128)(2,1)S(1)}, u32[]{:S(2)}, u32[]{:S(2)}) collective-permute-start(bf16[320,128]{1,0:T(8,128)(2,1)S(1)} %get-tuple-element.43), channel_id=1, source_target_pairs={{0,1},{1,0},{2,3},{3,2},{4,6},{5,7},{6,4},{7,5},{8,9},{9,8},{10,11... | collective-permute-start | bytes 245768 | tf_op jit(solution)/shard_map/ppermute | solution.py:260
  17.5 1.1 %collective-permute-start.6 = (bf16[320,128]{1,0:T(8,128)(2,1)S(1)}, bf16[320,128]{1,0:T(8,128)(2,1)S(1)}, u32[]{:S(2)}, u32[]{:S(2)}) collective-permute-start(bf16[320,128]{1,0:T(8,128)(2,1)S(1)} %get-tuple-element.44), channel_id=1, source_target_pairs={{0,2},{1,3},{2,0},{3,1},{4,5},{5,4},{6,7},{7,6},{8,10},{9,11},{10,... | collective-permute-start | bytes 245768 | tf_op jit(solution)/shard_map/ppermute | solution.py:260
  18.6 0.0 collective-permute-done.7.refs_2_
  18.6 1.6 %collective-permute-start.8 = (bf16[176,128]{1,0:T(8,128)(2,1)S(1)}, bf16[176,128]{1,0:T(8,128)(2,1)S(1)}, u32[]{:S(2)}, u32[]{:S(2)}) collective-permute-start(bf16[176,128]{1,0:T(8,128)(2,1)S(1)} %gather.3), channel_id=1, source_target_pairs={{0,8},{4,12},{8,0},{12,4},{16,24},{20,28},{24,16},{28,20},{1,9},{5... | collective-permute-start | bytes 135176 | tf_op jit(solution)/shard_map/ppermute | solution.py:339
  20.3 0.4 %collective-permute-done.4.refs_1_ = bf16[320,128]{1,0:T(8,128)(2,1)S(1)} collective-permute-done((bf16[320,128]{1,0:T(8,128)(2,1)S(1)}, bf16[320,128]{1,0:T(8,128)(2,1)S(1)}, u32[]{:S(2)}, u32[]{:S(2)}) %collective-permute-start.4) | collective-permute-done | bytes 81952 | tf_op jit(solution)/shard_map/ppermute | solution.py:260
  20.7 1.1 %collective-permute-done.5.refs_2_ = bf16[320,128]{1,0:T(8,128)(2,1)S(1)} collective-permute-done((bf16[320,128]{1,0:T(8,128)(2,1)S(1)}, bf16[320,128]{1,0:T(8,128)(2,1)S(1)}, u32[]{:S(2)}, u32[]{:S(2)}) %collective-permute-start.5) | collective-permute-done | bytes 81952 | tf_op jit(solution)/shard_map/ppermute | solution.py:260
  21.7 0.3 %collective-permute-done.6.refs_3_ = bf16[320,128]{1,0:T(8,128)(2,1)S(1)} collective-permute-done((bf16[320,128]{1,0:T(8,128)(2,1)S(1)}, bf16[320,128]{1,0:T(8,128)(2,1)S(1)}, u32[]{:S(2)}, u32[]{:S(2)}) %collective-permute-start.6) | collective-permute-done | bytes 81952 | tf_op jit(solution)/shard_map/ppermute | solution.py:260
  22.0 0.8 %total.1 = f32[6,8192]{1,0:T(8,128)} custom-call(f32[320,128]{1,0:T(8,128)S(1)} %get-tuple-element.36.refs_0_, bf16[320,128]{1,0:T(8,128)(2,1)S(1)} %collective-permute-done.4.refs_1_, bf16[320,128]{1,0:T(8,128)(2,1)S(1)} %collective-permute-done.5.refs_2_, bf16[320,128]{1,0:T(8,128)(2,1)S(1)} %collective-permute-done.6.refs_3_), custom_call_target="tpu_custom_call" | custom-call | tf_op jit(solution)/shard_map/total/pallas_call | solution.py:372
  22.8 0.0 collective-permute-done.8.refs_3_
  22.8 0.7 %arrive.1 = f32[4,8192]{1,0:T(4,128)} custom-call(bf16[128,128]{1,0:T(8,128)(2,1)S(1)} %get-tuple-element.37.refs_0_, bf16[128,128]{1,0:T(8,128)(2,1)S(1)} %collective-permute-done.3.refs_1_, bf16[176,128]{1,0:T(8,128)(2,1)S(1)} %collective-permute-done.7.refs_2_, bf16[176,128]{1,0:T(8,128)(2,1)S(1)} %collective-permute-done.8.refs_3_), custom_call_target="tpu_custom_call" | custom-call | tf_op jit(solution)/shard_map/arrive/pallas_call | solution.py:381
  (3 shorter events, 0.0 us)
Async XLA Ops:
  0.6 5.6 %copy-start.1 = (s32[4096,1]{0,1:T(1,128)S(1)}, s32[4096,1]{0,1:T(1,128)}, u32[]{:S(2)}) copy-start(s32[4096,1]{0,1:T(1,128)} %param.15) | copy-start | bytes 49156
  1.6 7.8 %collective-permute-start.2 = (bf16[320,128]{1,0:T(8,128)(2,1)S(1)}, bf16[320,128]{1,0:T(8,128)(2,1)S(1)}, u32[]{:S(2)}, u32[]{:S(2)}) collective-permute-start(bf16[320,128]{1,0:T(8,128)(2,1)S(1)} %get-tuple-element.33.refs_8_), channel_id=1, source_target_pairs={{0,3},{1,2},{2,1},{3,0},{4,7},{5,6},{6,5},{7,4},{8,11},{9,10},{10,... | collective-permute-start | bytes 245768 | tf_op jit(solution)/shard_map/ppermute | solution.py:260
  5.6 4.7 %collective-permute-start.1 = (bf16[320,128]{1,0:T(8,128)(2,1)S(1)}, bf16[320,128]{1,0:T(8,128)(2,1)S(1)}, u32[]{:S(2)}, u32[]{:S(2)}) collective-permute-start(bf16[320,128]{1,0:T(8,128)(2,1)S(1)} %get-tuple-element.33.refs_8_), channel_id=1, source_target_pairs={{0,1},{1,0},{2,3},{3,2},{4,6},{5,7},{6,4},{7,5},{8,9},{9,8},{10,11... | collective-permute-start | bytes 245768 | tf_op jit(solution)/shard_map/ppermute | solution.py:260
  6.1 4.4 %collective-permute-start = (bf16[320,128]{1,0:T(8,128)(2,1)S(1)}, bf16[320,128]{1,0:T(8,128)(2,1)S(1)}, u32[]{:S(2)}, u32[]{:S(2)}) collective-permute-start(bf16[320,128]{1,0:T(8,128)(2,1)S(1)} %get-tuple-element.33.refs_8_), channel_id=1, source_target_pairs={{0,2},{1,3},{2,0},{3,1},{4,5},{5,4},{6,7},{7,6},{8,10},{9,11},{10,... | collective-permute-start | bytes 245768 | tf_op jit(solution)/shard_map/ppermute | solution.py:260
  6.3 2.1 %copy-start = (f32[3,4096]{1,0:T(4,128)S(1)}, f32[3,4096]{1,0:T(4,128)}, u32[]{:S(2)}) copy-start(f32[3,4096]{1,0:T(4,128)} %refs_2_.1) | copy-start | bytes 147460
  6.3 2.1 %copy-start.2 = (s32[4096]{0:T(1024)S(1)}, s32[4096]{0:T(1024)}, u32[]{:S(2)}) copy-start(s32[4096]{0:T(1024)} %param.12) | copy-start | bytes 49156
  8.4 2.2 %copy-start.3 = (f32[4096]{0:T(1024)S(1)}, f32[4096]{0:T(1024)}, u32[]{:S(2)}) copy-start(f32[4096]{0:T(1024)} %param.13) | copy-start | bytes 49156
  11.2 1.3 %collective-permute-start.3 = (bf16[128,128]{1,0:T(8,128)(2,1)S(1)}, bf16[128,128]{1,0:T(8,128)(2,1)S(1)}, u32[]{:S(2)}, u32[]{:S(2)}) collective-permute-start(bf16[128,128]{1,0:T(8,128)(2,1)S(1)} %get-tuple-element.38), channel_id=1, source_target_pairs={{0,4},{4,0},{8,12},{12,8},{16,20},{20,16},{24,28},{28,24},{1,5},{5... | collective-permute-start | bytes 98312 | tf_op jit(solution)/shard_map/ppermute | solution.py:339
  12.5 6.1 %collective-permute-start.7 = (bf16[176,128]{1,0:T(8,128)(2,1)S(1)}, bf16[176,128]{1,0:T(8,128)(2,1)S(1)}, u32[]{:S(2)}, u32[]{:S(2)}) collective-permute-start(bf16[176,128]{1,0:T(8,128)(2,1)S(1)} %get-tuple-element.45), channel_id=1, source_target_pairs={{0,16},{4,20},{8,24},{12,28},{16,0},{20,4},{24,8},{28,12},{1,17},{... | collective-permute-start | bytes 135176 | tf_op jit(solution)/shard_map/ppermute | solution.py:339
  15.1 5.6 %collective-permute-start.4 = (bf16[320,128]{1,0:T(8,128)(2,1)S(1)}, bf16[320,128]{1,0:T(8,128)(2,1)S(1)}, u32[]{:S(2)}, u32[]{:S(2)}) collective-permute-start(bf16[320,128]{1,0:T(8,128)(2,1)S(1)} %get-tuple-element.42), channel_id=1, source_target_pairs={{0,3},{1,2},{2,1},{3,0},{4,7},{5,6},{6,5},{7,4},{8,11},{9,10},{10,... | collective-permute-start | bytes 245768 | tf_op jit(solution)/shard_map/ppermute | solution.py:260
  16.9 4.8 %collective-permute-start.5 = (bf16[320,128]{1,0:T(8,128)(2,1)S(1)}, bf16[320,128]{1,0:T(8,128)(2,1)S(1)}, u32[]{:S(2)}, u32[]{:S(2)}) collective-permute-start(bf16[320,128]{1,0:T(8,128)(2,1)S(1)} %get-tuple-element.43), channel_id=1, source_target_pairs={{0,1},{1,0},{2,3},{3,2},{4,6},{5,7},{6,4},{7,5},{8,9},{9,8},{10,11... | collective-permute-start | bytes 245768 | tf_op jit(solution)/shard_map/ppermute | solution.py:260
  17.5 4.5 %collective-permute-start.6 = (bf16[320,128]{1,0:T(8,128)(2,1)S(1)}, bf16[320,128]{1,0:T(8,128)(2,1)S(1)}, u32[]{:S(2)}, u32[]{:S(2)}) collective-permute-start(bf16[320,128]{1,0:T(8,128)(2,1)S(1)} %get-tuple-element.44), channel_id=1, source_target_pairs={{0,2},{1,3},{2,0},{3,1},{4,5},{5,4},{6,7},{7,6},{8,10},{9,11},{10,... | collective-permute-start | bytes 245768 | tf_op jit(solution)/shard_map/ppermute | solution.py:260
  18.6 4.2 %collective-permute-start.8 = (bf16[176,128]{1,0:T(8,128)(2,1)S(1)}, bf16[176,128]{1,0:T(8,128)(2,1)S(1)}, u32[]{:S(2)}, u32[]{:S(2)}) collective-permute-start(bf16[176,128]{1,0:T(8,128)(2,1)S(1)} %gather.3), channel_id=1, source_target_pairs={{0,8},{4,12},{8,0},{12,4},{16,24},{20,28},{24,16},{28,20},{1,9},{5... | collective-permute-start | bytes 135176 | tf_op jit(solution)/shard_map/ppermute | solution.py:339
